TPU v7x, 32 devices: a whole 2x2x4 slice. The times are simulated.
32 devices in a mesh: fsdp: 4 (over z), ctx: 4 (over x, core), tp: 2 (over y).
Axes of the slice: x: 2, y: 2, z: 4, core: 2. Of those that a mesh axis runs over, the one named last changes fastest.
Arguments:
- tokens: bfloat16 [8, 4096, 1024], P('fsdp', ('ctx', 'tp')), may hold values from -6 to 6
- time_embed: float32 [8, 256], P('fsdp'), may hold values from -6 to 6
- segment_ids: int32 [8, 4096], P('fsdp'), may hold values from 0 to 15, as said below
- block_pairs: int32 [8, 4, 15, 2], P('fsdp', 'ctx'), may hold values from 0 to 7, as said below
- pair_counts: int32 [8, 4], P('fsdp', 'ctx'), may hold values from 2 to 15, as said below
- w_time: float32 [256, 2048], P(('fsdp', 'ctx')), may hold values from -0.1875 to 0.1875
- w_qkv: float32 [1024, 3072], P(('fsdp', 'ctx'), 'tp'), may hold values from -0.1875 to 0.1875
- w_out: float32 [1024, 1024], P(('fsdp', 'ctx'), 'tp'), may hold values from -1.5 to 1.5
- w_up: float32 [1024, 4096], P(('fsdp', 'ctx'), 'tp'), may hold values from -0.1875 to 0.1875
- w_down: float32 [1024, 4096], P(('fsdp', 'ctx'), 'tp'), may hold values from -0.09375 to 0.09375
- cotangent: bfloat16 [8, 4096, 1024], P('fsdp', ('ctx', 'tp')), may hold values from -6 to 6
Outputs:
- layer_out: bfloat16 [8, 4096, 1024], P('fsdp', ('ctx', 'tp'))
- grad_tokens: bfloat16 [8, 4096, 1024], P('fsdp', ('ctx', 'tp'))
- grad_time: float32 [256, 2048], P(('fsdp', 'ctx'))
- grad_qkv: float32 [1024, 3072], P(('fsdp', 'ctx'), 'tp')
- grad_proj: float32 [1024, 1024], P(('fsdp', 'ctx'), 'tp')
- grad_up: float32 [1024, 4096], P(('fsdp', 'ctx'), 'tp')
- grad_down: float32 [1024, 4096], P(('fsdp', 'ctx'), 'tp')
Inputs may be any that keep to these rules, and one draw needn't show every extreme that they name: `segment_ids`: in each row the ids start at 0 and never fall; a new document starts at a position with probability 1 / 512; row 0 holds one document; in the last row a document also starts at every multiple of 256 until the id reaches 15; ids stop rising at 15, so the last documents of a row may merge. `block_pairs`: for row r and ctx index c, slots p < pair_counts[r, c] list in increasing order of (local query block, key block) exactly the pairs of a local query block (0 to 1) and a key block of the row that share a document with the key not after the query; other slots hold 0. `pair_counts`: the number of listed pairs; the last ctx index of row 0 reaches 15.
All inputs are finite; a program needn't handle non-finite values.
Results may differ from a plain program's by a relative error of at most 0.02.
Values may be sent and summed in bfloat16 or wider, within the bound.
No kernel may reach another device: no remote copies, remote signals or barrier semaphores. Data moves between devices by JAX's collectives and lax.ppermute only.
A program may use at most 256 MiB of HBM per device.

v0:
```python
import jax
import jax.numpy as jnp
from jax import lax
from jax.sharding import PartitionSpec as P

HEAD_DIM = 64
BLK = 512


epsilon = 1e-05
highest = lax.Precision.HIGHEST
masked_out = -1e30


def normalize(values):
    mean_value = jnp.mean(values, axis=-1, keepdims=True)
    centred = values - mean_value
    variance = jnp.mean(centred * centred, axis=-1, keepdims=True)
    inverse = lax.rsqrt(variance + epsilon)
    return (centred * inverse, inverse)


def normalize_back(grad_hat, normal_hat, inverse):
    first_mean = jnp.mean(grad_hat, axis=-1, keepdims=True)
    second_mean = jnp.mean(grad_hat * normal_hat, axis=-1, keepdims=True)
    return inverse * (grad_hat - first_mean - normal_hat * second_mean)


def smooth_gate(values):
    return jax.nn.gelu(values, approximate=True)


def block_scores(pair_entry, query_rows, key_rows, seg_row, offset):
    query_start = pair_entry[0] * BLK
    key_start = pair_entry[1] * BLK
    query_block = lax.dynamic_slice_in_dim(query_rows, query_start, BLK, 0)
    key_block = lax.dynamic_slice_in_dim(key_rows, key_start, BLK, 0)
    seg_query = lax.dynamic_slice_in_dim(seg_row, offset + query_start, BLK, 0)
    seg_keys = lax.dynamic_slice_in_dim(seg_row, key_start, BLK, 0)
    steps_in = jnp.arange(BLK, dtype=jnp.int32)
    allowed = (seg_query[:, None] == seg_keys[None, :]) & (
        key_start + steps_in[None, :] <= offset + query_start + steps_in[:, None]
    )
    scores = jnp.einsum(
        "qhe,khe->hqk", query_block, key_block, preferred_element_type=jnp.float32
    ) * HEAD_DIM ** (-0.5)
    return (query_block, key_block, query_start, key_start, allowed, scores)


def attend_forward(query_rows, key_rows, value_rows, seg_row, pair_rows, pair_total, offset):
    length_here, head_count, _ = query_rows.shape

    def statistic_step(pair_index, carried):
        running_max, running_sum = carried
        _, _, query_start, _, allowed, scores = block_scores(
            pair_rows[pair_index], query_rows, key_rows, seg_row, offset
        )
        scores = jnp.where(allowed[None], scores, masked_out)
        old_max = lax.dynamic_slice_in_dim(running_max, query_start, BLK, 1)
        old_sum = lax.dynamic_slice_in_dim(running_sum, query_start, BLK, 1)
        new_max = jnp.maximum(old_max, jnp.max(scores, axis=-1))
        weights = jnp.where(allowed[None], jnp.exp(scores - new_max[:, :, None]), 0.0)
        new_sum = old_sum * jnp.exp(old_max - new_max) + jnp.sum(weights, axis=-1)
        return (
            lax.dynamic_update_slice_in_dim(running_max, new_max, query_start, 1),
            lax.dynamic_update_slice_in_dim(running_sum, new_sum, query_start, 1),
        )

    start_max = jnp.full((head_count, length_here), masked_out, jnp.float32)
    start_sum = jnp.zeros((head_count, length_here), jnp.float32)
    running_max, running_sum = lax.fori_loop(0, pair_total, statistic_step, (start_max, start_sum))
    log_total = running_max + jnp.log(running_sum)

    def output_step(pair_index, accumulated):
        _, _, query_start, key_start, allowed, scores = block_scores(
            pair_rows[pair_index], query_rows, key_rows, seg_row, offset
        )
        block_log = lax.dynamic_slice_in_dim(log_total, query_start, BLK, 1)
        probabilities = jnp.where(
            allowed[None], jnp.exp(scores - block_log[:, :, None]), 0.0
        ).astype(jnp.bfloat16)
        value_block = lax.dynamic_slice_in_dim(value_rows, key_start, BLK, 0)
        addition = jnp.einsum(
            "hqk,khe->qhe", probabilities, value_block, preferred_element_type=jnp.float32
        )
        previous = lax.dynamic_slice_in_dim(accumulated, query_start, BLK, 0)
        return lax.dynamic_update_slice_in_dim(accumulated, previous + addition, query_start, 0)

    mixed_rows = lax.fori_loop(0, pair_total, output_step, jnp.zeros(query_rows.shape, jnp.float32))
    return (mixed_rows, log_total)


def attend_backward(
    query_rows,
    key_rows,
    value_rows,
    seg_row,
    pair_rows,
    pair_total,
    offset,
    log_total,
    grad_mixed,
    inner_sums,
):
    scale_factor = HEAD_DIM ** (-0.5)

    def add_block(whole, start_at, addition):
        previous = lax.dynamic_slice_in_dim(whole, start_at, BLK, 0)
        return lax.dynamic_update_slice_in_dim(whole, previous + addition, start_at, 0)

    def gradient_step(pair_index, carried):
        grad_query, grad_keys, grad_values = carried
        query_block, key_block, query_start, key_start, allowed, scores = block_scores(
            pair_rows[pair_index], query_rows, key_rows, seg_row, offset
        )
        block_log = lax.dynamic_slice_in_dim(log_total, query_start, BLK, 1)
        probabilities = jnp.where(allowed[None], jnp.exp(scores - block_log[:, :, None]), 0.0)
        grad_block = lax.dynamic_slice_in_dim(grad_mixed, query_start, BLK, 0)
        value_block = lax.dynamic_slice_in_dim(value_rows, key_start, BLK, 0)
        grad_probs = jnp.einsum(
            "qhe,khe->hqk", grad_block, value_block, preferred_element_type=jnp.float32
        )
        inner_block = lax.dynamic_slice_in_dim(inner_sums, query_start, BLK, 1)
        grad_scores = (probabilities * (grad_probs - inner_block[:, :, None])).astype(jnp.bfloat16)
        query_add = (
            jnp.einsum("hqk,khe->qhe", grad_scores, key_block, preferred_element_type=jnp.float32)
            * scale_factor
        )
        key_add = (
            jnp.einsum("hqk,qhe->khe", grad_scores, query_block, preferred_element_type=jnp.float32)
            * scale_factor
        )
        value_add = jnp.einsum(
            "hqk,qhe->khe",
            probabilities.astype(jnp.bfloat16),
            grad_block,
            preferred_element_type=jnp.float32,
        )
        return (
            add_block(grad_query, query_start, query_add),
            add_block(grad_keys, key_start, key_add),
            add_block(grad_values, key_start, value_add),
        )

    start_state = (
        jnp.zeros(query_rows.shape, jnp.float32),
        jnp.zeros(key_rows.shape, jnp.float32),
        jnp.zeros(value_rows.shape, jnp.float32),
    )
    return lax.fori_loop(0, pair_total, gradient_step, start_state)


def body(
    tokens,
    time_embed,
    segment_ids,
    block_pairs,
    pair_counts,
    w_time,
    w_qkv,
    w_out,
    w_up,
    w_down,
    cotangent,
):
    row_count, local_len, model_width = tokens.shape
    time_all, qkv_all, out_all, up_all, down_all = (
        lax.all_gather(w_time.astype(jnp.bfloat16), ("fsdp", "ctx"), axis=0, tiled=True),
        lax.all_gather(w_qkv.astype(jnp.bfloat16), ("fsdp", "ctx"), axis=0, tiled=True),
        lax.all_gather(w_out.astype(jnp.bfloat16), ("fsdp", "ctx"), axis=0, tiled=True),
        lax.all_gather(w_up.astype(jnp.bfloat16), ("fsdp", "ctx"), axis=0, tiled=True),
        lax.all_gather(w_down.astype(jnp.bfloat16), ("fsdp", "ctx"), axis=0, tiled=True),
    )
    scales = 1.0 + jnp.dot(time_embed, time_all.astype(jnp.float32), precision=highest)
    scale_attn = scales[:, None, :model_width]
    scale_mlp = scales[:, None, model_width:]
    x_input = tokens.astype(jnp.float32)
    hat_attn, inverse_attn = normalize(x_input)
    normed = (hat_attn * scale_attn).astype(jnp.bfloat16)
    normed_all = lax.all_gather(normed, "tp", axis=1, tiled=True)
    ctx_len = normed_all.shape[1]
    head_count = qkv_all.shape[1] // (3 * HEAD_DIM)
    projected = jnp.einsum("rtd,dc->rtc", normed_all, qkv_all, preferred_element_type=jnp.float32)
    projected = projected.astype(jnp.bfloat16).reshape(row_count, ctx_len, head_count, 3, HEAD_DIM)
    query_all = projected[:, :, :, 0]
    key_part = projected[:, :, :, 1]
    value_part = projected[:, :, :, 2]
    key_all, value_all = (
        lax.all_gather(key_part, "ctx", axis=1, tiled=True),
        lax.all_gather(value_part, "ctx", axis=1, tiled=True),
    )
    offset = lax.axis_index("ctx") * ctx_len
    mixed_list = []
    log_list = []
    for row_index in range(row_count):
        mixed_rows, log_total = attend_forward(
            query_all[row_index],
            key_all[row_index],
            value_all[row_index],
            segment_ids[row_index],
            block_pairs[row_index, 0],
            pair_counts[row_index, 0],
            offset,
        )
        mixed_list.append(mixed_rows)
        log_list.append(log_total)
    mixed_exact = jnp.stack(mixed_list)
    mixed_heads = mixed_exact.astype(jnp.bfloat16).reshape(
        row_count, ctx_len, head_count * HEAD_DIM
    )
    attn_part = jnp.einsum("rtc,dc->rtd", mixed_heads, out_all, preferred_element_type=jnp.float32)
    attn_local = lax.psum_scatter(
        attn_part.astype(jnp.bfloat16), "tp", scatter_dimension=1, tiled=True
    ).astype(jnp.float32)
    hidden = x_input + attn_local
    hat_mlp, inverse_mlp = normalize(hidden)
    normed_mlp = (hat_mlp * scale_mlp).astype(jnp.bfloat16)
    mlp_all = lax.all_gather(normed_mlp, "tp", axis=1, tiled=True)
    pre_act = jnp.einsum("rtd,df->rtf", mlp_all, up_all, preferred_element_type=jnp.float32)
    activated = smooth_gate(pre_act).astype(jnp.bfloat16)
    mlp_part = jnp.einsum("rtf,df->rtd", activated, down_all, preferred_element_type=jnp.float32)
    mlp_local = lax.psum_scatter(
        mlp_part.astype(jnp.bfloat16), "tp", scatter_dimension=1, tiled=True
    ).astype(jnp.float32)
    grad_all = lax.all_gather(cotangent, "tp", axis=1, tiled=True)
    grad_act = jnp.einsum("rtd,df->rtf", grad_all, down_all, preferred_element_type=jnp.float32)
    _, gate_back = jax.vjp(smooth_gate, pre_act)
    grad_pre = gate_back(grad_act)[0].astype(jnp.bfloat16)
    grad_down = jnp.einsum("rtd,rtf->df", grad_all, activated, preferred_element_type=jnp.float32)
    grad_up = jnp.einsum("rtd,rtf->df", mlp_all, grad_pre, preferred_element_type=jnp.float32)
    norm_part = jnp.einsum("rtf,df->rtd", grad_pre, up_all, preferred_element_type=jnp.float32)
    grad_normed_mlp = lax.psum_scatter(
        norm_part.astype(jnp.bfloat16), "tp", scatter_dimension=1, tiled=True
    ).astype(jnp.float32)
    layer_out = (hidden + mlp_local).astype(jnp.bfloat16)
    grad_output = cotangent.astype(jnp.float32)
    grad_scale_mlp = jnp.sum(grad_normed_mlp * hat_mlp, axis=1)
    grad_hidden = grad_output + normalize_back(grad_normed_mlp * scale_mlp, hat_mlp, inverse_mlp)
    grad_attn_all = lax.all_gather(grad_hidden.astype(jnp.bfloat16), "tp", axis=1, tiled=True)
    grad_mixed = jnp.einsum(
        "rtd,dc->rtc", grad_attn_all, out_all, preferred_element_type=jnp.float32
    ).astype(jnp.bfloat16)
    grad_proj = jnp.einsum(
        "rtd,rtc->dc", grad_attn_all, mixed_heads, preferred_element_type=jnp.float32
    )
    grad_mixed = grad_mixed.reshape(row_count, ctx_len, head_count, HEAD_DIM)
    inner_sums = jnp.einsum("rqhe,rqhe->rhq", grad_mixed.astype(jnp.float32), mixed_exact)
    query_grads = []
    key_grads = []
    value_grads = []
    for row_index in range(row_count):
        grad_query, grad_keys, grad_values = attend_backward(
            query_all[row_index],
            key_all[row_index],
            value_all[row_index],
            segment_ids[row_index],
            block_pairs[row_index, 0],
            pair_counts[row_index, 0],
            offset,
            log_list[row_index],
            grad_mixed[row_index],
            inner_sums[row_index],
        )
        query_grads.append(grad_query)
        key_grads.append(grad_keys)
        value_grads.append(grad_values)
    key_local, value_local = (
        lax.psum_scatter(
            jnp.stack(key_grads).astype(jnp.bfloat16), "ctx", scatter_dimension=1, tiled=True
        ).astype(jnp.float32),
        lax.psum_scatter(
            jnp.stack(value_grads).astype(jnp.bfloat16), "ctx", scatter_dimension=1, tiled=True
        ).astype(jnp.float32),
    )
    grad_projected = jnp.stack(
        [
            jnp.stack(query_grads).astype(jnp.bfloat16),
            key_local.astype(jnp.bfloat16),
            value_local.astype(jnp.bfloat16),
        ],
        axis=3,
    )
    grad_projected = grad_projected.reshape(row_count, ctx_len, head_count * 3 * HEAD_DIM)
    grad_qkv = jnp.einsum(
        "rtd,rtc->dc", normed_all, grad_projected, preferred_element_type=jnp.float32
    )
    first_part = jnp.einsum(
        "rtc,dc->rtd", grad_projected, qkv_all, preferred_element_type=jnp.float32
    )
    grad_normed = lax.psum_scatter(
        first_part.astype(jnp.bfloat16), "tp", scatter_dimension=1, tiled=True
    ).astype(jnp.float32)
    grad_scale_attn = jnp.sum(grad_normed * hat_attn, axis=1)
    grad_tokens = grad_hidden + normalize_back(grad_normed * scale_attn, hat_attn, inverse_attn)
    grad_scales = lax.psum(jnp.concatenate([grad_scale_attn, grad_scale_mlp], axis=1), "tp")
    grad_time = jnp.dot(time_embed.T, grad_scales, precision=highest)
    shared = (
        lax.psum_scatter(
            grad_time.astype(jnp.bfloat16), ("fsdp", "ctx"), scatter_dimension=0, tiled=True
        ).astype(jnp.float32),
        lax.psum_scatter(
            grad_qkv.astype(jnp.bfloat16), ("fsdp", "ctx"), scatter_dimension=0, tiled=True
        ).astype(jnp.float32),
        lax.psum_scatter(
            grad_proj.astype(jnp.bfloat16), ("fsdp", "ctx"), scatter_dimension=0, tiled=True
        ).astype(jnp.float32),
        lax.psum_scatter(
            grad_up.astype(jnp.bfloat16), ("fsdp", "ctx"), scatter_dimension=0, tiled=True
        ).astype(jnp.float32),
        lax.psum_scatter(
            grad_down.astype(jnp.bfloat16), ("fsdp", "ctx"), scatter_dimension=0, tiled=True
        ).astype(jnp.float32),
    )
    return (
        layer_out,
        grad_tokens.astype(jnp.bfloat16),
        shared[0],
        shared[1],
        shared[2],
        shared[3],
        shared[4],
    )


def solution(mesh):
    placed = (
        P("fsdp", ("ctx", "tp"), None),
        P("fsdp", None),
        P("fsdp", None),
        P("fsdp", "ctx", None, None),
        P("fsdp", "ctx"),
        P(("fsdp", "ctx"), None),
        P(("fsdp", "ctx"), "tp"),
        P(("fsdp", "ctx"), "tp"),
        P(("fsdp", "ctx"), "tp"),
        P(("fsdp", "ctx"), "tp"),
        P("fsdp", ("ctx", "tp"), None),
    )
    return jax.shard_map(
        body,
        mesh=mesh,
        in_specs=placed,
        out_specs=(
            P("fsdp", ("ctx", "tp"), None),
            P("fsdp", ("ctx", "tp"), None),
            P(("fsdp", "ctx"), None),
            P(("fsdp", "ctx"), "tp"),
            P(("fsdp", "ctx"), "tp"),
            P(("fsdp", "ctx"), "tp"),
            P(("fsdp", "ctx"), "tp"),
        ),
        check_vma=False,
    )
```

profile of v0, /device:TPU:0, one launch (start us, length us, event | category | flops | bytes accessed | tf_op | source)
XLA Modules:
  0.0 2186.8 jit_solution(10200135109171800613)
XLA Ops:
  13.5 38.0 %all-gather.14.cloned.1.call-done = bf16[256,2048]{1,0:T(8,128)(2,1)} async-done(((bf16[16,2048]{1,0:T(8,128)(2,1)}), bf16[256,2048]{1,0:T(8,128)(2,1)}) %all-gather.14.cloned.1.call-update) | async-done | bytes 1048592 | tf_op jit(solution)/shard_map/all_gather | solution.py:168
  56.5 42.2 %all-gather.18.cloned.1.call-done = bf16[1024,1536]{1,0:T(8,128)(2,1)} async-done(((bf16[64,1536]{1,0:T(8,128)(2,1)}), bf16[1024,1536]{1,0:T(8,128)(2,1)}) %all-gather.18.cloned.1.call-update) | async-done | bytes 3145744 | tf_op jit(solution)/shard_map/all_gather | solution.py:169
  98.7 57.7 %all-gather.16.cloned.1.call-done = bf16[2,1024,1024]{2,1,0:T(8,128)(2,1)} async-done(((bf16[2,512,1024]{2,1,0:T(8,128)(2,1)}), bf16[2,1024,1024]{2,1,0:T(8,128)(2,1)}) %all-gather.16.cloned.1.call-update) | async-done | bytes 4194320 | tf_op jit(solution)/shard_map/all_gather | solution.py:180
  156.4 11.2 convolution_convert_fusion
  167.6 8.6 copy.50
  186.9 52.8 %all-gather.34.cloned.1.call-done = bf16[2,4096,8,1,64]{1,4,3,2,0:T(8,128)(2,1)} async-done(((bf16[2,1024,8,1,64]{1,4,3,2,0:T(8,128)(2,1)}), bf16[2,4096,8,1,64]{1,4,3,2,0:T(8,128)(2,1)}) %all-gather.34.cloned.1.call-update) | async-done | bytes 8388624 | tf_op jit(solution)/shard_map/all_gather | solution.py:189
  239.7 6.0 slice_bitcast_fusion.2
  245.7 24.1 %while.72 = (s32[]{:T(128)}, f32[8,1024]{1,0:T(8,128)S(1)}, f32[8,1024]{1,0:T(8,128)S(1)}, s32[]{:T(128)}, s32[15,2]{0,1:T(2,128)S(1)}, /*index=5*/s32[]{:T(128)...) while((s32[]{:T(128)}, f32[8,1024]{1,0:T(8,128)S(1)}, ...), condition=%wide.region_5.6_spmd, body=%wide.region_2.5_spmd.sunk | while | flops 286008320 | bytes 18960764 | solution.py:71
  269.9 30.1 %all-gather.32.cloned.1.call-done = bf16[2,4096,8,1,64]{1,4,3,2,0:T(8,128)(2,1)} async-done(((bf16[2,1024,8,1,64]{1,4,3,2,0:T(8,128)(2,1)}), bf16[2,4096,8,1,64]{1,4,3,2,0:T(8,128)(2,1)}) %all-gather.32.cloned.1.call-update) | async-done | bytes 8388624 | tf_op jit(solution)/shard_map/all_gather | solution.py:190
  300.0 6.0 slice_bitcast_fusion.3
  307.5 28.2 %while.73 = (s32[]{:T(128)}, f32[1024,8,64]{0,2,1:T(8,128)}, s32[]{:T(128)}, s32[15,2]{0,1:T(2,128)S(1)}, bf16[4096,8,64]{0,2,1:T(8,128)(2,1)}, /*index=5*/s32[]...) while((s32[]{:T(128)}, f32[1024,8,64]{0,2,1:T(8,128)}, ...), condition=%wide.region_7.8_spmd, body=%wide.region_6.7_spmd.sunk | while | flops 546309120 | bytes 4266361 | solution.py:89
  310.9 6.1 fusion.264
  320.0 6.1 fusion.264
  329.1 6.1 fusion.264
  336.4 25.7 %while.74 = (s32[]{:T(128)}, f32[8,1024]{1,0:T(8,128)S(1)}, f32[8,1024]{1,0:T(8,128)S(1)}, s32[]{:T(128)}, s32[15,2]{0,1:T(2,128)S(1)}, /*index=5*/s32[]{:T(128)...) while((s32[]{:T(128)}, f32[8,1024]{1,0:T(8,128)S(1)}, ...), condition=%wide.region_11.12_spmd, body=%wide.region_8.11_spmd.sunk | while | flops 286008320 | bytes 18960764 | solution.py:71
  363.7 29.6 %while.75 = (s32[]{:T(128)}, f32[1024,8,64]{0,2,1:T(8,128)}, s32[]{:T(128)}, s32[15,2]{0,1:T(2,128)S(1)}, bf16[4096,8,64]{0,2,1:T(8,128)(2,1)}, /*index=5*/s32[]...) while((s32[]{:T(128)}, f32[1024,8,64]{0,2,1:T(8,128)}, ...), condition=%wide.region_13.14_spmd, body=%wide.region_12.13_spmd.sunk | while | flops 546309120 | bytes 4266361 | solution.py:89
  367.4 6.0 fusion.273
  377.1 6.0 fusion.273
  386.8 6.0 fusion.273
  403.1 6.3 convolution_convert_fusion.1
  411.2 240.9 %reduce-scatter.16.cloned.1.call-done = bf16[2,512,1024]{2,1,0:T(8,128)(2,1)} async-done(((bf16[2,1024,1024]{2,1,0:T(8,128)(2,1)}), bf16[2,512,1024]{2,1,0:T(8,128)(2,1)}) %reduce-scatter.16.cloned.1.call-update) | async-done | bytes 2097168 | tf_op jit(solution)/shard_map/reduce_scatter | solution.py:212
  659.4 46.2 %all-gather.24.cloned.1.call-done = bf16[1024,2048]{1,0:T(8,128)(2,1)} async-done(((bf16[64,2048]{1,0:T(8,128)(2,1)}), bf16[1024,2048]{1,0:T(8,128)(2,1)}) %all-gather.24.cloned.1.call-update) | async-done | bytes 4194320 | tf_op jit(solution)/shard_map/all_gather | solution.py:171
  705.6 56.9 %all-gather.22.cloned.1.call-done = bf16[2,1024,1024]{2,1,0:T(8,128)(2,1)} async-done(((bf16[2,512,1024]{2,1,0:T(8,128)(2,1)}), bf16[2,1024,1024]{2,1,0:T(8,128)(2,1)}) %all-gather.22.cloned.1.call-update) | async-done | bytes 4194320 | tf_op jit(solution)/shard_map/all_gather | solution.py:218
  762.5 15.2 fusion.147
  777.8 43.0 %all-gather.28.cloned.1.call-done = bf16[2,1024,1024]{2,1,0:T(8,128)(2,1)} async-done(((bf16[2,512,1024]{2,1,0:T(8,128)(2,1)}), bf16[2,1024,1024]{2,1,0:T(8,128)(2,1)}) %all-gather.28.cloned.1.call-update) | async-done | bytes 4194320 | tf_op jit(solution)/shard_map/all_gather | solution.py:225
  820.8 53.7 %all-gather.26.cloned.1.call-done = bf16[1024,2048]{1,0:T(8,128)(2,1)} async-done(((bf16[64,2048]{1,0:T(8,128)(2,1)}), bf16[1024,2048]{1,0:T(8,128)(2,1)}) %all-gather.26.cloned.1.call-update) | async-done | bytes 4194320 | tf_op jit(solution)/shard_map/all_gather | solution.py:172
  874.5 22.3 %fusion.116 = bf16[2,1024,2048]{2,1,0:T(8,128)(2,1)S(1)} fusion(f32[2,1024,2048]{2,1,0:T(8,128)} %fusion.147, bf16[2,1024,1024]{2,1,0:T(8,128)(2,1)} %all-gather.28.cloned.1.call-done, bf16[1024,2048]{1,0:T(8,128)(2,1)} %all-gather.26.cloned.1.call-done), kind=kOutput, calls=%fused_computation.146 | convolution fusion | flops 8673820672 | bytes 33554432 | tf_op jit(solution)/shard_map/rtd,df->rtf/dot_general | solution.py:226
  900.1 11.2 fusion.157
  911.4 52.9 %reduce-scatter.20.cloned.1.call-done = bf16[2,512,1024]{2,1,0:T(8,128)(2,1)} async-done(((bf16[2,1024,1024]{2,1,0:T(8,128)(2,1)}), bf16[2,512,1024]{2,1,0:T(8,128)(2,1)}) %reduce-scatter.20.cloned.1.call-update) | async-done | bytes 2097168 | tf_op jit(solution)/shard_map/reduce_scatter | solution.py:232
  972.4 56.9 %all-gather.30.cloned.1.call-done = bf16[2,1024,1024]{2,1,0:T(8,128)(2,1)} async-done(((bf16[2,512,1024]{2,1,0:T(8,128)(2,1)}), bf16[2,1024,1024]{2,1,0:T(8,128)(2,1)}) %all-gather.30.cloned.1.call-update) | async-done | bytes 4194320 | tf_op jit(solution)/shard_map/all_gather | solution.py:239
  1029.3 6.0 fusion.141
  1046.7 78.6 %while.76 = (s32[]{:T(128)}, f32[1024,8,64]{0,2,1:T(8,128)}, f32[4096,8,64]{0,2,1:T(8,128)}, f32[4096,8,64]{0,2,1:T(8,128)}, s32[]{:T(128)}, /*index=5*/s32[15,2...) while((s32[]{:T(128)}, f32[1024,8,64]{0,2,1:T(8,128)}, ...), condition=%wide.region_22.23_spmd, body=%wide.region_21.22_spmd.sunk | while | flops 1365246976 | bytes 77992456 | solution.py:150
  1049.2 5.6 fusion.285
  1056.0 5.7 multiply_convert_fusion.8
  1075.0 5.6 fusion.285
  1081.8 5.7 multiply_convert_fusion.8
  1100.9 5.6 fusion.285
  1107.7 5.7 multiply_convert_fusion.8
  1125.3 6.0 convert_bitcast_fusion.3
  1141.5 77.7 %while.77 = (s32[]{:T(128)}, f32[1024,8,64]{0,2,1:T(8,128)}, f32[4096,8,64]{0,2,1:T(8,128)}, f32[4096,8,64]{0,2,1:T(8,128)}, s32[]{:T(128)}, /*index=5*/s32[15,2...) while((s32[]{:T(128)}, f32[1024,8,64]{0,2,1:T(8,128)}, ...), condition=%wide.region_24.25_spmd, body=%wide.region_23.24_spmd.sunk | while | flops 1365246976 | bytes 73798128 | solution.py:150
  1144.1 5.6 fusion.301
  1150.8 5.6 multiply_convert_fusion.9
  1169.8 5.6 fusion.301
  1195.5 5.6 fusion.301
  1219.3 6.2 convert_bitcast_fusion.2
  1225.5 6.2 pad_maximum_fusion
  1235.8 6.1 convert_bitcast_fusion
  1241.9 6.2 pad_maximum_fusion.1
  1251.9 383.3 %reduce-scatter.22.cloned.1.call-done = bf16[2,1024,8,64]{1,3,2,0:T(8,128)(2,1)} async-done(((bf16[2,4096,8,64]{1,3,2,0:T(8,128)(2,1)}), bf16[2,1024,8,64]{1,3,2,0:T(8,128)(2,1)}) %reduce-scatter.22.cloned.1.call-update) | async-done | bytes 2097168 | tf_op jit(solution)/shard_map/reduce_scatter | solution.py:268
  1635.1 74.3 %reduce-scatter.24.cloned.1.call-done = bf16[2,1024,8,64]{1,3,2,0:T(8,128)(2,1)} async-done(((bf16[2,4096,8,64]{1,3,2,0:T(8,128)(2,1)}), bf16[2,1024,8,64]{1,3,2,0:T(8,128)(2,1)}) %reduce-scatter.24.cloned.1.call-update) | async-done | bytes 2097168 | tf_op jit(solution)/shard_map/reduce_scatter | solution.py:271
  1715.5 8.7 fusion.154
  1724.2 16.9 fusion.150
  1741.2 6.5 copy.76
  1747.9 14.3 bitcast_convert_fusion.1
  1769.4 11.4 bitcast_convert_fusion.2
  1781.1 16.2 fusion.160
  1802.3 8.4 psum.7
  1814.1 41.1 %reduce-scatter.36.cloned.1.call-done = bf16[64,2048]{1,0:T(8,128)(2,1)} async-done(((bf16[1024,2048]{1,0:T(8,128)(2,1)}), bf16[64,2048]{1,0:T(8,128)(2,1)}) %reduce-scatter.36.cloned.1.call-update) | async-done | bytes 262160
  1857.4 73.1 %reduce-scatter.32.cloned.1.call-done = bf16[64,2048]{1,0:T(8,128)(2,1)} async-done(((bf16[1024,2048]{1,0:T(8,128)(2,1)}), bf16[64,2048]{1,0:T(8,128)(2,1)}) %reduce-scatter.32.cloned.1.call-update) | async-done | bytes 262160 | tf_op jit(solution)/shard_map/reduce_scatter | solution.py:307
  1932.3 59.3 %reduce-scatter.30.cloned.1.call-done = bf16[64,512]{1,0:T(8,128)(2,1)} async-done(((bf16[1024,512]{1,0:T(8,128)(2,1)}), bf16[64,512]{1,0:T(8,128)(2,1)}) %reduce-scatter.30.cloned.1.call-update) | async-done | bytes 65552 | tf_op jit(solution)/shard_map/reduce_scatter | solution.py:304
  1993.1 67.4 %reduce-scatter.28.cloned.1.call-done = bf16[64,1536]{1,0:T(8,128)(2,1)} async-done(((bf16[1024,1536]{1,0:T(8,128)(2,1)}), bf16[64,1536]{1,0:T(8,128)(2,1)}) %reduce-scatter.28.cloned.1.call-update) | async-done | bytes 196624 | tf_op jit(solution)/shard_map/reduce_scatter | solution.py:301
  2062.2 53.9 %reduce-scatter.18.cloned.1.call-done = bf16[2,512,1024]{2,1,0:T(8,128)(2,1)} async-done(((bf16[2,1024,1024]{2,1,0:T(8,128)(2,1)}), bf16[2,512,1024]{2,1,0:T(8,128)(2,1)}) %reduce-scatter.18.cloned.1.call-update) | async-done | bytes 2097168 | tf_op jit(solution)/shard_map/reduce_scatter | solution.py:222
  2116.1 8.4 fusion.131
  2124.5 53.0 %reduce-scatter.34.cloned.1.call-done = bf16[16,2048]{1,0:T(8,128)(2,1)} async-done(((bf16[256,2048]{1,0:T(8,128)(2,1)}), bf16[16,2048]{1,0:T(8,128)(2,1)}) %reduce-scatter.34.cloned.1.call-update) | async-done | bytes 65552
  (397 shorter events, 247.8 us)
Async XLA Ops:
  7.2 44.3 %copy-start = (f32[2,256]{1,0:T(2,128)S(1)}, f32[2,256]{1,0:T(2,128)}, u32[]{:S(2)}) copy-start(f32[2,256]{1,0:T(2,128)} %param.24) | copy-start | bytes 6148
  7.2 5.5 copy-start.1
  7.2 44.2 %all-gather.14.cloned.1.call-start = ((), (), s32[]{:S(2)}) async-start(), calls=%async_computation.11 | async-start | bytes 1114112 | tf_op jit(solution)/shard_map/all_gather | solution.py:168
  8.9 89.7 %all-gather.18.cloned.1.call-start = ((), (), s32[]{:S(2)}) async-start(), calls=%async_computation.13 | async-start | bytes 3342336 | tf_op jit(solution)/shard_map/all_gather | solution.py:169
  10.7 145.7 %all-gather.16.cloned.1.call-start = ((), (), s32[]{:S(2)}) async-start(), calls=%async_computation.12 | async-start | bytes 6291456 | tf_op jit(solution)/shard_map/all_gather | solution.py:180
  12.7 43.7 %copy-start.32 = (f32[2,512]{1,0:T(2,128)}, f32[2,512]{1,0:T(2,128)S(1)}, u32[]{:S(2)}) copy-start(f32[2,512]{1,0:T(2,128)S(1)} %broadcast_multiply_fusion.5) | copy-start | bytes 12292
  13.4 154.2 %copy-start.34 = (f32[2,512]{1,0:T(2,128)}, f32[2,512]{1,0:T(2,128)S(1)}, u32[]{:S(2)}) copy-start(f32[2,512]{1,0:T(2,128)S(1)} %add_rsqrt_fusion.1) | copy-start | bytes 12292
  56.4 183.2 %all-gather.34.cloned.1.call-start = ((), (), s32[]{:S(2)}) async-start(), calls=%async_computation.30 | async-start | bytes 10485760 | tf_op jit(solution)/shard_map/all_gather | solution.py:189
  181.2 118.7 %all-gather.32.cloned.1.call-start = ((), (), s32[]{:S(2)}) async-start(), calls=%async_computation.29 | async-start | bytes 10485760 | tf_op jit(solution)/shard_map/all_gather | solution.py:190
  181.8 221.2 %all-gather.20.cloned.1.call-start = ((), (), s32[]{:S(2)}) async-start(), calls=%async_computation.14 | async-start | bytes 1114112 | tf_op jit(solution)/shard_map/all_gather | solution.py:170
  182.8 469.3 %reduce-scatter.16.cloned.1.call-start = ((), (), s32[]{:S(2)}) async-start(), calls=%async_computation.15 | async-start | bytes 6291456 | tf_op jit(solution)/shard_map/reduce_scatter | solution.py:212
  393.4 8.2 copy-start.3
  393.4 8.2 copy-start.12
  393.4 8.1 copy-start.21
  403.0 6.3 copy-start.15
  409.4 296.2 %all-gather.24.cloned.1.call-start = ((), (), s32[]{:S(2)}) async-start(), calls=%async_computation.17 | async-start | bytes 4456448 | tf_op jit(solution)/shard_map/all_gather | solution.py:171
  411.1 244.3 %copy-start.23 = (f32[2,1024]{1,0:T(2,128)S(1)}, f32[2,1024]{1,0:T(2,128)}, u32[]{:S(2)}) copy-start(f32[2,1024]{1,0:T(2,128)} %get-tuple-element.637) | copy-start | bytes 24580
  411.2 351.4 %all-gather.22.cloned.1.call-start = ((), (), s32[]{:S(2)}) async-start(), calls=%async_computation.16 | async-start | bytes 6291456 | tf_op jit(solution)/shard_map/all_gather | solution.py:218
  654.5 314.6 %copy-start.25 = (f32[2,512]{1,0:T(2,128)}, f32[2,512]{1,0:T(2,128)S(1)}, u32[]{:S(2)}) copy-start(f32[2,512]{1,0:T(2,128)S(1)} %broadcast_multiply_fusion.4) | copy-start | bytes 12292
  655.5 313.7 %copy-start.30 = (f32[2,512]{1,0:T(2,128)}, f32[2,512]{1,0:T(2,128)S(1)}, u32[]{:S(2)}) copy-start(f32[2,512]{1,0:T(2,128)S(1)} %add_rsqrt_fusion) | copy-start | bytes 12292
  657.8 163.0 %all-gather.28.cloned.1.call-start = ((), (), s32[]{:S(2)}) async-start(), calls=%async_computation.20 | async-start | bytes 6291456 | tf_op jit(solution)/shard_map/all_gather | solution.py:225
  658.4 216.1 %all-gather.26.cloned.1.call-start = ((), (), s32[]{:S(2)}) async-start(), calls=%async_computation.18 | async-start | bytes 4456448 | tf_op jit(solution)/shard_map/all_gather | solution.py:172
  659.2 305.1 %reduce-scatter.20.cloned.1.call-start = ((), (), s32[]{:S(2)}) async-start(), calls=%async_computation.21 | async-start | bytes 6291456 | tf_op jit(solution)/shard_map/reduce_scatter | solution.py:232
  874.5 25.6 %copy-start.44 = (bf16[1024,2048]{1,0:T(8,128)(2,1)S(1)}, bf16[1024,2048]{1,0:T(8,128)(2,1)}, u32[]{:S(2)}) copy-start(bf16[1024,2048]{1,0:T(8,128)(2,1)} %all-gather.24.cloned.1.call-done) | copy-start | bytes 12582916
  896.8 3.4 copy-start.47
  911.4 117.9 %all-gather.30.cloned.1.call-start = ((), (), s32[]{:S(2)}) async-start(), calls=%async_computation.22 | async-start | bytes 6291456 | tf_op jit(solution)/shard_map/all_gather | solution.py:239
  964.3 4.8 copy-start.7
  964.3 4.8 copy-start.8
  964.3 4.9 copy-start.9
  969.1 3.2 copy-start.38
  969.2 60.1 %copy-start.46 = (bf16[1024,512]{1,0:T(8,128)(2,1)S(1)}, bf16[1024,512]{1,0:T(8,128)(2,1)}, u32[]{:S(2)}) copy-start(bf16[1024,512]{1,0:T(8,128)(2,1)} %all-gather.20.cloned.1.call-done) | copy-start | bytes 3145732
  972.4 662.8 %reduce-scatter.22.cloned.1.call-start = ((), (), s32[]{:S(2)}) async-start(), calls=%async_computation.23 | async-start | bytes 10485760 | tf_op jit(solution)/shard_map/reduce_scatter | solution.py:268
  1040.7 5.9 copy-start.5
  1055.6 9.2 slice-start
  1056.0 8.9 slice-start.1
  1081.5 9.2 slice-start
  1081.8 8.9 slice-start.1
  1107.4 9.2 slice-start
  1107.7 8.9 slice-start.1
  1135.6 5.9 copy-start.4
  1135.6 5.9 copy-start.13
  1135.6 5.9 copy-start.22
  1150.5 9.1 slice-start.2
  1150.8 8.8 slice-start.3
  1176.2 9.0 slice-start.2
  1176.6 8.7 slice-start.3
  1201.9 9.0 slice-start.2
  1202.3 8.7 slice-start.3
  1219.3 6.2 copy-start.10
  1231.8 477.7 %reduce-scatter.24.cloned.1.call-start = ((), (), s32[]{:S(2)}) async-start(), calls=%async_computation.24 | async-start | bytes 10485760 | tf_op jit(solution)/shard_map/reduce_scatter | solution.py:271
  1248.1 549.2 %reduce-scatter.26.cloned.1.call-start = ((), (), s32[]{:S(2)}) async-start(), calls=%async_computation.25 | async-start | bytes 6291456 | tf_op jit(solution)/shard_map/reduce_scatter | solution.py:290
  1709.5 6.0 copy-start.45
  1724.2 131.0 %reduce-scatter.36.cloned.1.call-start = ((), (), s32[]{:S(2)}) async-start(), calls=%async_computation.32 | async-start | bytes 4456448
  1747.7 182.9 %reduce-scatter.32.cloned.1.call-start = ((), (), s32[]{:S(2)}) async-start(), calls=%async_computation.28 | async-start | bytes 4456448 | tf_op jit(solution)/shard_map/reduce_scatter | solution.py:307
  1762.2 229.4 %reduce-scatter.30.cloned.1.call-start = ((), (), s32[]{:S(2)}) async-start(), calls=%async_computation.27 | async-start | bytes 1114112 | tf_op jit(solution)/shard_map/reduce_scatter | solution.py:304
  1769.3 291.2 %reduce-scatter.28.cloned.1.call-start = ((), (), s32[]{:S(2)}) async-start(), calls=%async_computation.26 | async-start | bytes 3342336 | tf_op jit(solution)/shard_map/reduce_scatter | solution.py:301
  1780.7 335.3 %reduce-scatter.18.cloned.1.call-start = ((), (), s32[]{:S(2)}) async-start(), calls=%async_computation.19 | async-start | bytes 6291456 | tf_op jit(solution)/shard_map/reduce_scatter | solution.py:222
  1797.3 5.0 copy-start.40
  1797.3 380.3 %reduce-scatter.34.cloned.1.call-start = ((), (), s32[]{:S(2)}) async-start(), calls=%async_computation.31 | async-start | bytes 1114112
  1802.3 313.8 %copy-start.24 = (f32[2,1024]{1,0:T(2,128)S(1)}, f32[2,1024]{1,0:T(2,128)}, u32[]{:S(2)}) copy-start(f32[2,1024]{1,0:T(2,128)} %get-tuple-element.637) | copy-start | bytes 24580
  1802.3 313.8 %copy-start.26 = (f32[2,512]{1,0:T(2,128)S(1)}, f32[2,512]{1,0:T(2,128)}, u32[]{:S(2)}) copy-start(f32[2,512]{1,0:T(2,128)} %copy-done.25) | copy-start | bytes 12292
  1802.3 313.8 %copy-start.31 = (f32[2,512]{1,0:T(2,128)S(1)}, f32[2,512]{1,0:T(2,128)}, u32[]{:S(2)}) copy-start(f32[2,512]{1,0:T(2,128)} %copy-done.30) | copy-start | bytes 12292
  1802.3 313.8 %copy-start.37 = (f32[2,512]{1,0:T(2,128)S(1)}, f32[2,512]{1,0:T(2,128)}, u32[]{:S(2)}) copy-start(f32[2,512]{1,0:T(2,128)} %copy-done.36) | copy-start | bytes 12292
  1802.3 313.8 %copy-start.39 = (f32[2,512]{1,0:T(2,128)S(1)}, f32[2,512]{1,0:T(2,128)}, u32[]{:S(2)}) copy-start(f32[2,512]{1,0:T(2,128)} %copy-done.38) | copy-start | bytes 12292
  (20 other events, 39.5 us)
Sparse Core Ops, SparseCore 0:
  10.8 40.6 all-gather.13
  54.3 44.3 all-gather.17
  100.8 55.5 all-gather.15
  181.4 58.2 all-gather.33
  241.7 58.2 all-gather.31
  302.6 37.9 all-gather.19
  409.5 242.5 reduce-scatter.15
  655.1 50.5 all-gather.23
  707.2 55.2 all-gather.21
  764.0 56.7 all-gather.27
  823.7 50.7 all-gather.25
  911.5 52.7 reduce-scatter.19
  972.5 56.7 all-gather.29
  1231.9 403.1 reduce-scatter.21
  1637.7 71.6 reduce-scatter.23
  1724.3 54.2 reduce-scatter.25
  1782.8 72.3 reduce-scatter.35
  1858.9 71.5 reduce-scatter.31
  1935.1 56.3 reduce-scatter.29
  1995.2 65.2 reduce-scatter.27
  2062.8 53.2 reduce-scatter.17
  2120.2 57.3 reduce-scatter.33
where the time goes:
time: 2220 us; the launch traced here: 2190 us
  waiting for transfers between devices  1580 us (71%)
  matrix products  334 us (15%)
  local copies, waits for them, and re-layouts  105 us (5%)
  other arithmetic  105 us (5%)
  loops' own time  39.8 us (2%)
    reduce_scatter x1, waiting for transfers between devices, body(): lax.psum_scatter(jnp.stack(key_grads).astype(jnp.bfloat16), 'ctx', scatte...  383 us
    reduce_scatter x1, waiting for transfers between devices, body(): lax.psum_scatter(attn_part.astype(jnp.bfloat16), 'tp', scatter_dimension=...  241 us
    unnamed x24, waiting for transfers between devices  95.5 us
    reduce_scatter x1, waiting for transfers between devices, body(): lax.psum_scatter(jnp.stack(value_grads).astype(jnp.bfloat16), 'ctx', scat...  74.3 us
    reduce_scatter x1, waiting for transfers between devices, body(): lax.psum_scatter(grad_up.astype(jnp.bfloat16), ('fsdp', 'ctx'), scatter_d...  73.1 us
    reduce_scatter x1, waiting for transfers between devices, body(): lax.psum_scatter(grad_qkv.astype(jnp.bfloat16), ('fsdp', 'ctx'), scatter_...  67.4 us
    reduce_scatter x1, waiting for transfers between devices, body(): lax.psum_scatter(grad_proj.astype(jnp.bfloat16), ('fsdp', 'ctx'), scatter...  59.3 us
    all_gather x1, waiting for transfers between devices, body(): normed_all = lax.all_gather(normed, 'tp', axis=1, tiled=True)  57.7 us
  transfers between devices with their start and end apart: 22, of which 20 were waited for; matrix products, arithmetic and copies ran while one was open for 12% of the time, Pallas kernels for 0%

commit v1 on v0

--- a/solution.py
+++ b/solution.py
@@ -1,6 +1,10 @@
+import functools
+
 import jax
 import jax.numpy as jnp
 from jax import lax
+from jax.experimental import pallas as pl
+from jax.experimental.pallas import tpu as pltpu
 from jax.sharding import PartitionSpec as P
 
 HEAD_DIM = 64
@@ -322,6 +326,903 @@
     )
 
 
+def params(limit=58):
+    return pltpu.CompilerParams(vmem_limit_bytes=limit * 1024 * 1024)
+
+
+def whole(shape):
+    zeros = (0,) * len(shape)
+    return pl.BlockSpec(shape, lambda *_: zeros, pipeline_mode=pl.Buffered(1))
+
+
+def cost(flops, nbytes, exps=0):
+    return pl.CostEstimate(flops=int(flops), bytes_accessed=int(nbytes), transcendentals=int(exps))
+
+
+def dot_nn(left, right):
+    return jnp.dot(left, right, preferred_element_type=jnp.float32)
+
+
+def dot_nt(left, right):
+    return lax.dot_general(left, right, (((1,), (1,)), ((), ())), preferred_element_type=jnp.float32)
+
+
+def transposed(values):
+    return values.astype(jnp.float32).T.astype(values.dtype)
+
+
+def turned_apart(into_ref, values, chunk_at, chunks):
+    turned = values.astype(jnp.float32).T.astype(values.dtype)
+    high = turned.shape[0] // chunks
+    bits = chunks.bit_length() - 1
+    for chunk in range(chunks):
+        apart = chunk ^ chunk_at
+        place = 0
+        for bit in range(bits):
+            place += ((apart >> bit) & 1) << (bits - 1 - bit)
+        into_ref[pl.ds(pl.multiple_of(place * high, high), high), :] = turned[
+            chunk * high : (chunk + 1) * high, :
+        ]
+
+
+def low_lanes(shape):
+    return lax.broadcasted_iota(jnp.int32, shape, 1) < HEAD_DIM
+
+
+def pair_apart(stored):
+    first, second, third = stored[:, :128], stored[:, 128:256], stored[:, 256:]
+    low = low_lanes(first.shape)
+    keys = pltpu.roll(jnp.where(low, third, first), HEAD_DIM, 1)
+    return jnp.concatenate(
+        [jnp.where(low, first, second), keys, jnp.where(low, second, third)], axis=1
+    )
+
+
+def pair_together(query, keys, values):
+    low = low_lanes(query.shape)
+    turned = pltpu.roll(keys, HEAD_DIM, 1)
+    return jnp.concatenate(
+        [jnp.where(low, query, turned), jnp.where(low, values, query), jnp.where(low, turned, values)],
+        axis=1,
+    )
+
+
+def project_kernel(te_ref, tok_ref, w_ref, qkv_ref, normed_ref, scales_ref, *, tiles, k_rows, q_cols, t_cols):
+    step = pl.program_id(0)
+    chunks, halves = w_ref.shape[0], w_ref.shape[1]
+
+    @pl.when(step == 0)
+    def _():
+        exact = te_ref[...]
+        high = exact.astype(jnp.bfloat16)
+        rest = exact - high.astype(jnp.float32)
+        middle = rest.astype(jnp.bfloat16)
+        last = (rest - middle.astype(jnp.float32)).astype(jnp.bfloat16)
+        folds = w_ref.shape[2] // k_rows
+        for half in range(halves):
+            for fold in range(folds):
+                weights = w_ref[:, half, fold * k_rows : (fold + 1) * k_rows, q_cols : q_cols + t_cols]
+                weights = weights.reshape(chunks * k_rows, t_cols)
+                total = dot_nn(last, weights) + dot_nn(middle, weights) + dot_nn(high, weights)
+                at = (half * folds + fold) * t_cols
+                scales_ref[:, at : at + t_cols] = 1.0 + total
+
+    row = step // tiles
+    values = tok_ref[0].astype(jnp.float32)
+    width = values.shape[1]
+    hat, _ = normalize(values)
+    normed = (hat * scales_ref[pl.ds(row, 1), :width]).astype(jnp.bfloat16)
+    normed_ref[0] = normed
+    pair = 6 * HEAD_DIM
+    for half in range(halves):
+        weights = w_ref[:, half, :, :q_cols].reshape(width, q_cols)
+        out = dot_nn(normed, weights)
+        for group in range(q_cols // pair):
+            qkv_ref[half * (q_cols // pair) + group, 0] = pair_apart(
+                out[:, group * pair : (group + 1) * pair]
+            ).astype(jnp.bfloat16)
+
+
+def project(time_embed, tokens, w_all, k_rows, q_cols, t_cols):
+    rows, length, width = tokens.shape
+    chunks, halves = w_all.shape[:2]
+    groups = halves * q_cols // (6 * HEAD_DIM)
+    tile = 256
+    tiles = length // tile
+    return pl.pallas_call(
+        functools.partial(project_kernel, tiles=tiles, k_rows=k_rows, q_cols=q_cols, t_cols=t_cols),
+        grid=(rows * tiles,),
+        in_specs=[
+            whole(time_embed.shape),
+            pl.BlockSpec((1, tile, width), lambda i: (i // tiles, i % tiles, 0)),
+            whole(w_all.shape),
+        ],
+        out_specs=[
+            pl.BlockSpec((groups, 1, tile, 6 * HEAD_DIM), lambda i: (0, i // tiles, i % tiles, 0)),
+            pl.BlockSpec((1, tile, width), lambda i: (i // tiles, i % tiles, 0)),
+            whole((rows, 2 * width)),
+        ],
+        out_shape=[
+            jax.ShapeDtypeStruct((groups, rows, length, 6 * HEAD_DIM), jnp.bfloat16),
+            jax.ShapeDtypeStruct(tokens.shape, jnp.bfloat16),
+            jax.ShapeDtypeStruct((rows, 2 * width), jnp.float32),
+        ],
+        compiler_params=params(),
+        cost_estimate=cost(2 * rows * length * width * halves * q_cols, 2 * w_all.size + 10 * tokens.size),
+        name="project",
+    )(time_embed, tokens, w_all)
+
+
+def tile_mask(segc_ref, segr_ref, key_block, query_block):
+    key_at = pl.multiple_of(key_block * BLK, BLK)
+    query_at = pl.multiple_of(query_block * BLK, BLK)
+    same = segc_ref[0, pl.ds(key_at, BLK), :] == segr_ref[0, :, pl.ds(query_at, BLK)]
+    key_pos = key_at + lax.broadcasted_iota(jnp.int32, (BLK, BLK), 0)
+    query_pos = query_at + lax.broadcasted_iota(jnp.int32, (BLK, BLK), 1)
+    return same & (key_pos <= query_pos)
+
+
+def split_heads(values):
+    low = low_lanes(values.shape)
+    zero = jnp.zeros_like(values)
+    return jnp.concatenate([jnp.where(low, values, zero), jnp.where(low, zero, values)], axis=0)
+
+
+def is_full(edge_ref, row, blocks, key_block, query_block):
+    same = edge_ref[row, key_block] == edge_ref[row, blocks + query_block]
+    return same & (key_block < query_block)
+
+
+def attend_kernel(listed_ref, edge_ref, qkv_ref, segc_ref, segr_ref, mixed_ref, lse_ref, vt_ref, qz_ref, acc_ref, stat_ref):
+    row = pl.program_id(0)
+    blocks = qkv_ref.shape[0]
+
+    def turn(block, carried):
+        at = pl.multiple_of(block * BLK, BLK)
+        vt_ref[:, pl.ds(at, BLK)] = transposed(qkv_ref[block, 0, :, 256:384])
+        return carried
+
+    lax.fori_loop(0, blocks, turn, 0)
+
+    def one_query(query_block, carried):
+        query = qkv_ref[query_block, 0, :, :128].astype(jnp.float32) * HEAD_DIM ** (-0.5)
+        qz_ref[...] = split_heads(query.astype(jnp.bfloat16))
+        stat_ref[0:1, :] = jnp.full((1, 2 * BLK), masked_out, jnp.float32)
+        stat_ref[1:2, :] = jnp.zeros((1, 2 * BLK), jnp.float32)
+        acc_ref[...] = jnp.zeros(acc_ref.shape, jnp.float32)
+
+        def update(key_block, mask):
+            scores = dot_nt(qkv_ref[key_block, 0, :, 128:256], qz_ref[...])
+            if mask is not None:
+                scores = jnp.concatenate(
+                    [
+                        jnp.where(mask, scores[:, :BLK], masked_out),
+                        jnp.where(mask, scores[:, BLK:], masked_out),
+                    ],
+                    axis=1,
+                )
+            old_max = stat_ref[0:1, :]
+            new_max = jnp.maximum(old_max, jnp.max(scores, axis=0, keepdims=True))
+            weights = jnp.exp(scores - new_max)
+            shrink = jnp.exp(old_max - new_max)
+            stat_ref[0:1, :] = new_max
+            stat_ref[1:2, :] = stat_ref[1:2, :] * shrink + jnp.sum(weights, axis=0, keepdims=True)
+            rounded = weights.astype(jnp.bfloat16)
+            at = pl.multiple_of(key_block * BLK, BLK)
+            for head in range(2):
+                part = slice(head * BLK, (head + 1) * BLK)
+                value = vt_ref[head * HEAD_DIM : (head + 1) * HEAD_DIM, pl.ds(at, BLK)]
+                acc_ref[:, part] = acc_ref[:, part] * shrink[:, part] + dot_nn(value, rounded[:, part])
+
+        def one_key(key_block, carried):
+            listed = listed_ref[row, query_block * blocks + key_block] != 0
+            full = is_full(edge_ref, row, blocks, key_block, query_block)
+
+            @pl.when(listed & full)
+            def _():
+                update(key_block, None)
+
+            @pl.when(listed & jnp.logical_not(full))
+            def _():
+                update(key_block, tile_mask(segc_ref, segr_ref, key_block, query_block))
+
+            return carried
+
+        lax.fori_loop(0, query_block + 1, one_key, 0)
+        total = stat_ref[1:2, :]
+        mixed = acc_ref[...] / total
+        mixed = jnp.concatenate([mixed[:, :BLK], mixed[:, BLK:]], axis=0).T
+        mixed_ref[query_block, 0] = mixed.astype(jnp.bfloat16)
+        log_total = stat_ref[0:1, :] + jnp.log(total)
+        at = pl.multiple_of(query_block * BLK, BLK)
+        lse_ref[0, 0:1, pl.ds(at, BLK)] = log_total[:, :BLK]
+        lse_ref[0, 1:2, pl.ds(at, BLK)] = log_total[:, BLK:]
+        return carried
+
+    lax.fori_loop(0, blocks, one_query, 0)
+
+
+def attend(listed, edges, qkv, segc, segr):
+    blocks, rows, blk, width = qkv.shape
+    length = blocks * blk
+    pair = 2 * HEAD_DIM
+    return pl.pallas_call(
+        attend_kernel,
+        grid_spec=pltpu.PrefetchScalarGridSpec(
+            num_scalar_prefetch=2,
+            grid=(rows,),
+            in_specs=[
+                pl.BlockSpec((blocks, 1, blk, width), lambda r, *_: (0, r, 0, 0)),
+                pl.BlockSpec((1, length, 1), lambda r, *_: (r, 0, 0)),
+                pl.BlockSpec((1, 1, length), lambda r, *_: (r, 0, 0)),
+            ],
+            out_specs=[
+                pl.BlockSpec((blocks, 1, blk, pair), lambda r, *_: (0, r, 0, 0)),
+                pl.BlockSpec((1, 2, length), lambda r, *_: (r, 0, 0)),
+            ],
+            scratch_shapes=[
+                pltpu.VMEM((pair, length), jnp.bfloat16),
+                pltpu.VMEM((2 * blk, pair), jnp.bfloat16),
+                pltpu.VMEM((HEAD_DIM, 2 * blk), jnp.float32),
+                pltpu.VMEM((2, 2 * blk), jnp.float32),
+            ],
+        ),
+        out_shape=[
+            jax.ShapeDtypeStruct((blocks, rows, blk, pair), jnp.bfloat16),
+            jax.ShapeDtypeStruct((rows, 2, length), jnp.float32),
+        ],
+        compiler_params=params(),
+        cost_estimate=cost(30e9, 12e6, 40e6),
+        name="attend",
+    )(listed, edges, qkv, segc, segr)
+
+
+def attend_back_kernel(
+    listed_ref, edge_ref, qkv_ref, grad_ref, mixed_ref, lse_ref, segc_ref, segr_ref, out_ref,
+    kt_ref, qz_ref, gz_ref, inner_ref, dq_ref, dk_ref, dv_ref,
+):
+    row = pl.program_id(0)
+    blocks = qkv_ref.shape[0]
+    scale = HEAD_DIM ** (-0.5)
+
+    def prepare(block, carried):
+        at = pl.multiple_of(block * BLK, BLK)
+        kt_ref[:, pl.ds(at, BLK)] = transposed(qkv_ref[block, 0, :, 128:256])
+        query = qkv_ref[block, 0, :, :128].astype(jnp.float32) * scale
+        qz_ref[block] = split_heads(query.astype(jnp.bfloat16))
+        grad = grad_ref[block, 0]
+        gz_ref[block] = split_heads(grad)
+        product = (grad.astype(jnp.float32) * mixed_ref[block, 0].astype(jnp.float32)).T
+        for head in range(2):
+            part = product[head * HEAD_DIM : (head + 1) * HEAD_DIM, :]
+            inner_ref[head : head + 1, pl.ds(at, BLK)] = jnp.sum(part, axis=0, keepdims=True)
+        return carried
+
+    lax.fori_loop(0, blocks, prepare, 0)
+    dq_ref[...] = jnp.zeros(dq_ref.shape, jnp.float32)
+
+    def one_key(key_block, carried):
+        dk_ref[...] = jnp.zeros(dk_ref.shape, jnp.float32)
+        dv_ref[...] = jnp.zeros(dv_ref.shape, jnp.float32)
+        key_at = pl.multiple_of(key_block * BLK, BLK)
+
+        def update(query_block, mask):
+            query_at = pl.multiple_of(query_block * BLK, BLK)
+            keys = qkv_ref[key_block, 0, :, 128:256]
+            values = qkv_ref[key_block, 0, :, 256:384]
+            for head in range(2):
+                part = slice(head * BLK, (head + 1) * BLK)
+                query = qz_ref[query_block, part, :]
+                grad = gz_ref[query_block, part, :]
+                scores = dot_nt(keys, query)
+                probs = jnp.exp(scores - lse_ref[0, head : head + 1, pl.ds(query_at, BLK)])
+                if mask is not None:
+                    probs = jnp.where(mask, probs, 0.0)
+                grad_probs = dot_nt(values, grad)
+                grad_scores = probs * (grad_probs - inner_ref[head : head + 1, pl.ds(query_at, BLK)])
+                probs = probs.astype(jnp.bfloat16)
+                grad_scores = grad_scores.astype(jnp.bfloat16)
+                dv_ref[...] += dot_nn(probs, grad)
+                dk_ref[...] += dot_nn(grad_scores, query)
+                lanes = slice(head * HEAD_DIM, (head + 1) * HEAD_DIM)
+                dq_ref[lanes, pl.ds(query_at, BLK)] += dot_nn(
+                    kt_ref[lanes, pl.ds(key_at, BLK)], grad_scores
+                )
+
+        def one_query(query_block, carried):
+            listed = listed_ref[row, query_block * blocks + key_block] != 0
+            full = is_full(edge_ref, row, blocks, key_block, query_block)
+
+            @pl.when(listed & full)
+            def _():
+                update(query_block, None)
+
+            @pl.when(listed & jnp.logical_not(full))
+            def _():
+                update(query_block, tile_mask(segc_ref, segr_ref, key_block, query_block))
+
+            return carried
+
+        lax.fori_loop(key_block, blocks, one_query, 0)
+        grad_query = dq_ref[:, pl.ds(key_at, BLK)].T * scale
+        out_ref[key_block, 0] = pair_together(grad_query, dk_ref[...], dv_ref[...]).astype(jnp.bfloat16)
+        return carried
+
+    lax.fori_loop(0, blocks, one_key, 0)
+
+
+def attend_back(listed, edges, qkv, grad, mixed, lse, segc, segr):
+    blocks, rows, blk, width = qkv.shape
+    length = blocks * blk
+    pair = 2 * HEAD_DIM
+    wide = pl.BlockSpec((blocks, 1, blk, width), lambda r, *_: (0, r, 0, 0))
+    narrow = pl.BlockSpec((blocks, 1, blk, pair), lambda r, *_: (0, r, 0, 0))
+    return pl.pallas_call(
+        attend_back_kernel,
+        grid_spec=pltpu.PrefetchScalarGridSpec(
+            num_scalar_prefetch=2,
+            grid=(rows,),
+            in_specs=[
+                wide,
+                narrow,
+                narrow,
+                pl.BlockSpec((1, 2, length), lambda r, *_: (r, 0, 0)),
+                pl.BlockSpec((1, length, 1), lambda r, *_: (r, 0, 0)),
+                pl.BlockSpec((1, 1, length), lambda r, *_: (r, 0, 0)),
+            ],
+            out_specs=wide,
+            scratch_shapes=[
+                pltpu.VMEM((pair, length), jnp.bfloat16),
+                pltpu.VMEM((blocks, 2 * blk, pair), jnp.bfloat16),
+                pltpu.VMEM((blocks, 2 * blk, pair), jnp.bfloat16),
+                pltpu.VMEM((2, length), jnp.float32),
+                pltpu.VMEM((pair, length), jnp.float32),
+                pltpu.VMEM((blk, pair), jnp.float32),
+                pltpu.VMEM((blk, pair), jnp.float32),
+            ],
+        ),
+        out_shape=jax.ShapeDtypeStruct(qkv.shape, jnp.bfloat16),
+        compiler_params=params(),
+        cost_estimate=cost(70e9, 20e6, 40e6),
+        name="attend_back",
+    )(listed, edges, qkv, grad, mixed, lse, segc, segr)
+
+
+def joined(ref, first, count):
+    return jnp.concatenate([ref[first + i, 0] for i in range(count)], axis=1)
+
+
+def outward_kernel(mixed_ref, tok_ref, w_ref, scales_ref, hidden_ref, normed_ref, *, tiles):
+    row = pl.program_id(0) // tiles
+    halves = w_ref.shape[1]
+    per_half = mixed_ref.shape[0] // halves
+    hidden = tok_ref[0].astype(jnp.float32)
+    width = hidden.shape[1]
+    for half in range(halves):
+        hidden += dot_nt(joined(mixed_ref, half * per_half, per_half), w_ref[:, half].reshape(width, -1))
+    hidden_ref[0] = hidden
+    hat, _ = normalize(hidden)
+    normed_ref[0] = (hat * scales_ref[pl.ds(row, 1), width:]).astype(jnp.bfloat16)
+
+
+def outward(mixed, tokens, w_all, scales, columns):
+    rows, length, width = tokens.shape
+    groups, _, _, pair = mixed.shape
+    chunks, halves, high, _ = w_all.shape
+    tile = 256
+    tiles = length // tile
+    one = pl.BlockSpec((1, tile, width), lambda i: (i // tiles, i % tiles, 0))
+    return pl.pallas_call(
+        functools.partial(outward_kernel, tiles=tiles),
+        grid=(rows * tiles,),
+        in_specs=[
+            pl.BlockSpec((groups, 1, tile, pair), lambda i: (0, i // tiles, i % tiles, 0)),
+            one,
+            whole((chunks, halves, high, columns)),
+            whole(scales.shape),
+        ],
+        out_specs=[one, one],
+        out_shape=[
+            jax.ShapeDtypeStruct(tokens.shape, jnp.float32),
+            jax.ShapeDtypeStruct(tokens.shape, jnp.bfloat16),
+        ],
+        compiler_params=params(),
+        cost_estimate=cost(2 * rows * length * width * width, 12 * tokens.size),
+        name="outward",
+    )(mixed, tokens, w_all, scales)
+
+
+def mlp_kernel(
+    me_ref, nm_ref, cot_ref, hidden_ref, scales_ref, up_ref, down_ref,
+    up_keep_ref, up_send_ref, down_keep_ref, down_send_ref,
+    layer_ref, grad_hidden_ref, grad_attn_ref, gscale_ref,
+    nmt_ref, cott_ref, out_ref, gn_ref, act_ref, gpre_ref,
+):
+    tile = pl.program_id(0)
+    phase = pl.program_id(1)
+    count, width = nm_ref.shape
+    chunk = 256
+    root = 0.7978845608028654
+    cube = 0.044715
+
+    @pl.when((tile == 0) & (phase == 0))
+    def _():
+        turned_apart(nmt_ref, nm_ref[...], me_ref[0], up_ref.shape[0])
+        turned_apart(cott_ref, cot_ref[...], me_ref[0], up_ref.shape[0])
+        out_ref[...] = jnp.zeros(out_ref.shape, jnp.float32)
+        gn_ref[...] = jnp.zeros(gn_ref.shape, jnp.float32)
+
+    @pl.when(phase == 0)
+    def _():
+        up = up_ref[:, 0].reshape(width, -1)
+        down = down_ref[:, 0].reshape(width, -1)
+        for at in range(0, count, chunk):
+            part = slice(at, at + chunk)
+            pre = dot_nn(nm_ref[part, :], up)
+            grad_act = dot_nn(cot_ref[part, :], down)
+            square = pre * pre
+            bent = jnp.tanh(root * (pre + cube * pre * square))
+            half = 0.5 * (1.0 + bent)
+            act_ref[part, :] = (pre * half).astype(jnp.bfloat16)
+            slope = half + (0.5 * root) * pre * (1.0 - bent * bent) * (1.0 + (3.0 * cube) * square)
+            gpre_ref[part, :] = (grad_act * slope).astype(jnp.bfloat16)
+        grad = dot_nn(nmt_ref[...], gpre_ref[...]).astype(jnp.bfloat16)
+        shape = up_keep_ref.shape[1:]
+        up_keep_ref[0] = grad[: width // 2].reshape(shape)
+        up_send_ref[0] = grad[width // 2 :].reshape(shape)
+
+    @pl.when(phase == 1)
+    def _():
+        up = up_ref[:, 0].reshape(width, -1)
+        down = down_ref[:, 0].reshape(width, -1)
+        out_ref[...] += dot_nt(act_ref[...], down)
+        gn_ref[...] += dot_nt(gpre_ref[...], up)
+        grad = dot_nn(cott_ref[...], act_ref[...]).astype(jnp.bfloat16)
+        shape = (down_keep_ref.shape[0],) + down_keep_ref.shape[2:]
+        down_keep_ref[:, 0] = grad[: width // 2].reshape(shape)
+        down_send_ref[:, 0] = grad[width // 2 :].reshape(shape)
+
+    @pl.when((tile == pl.num_programs(0) - 1) & (phase == 1))
+    def _():
+        rows = scales_ref.shape[0]
+        per_row = count // rows
+        for row in range(rows):
+            scale = scales_ref[row : row + 1, width:]
+            total = jnp.zeros((1, width), jnp.float32)
+            for at in range(row * per_row, (row + 1) * per_row, chunk):
+                part = slice(at, at + chunk)
+                hidden = hidden_ref[part, :]
+                layer_ref[part, :] = (hidden + out_ref[part, :]).astype(jnp.bfloat16)
+                hat, inverse = normalize(hidden)
+                grad = gn_ref[part, :]
+                total += jnp.sum(grad * hat, axis=0, keepdims=True)
+                back = cot_ref[part, :].astype(jnp.float32) + normalize_back(grad * scale, hat, inverse)
+                grad_hidden_ref[part, :] = back
+                grad_attn_ref[part, :] = back.astype(jnp.bfloat16)
+            gscale_ref[row : row + 1, :] = total
+
+
+def mlp(me, normed, cotangent, hidden, scales, w_all, skip, hidden_cols):
+    rows, length, width = hidden.shape
+    count = rows * length
+    chunks, halves, high, columns = w_all.shape
+    tile = 512
+    per_half = hidden_cols // tile
+    first = skip // tile
+    quarter = chunks // 4
+    flat = (count, width)
+    up_at = lambda f, s, me: (0, f // per_half, 0, first + f % per_half)
+    down_at = lambda f, s, me: (0, f // per_half, 0, first + per_half + f % per_half)
+    up_out = pl.BlockSpec(
+        (1, 2, quarter, high, tile), lambda f, s, me: ((f // per_half) ^ me[1], 0, 0, 0, f % per_half)
+    )
+    down_out = pl.BlockSpec(
+        (2, 1, quarter, high, tile), lambda f, s, me: (0, (f // per_half) ^ me[1], 0, 0, f % per_half)
+    )
+    grads = jax.ShapeDtypeStruct((2, 2, quarter, high, hidden_cols), jnp.bfloat16)
+    return pl.pallas_call(
+        mlp_kernel,
+        grid_spec=pltpu.PrefetchScalarGridSpec(
+            num_scalar_prefetch=1,
+            grid=(halves * per_half, 2),
+            in_specs=[
+                whole(flat),
+                whole(flat),
+                whole(flat),
+                whole(scales.shape),
+                pl.BlockSpec((chunks, 1, high, tile), up_at),
+                pl.BlockSpec((chunks, 1, high, tile), down_at),
+            ],
+            out_specs=[up_out, up_out, down_out, down_out]
+            + [whole(flat), whole(flat), whole(flat), whole((rows, width))],
+            scratch_shapes=[
+                pltpu.VMEM((width, count), jnp.bfloat16),
+                pltpu.VMEM((width, count), jnp.bfloat16),
+                pltpu.VMEM(flat, jnp.float32),
+                pltpu.VMEM(flat, jnp.float32),
+                pltpu.VMEM((count, tile), jnp.bfloat16),
+                pltpu.VMEM((count, tile), jnp.bfloat16),
+            ],
+        ),
+        out_shape=[grads] * 4
+        + [
+            jax.ShapeDtypeStruct(flat, jnp.bfloat16),
+            jax.ShapeDtypeStruct(flat, jnp.float32),
+            jax.ShapeDtypeStruct(flat, jnp.bfloat16),
+            jax.ShapeDtypeStruct((rows, width), jnp.float32),
+        ],
+        compiler_params=params(60),
+        cost_estimate=cost(12 * count * width * halves * hidden_cols, 4 * w_all.size + 16 * count * width),
+        name="mlp",
+    )(me, normed.reshape(flat), cotangent.reshape(flat), hidden.reshape(flat), scales, w_all, w_all)
+
+
+def grad_mixed_kernel(grad_ref, w_ref, out_ref):
+    halves = w_ref.shape[1]
+    per_half = out_ref.shape[0] // halves
+    grad = grad_ref[...]
+    pair = out_ref.shape[3]
+    for half in range(halves):
+        out = dot_nn(grad, w_ref[:, half].reshape(grad.shape[1], -1)).astype(jnp.bfloat16)
+        for group in range(per_half):
+            out_ref[half * per_half + group, 0] = out[:, group * pair : (group + 1) * pair]
+
+
+def grad_mixed_of(grad_attn, w_all, mixed_shape, columns):
+    groups, rows, length, pair = mixed_shape
+    chunks, halves, high, _ = w_all.shape
+    width = grad_attn.shape[1]
+    tile = 256
+    tiles = length // tile
+    return pl.pallas_call(
+        grad_mixed_kernel,
+        grid=(rows * tiles,),
+        in_specs=[
+            pl.BlockSpec((tile, width), lambda i: (i, 0)),
+            whole((chunks, halves, high, columns)),
+        ],
+        out_specs=pl.BlockSpec((groups, 1, tile, pair), lambda i: (0, i // tiles, i % tiles, 0)),
+        out_shape=jax.ShapeDtypeStruct(mixed_shape, jnp.bfloat16),
+        compiler_params=params(),
+        cost_estimate=cost(2 * rows * length * width * width, 8 * rows * length * width),
+        name="grad_mixed",
+    )(grad_attn, w_all)
+
+
+def grad_proj_kernel(me_ref, grad_ref, mixed_ref, keep_ref, send_ref, turned_ref):
+    count, width = grad_ref.shape
+
+    @pl.when(pl.program_id(0) == 0)
+    def _():
+        turned_apart(turned_ref, grad_ref[...], me_ref[0], 4 * keep_ref.shape[2])
+
+    pair = mixed_ref.shape[3]
+    mixed = jnp.concatenate(
+        [mixed_ref[i].reshape(count, pair) for i in range(mixed_ref.shape[0])], axis=1
+    )
+    grad = dot_nn(turned_ref[...], mixed).astype(jnp.bfloat16)
+    shape = keep_ref.shape[1:]
+    keep_ref[0] = grad[: width // 2].reshape(shape)
+    send_ref[0] = grad[width // 2 :].reshape(shape)
+
+
+def grad_proj_of(me, grad_attn, mixed, chunks, halves, columns):
+    groups, rows, length, pair = mixed.shape
+    count, width = grad_attn.shape
+    high = width // chunks
+    shape = (halves, 2, chunks // 4, high, columns)
+    one = pl.BlockSpec((1,) + shape[1:], lambda h, me: (h ^ me[1], 0, 0, 0, 0))
+    return pl.pallas_call(
+        grad_proj_kernel,
+        grid_spec=pltpu.PrefetchScalarGridSpec(
+            num_scalar_prefetch=1,
+            grid=(halves,),
+            in_specs=[
+                whole(grad_attn.shape),
+                pl.BlockSpec((groups // halves, rows, length, pair), lambda h, me: (h, 0, 0, 0)),
+            ],
+            out_specs=[one, one],
+            scratch_shapes=[pltpu.VMEM((width, count), jnp.bfloat16)],
+        ),
+        out_shape=[jax.ShapeDtypeStruct(shape, jnp.bfloat16)] * 2,
+        compiler_params=params(),
+        cost_estimate=cost(2 * count * width * width, 6 * count * width),
+        name="grad_proj",
+    )(me, grad_attn, mixed)
+
+
+def first_norm_kernel(gq_ref, tok_ref, grad_hidden_ref, w_ref, scales_ref, out_ref, gscale_ref, *, tiles, q_cols):
+    step = pl.program_id(0)
+    row = step // tiles
+    halves = w_ref.shape[1]
+    per_half = gq_ref.shape[0] // halves
+    values = tok_ref[0].astype(jnp.float32)
+    width = values.shape[1]
+    grad = jnp.zeros(values.shape, jnp.float32)
+    for half in range(halves):
+        weights = w_ref[:, half, :, :q_cols].reshape(width, q_cols)
+        grad += dot_nt(joined(gq_ref, half * per_half, per_half), weights)
+    hat, inverse = normalize(values)
+    total = jnp.sum(grad * hat, axis=0, keepdims=True)
+
+    @pl.when(step % tiles == 0)
+    def _():
+        gscale_ref[pl.ds(row, 1), :] = total
+
+    @pl.when(step % tiles != 0)
+    def _():
+        gscale_ref[pl.ds(row, 1), :] += total
+
+    back = normalize_back(grad * scales_ref[pl.ds(row, 1), :width], hat, inverse)
+    out_ref[0] = (grad_hidden_ref[0] + back).astype(jnp.bfloat16)
+
+
+def first_norm_back(grad_qkv, tokens, grad_hidden, w_all, scales, q_cols):
+    rows, length, width = tokens.shape
+    groups, _, _, pair = grad_qkv.shape
+    tile = 256
+    tiles = length // tile
+    one = pl.BlockSpec((1, tile, width), lambda i: (i // tiles, i % tiles, 0))
+    return pl.pallas_call(
+        functools.partial(first_norm_kernel, tiles=tiles, q_cols=q_cols),
+        grid=(rows * tiles,),
+        in_specs=[
+            pl.BlockSpec((groups, 1, tile, pair), lambda i: (0, i // tiles, i % tiles, 0)),
+            one,
+            one,
+            whole(w_all.shape),
+            whole(scales.shape),
+        ],
+        out_specs=[one, whole((rows, width))],
+        out_shape=[
+            jax.ShapeDtypeStruct(tokens.shape, jnp.bfloat16),
+            jax.ShapeDtypeStruct((rows, width), jnp.float32),
+        ],
+        compiler_params=params(),
+        cost_estimate=cost(2 * rows * length * width * groups * pair, 2 * w_all.size + 20 * tokens.size),
+        name="first_norm_back",
+    )(grad_qkv, tokens, grad_hidden, w_all, scales)
+
+
+def grad_qkv_kernel(
+    me_ref, normed_ref, gq_ref, tet_ref, gs_ref,
+    a_keep_ref, a_send_ref, b_keep_ref, b_send_ref, t_keep_ref, t_send_ref,
+    turned_ref, tet_apart_ref, *, pairs, chunks, folds, t_cols,
+):
+    half = pl.program_id(0)
+    part = pl.program_id(1)
+    count, width = normed_ref.shape
+
+    @pl.when((half == 0) & (part == 0))
+    def _():
+        turned_apart(turned_ref, normed_ref[...], me_ref[0], chunks)
+        bits = chunks.bit_length() - 1
+        high = tet_ref.shape[0] // chunks
+        for chunk in range(chunks):
+            apart = chunk ^ me_ref[0]
+            place = 0
+            for bit in range(bits):
+                place += ((apart >> bit) & 1) << (bits - 1 - bit)
+            tet_apart_ref[pl.ds(pl.multiple_of(place * high, high), high), :] = tet_ref[
+                chunk * high : (chunk + 1) * high, :
+            ]
+
+    def grad():
+        return dot_nn(turned_ref[...], gq_ref[0].reshape(count, -1)).astype(jnp.bfloat16)
+
+    @pl.when(part < pairs // 2)
+    def _():
+        found = grad()
+        shape = a_keep_ref.shape[1:]
+        a_keep_ref[0] = found[: width // 2].reshape(shape)
+        a_send_ref[0] = found[width // 2 :].reshape(shape)
+
+    @pl.when((part >= pairs // 2) & (part < pairs))
+    def _():
+        found = grad()
+        shape = (b_keep_ref.shape[0],) + b_keep_ref.shape[2:]
+        b_keep_ref[:, 0] = found[: width // 2].reshape(shape)
+        b_send_ref[:, 0] = found[width // 2 :].reshape(shape)
+
+    @pl.when(part == pairs)
+    def _():
+        k_rows = tet_ref.shape[0] // chunks
+        shape = t_keep_ref.shape[1:3] + (k_rows, t_cols)
+        for fold in range(folds):
+            at = pl.multiple_of((half * folds + fold) * t_cols, t_cols)
+            total = jnp.zeros((chunks * k_rows, t_cols), jnp.float32)
+            for row in range(gs_ref.shape[0]):
+                total += tet_apart_ref[:, row : row + 1] * gs_ref[row : row + 1, pl.ds(at, t_cols)]
+            total = total.astype(jnp.bfloat16)
+            middle = chunks * k_rows // 2
+            t_keep_ref[0, :, :, fold * k_rows : (fold + 1) * k_rows, :] = total[:middle].reshape(shape)
+            t_send_ref[0, :, :, fold * k_rows : (fold + 1) * k_rows, :] = total[middle:].reshape(shape)
+
+
+def grad_qkv_of(me, normed, grad_qkv, time_embed, grad_scales, chunks, halves, k_rows, t_cols):
+    rows, length, width = normed.shape
+    groups, _, _, pair = grad_qkv.shape
+    pairs = groups // halves
+    high = width // chunks
+    count = rows * length
+    quarter = chunks // 4
+    some = pairs // 2
+    turned = time_embed.T
+    a_out = pl.BlockSpec(
+        (1, 2, quarter, high, pair), lambda h, j, me: (h ^ me[1], 0, 0, 0, jnp.minimum(j, some - 1))
+    )
+    b_out = pl.BlockSpec(
+        (2, 1, quarter, high, pair),
+        lambda h, j, me: (0, h ^ me[1], 0, 0, jnp.clip(j - some, 0, some - 1)),
+    )
+    t_out = pl.BlockSpec((1, 2, quarter, high, t_cols), lambda h, j, me: (h ^ me[1], 0, 0, 0, 0))
+    wide = jax.ShapeDtypeStruct((halves, 2, quarter, high, some * pair), jnp.bfloat16)
+    thin = jax.ShapeDtypeStruct((halves, 2, quarter, high, t_cols), jnp.bfloat16)
+    return pl.pallas_call(
+        functools.partial(
+            grad_qkv_kernel, pairs=pairs, chunks=chunks, folds=high // k_rows, t_cols=t_cols
+        ),
+        grid_spec=pltpu.PrefetchScalarGridSpec(
+            num_scalar_prefetch=1,
+            grid=(halves, pairs + 1),
+            in_specs=[
+                whole((count, width)),
+                pl.BlockSpec(
+                    (1, rows, length, pair),
+                    lambda h, j, me: (h * pairs + jnp.minimum(j, pairs - 1), 0, 0, 0),
+                ),
+                whole(turned.shape),
+                whole(grad_scales.shape),
+            ],
+            out_specs=[a_out, a_out, b_out, b_out, t_out, t_out],
+            scratch_shapes=[
+                pltpu.VMEM((width, count), jnp.bfloat16),
+                pltpu.VMEM(turned.shape, jnp.float32),
+            ],
+        ),
+        out_shape=[wide] * 4 + [thin] * 2,
+        compiler_params=params(),
+        cost_estimate=cost(2 * count * width * groups * pair, 6 * count * width),
+        name="grad_qkv",
+    )(me, normed.reshape(count, width), grad_qkv, turned, grad_scales)
+
+
+def across(values, axis, apart):
+    size = lax.axis_size(axis)
+    return lax.ppermute(values, axis, [(i, i ^ apart) for i in range(size)])
+
+
+def summed(parts, index):
+    total = parts[0][index].astype(jnp.float32)
+    for part in parts[1:]:
+        total += part[index].astype(jnp.float32)
+    return total
+
+
+STAGES = {"x": ("ctx", 2), "y": ("tp", 1)}
+
+
+def scatter_sum(keep, send, order):
+    parts = [keep, across(send, "ctx", 1)]
+    for name in order:
+        axis, apart = STAGES[name]
+        given = across(summed(parts, 1).astype(jnp.bfloat16), axis, apart)
+        parts = [part[0] for part in parts] + [given]
+    given = across(summed(parts, slice(2, 4)).astype(jnp.bfloat16), "fsdp", 1)
+    parts = [part[:2] for part in parts] + [given]
+    given = across(summed(parts, 1).astype(jnp.bfloat16), "fsdp", 2)
+    parts = [part[0] for part in parts] + [given]
+    return summed(parts, slice(None))
+
+
+def listed_table(block_pairs, pair_counts, row_blocks, ctx_size):
+    rows, _, slots, _ = block_pairs.shape
+    packed = jnp.concatenate([block_pairs.reshape(rows, 1, slots * 2), pair_counts[:, :, None]], axis=2)
+    packed = jnp.concatenate(
+        [packed] + [across(packed, "ctx", apart) for apart in range(1, ctx_size)], axis=1
+    )
+    pairs = packed[:, :, : slots * 2].reshape(rows, ctx_size, slots, 2)
+    live = jnp.arange(slots, dtype=jnp.int32)[None, None, :] < packed[:, :, slots * 2 :]
+    owner = lax.axis_index("ctx") ^ jnp.arange(ctx_size, dtype=jnp.int32)[None, :, None]
+    base = owner * (row_blocks // ctx_size)
+    code = jnp.where(live, (base + pairs[..., 0]) * row_blocks + pairs[..., 1], -1)
+    code = code.reshape(rows, ctx_size * slots)
+    cells = jnp.arange(row_blocks * row_blocks, dtype=jnp.int32)
+    return jnp.any(code[:, :, None] == cells[None, None, :], axis=1).astype(jnp.int32)
+
+
+EVERY = ("fsdp", "ctx", "tp")
+GROUP = ("ctx", "tp")
+
+
+def spread_body(
+    tokens, time_embed, segment_ids, block_pairs, pair_counts,
+    w_time, w_qkv, w_out, w_up, w_down, cotangent,
+):
+    rows, length, width = tokens.shape
+    chunks = width // w_qkv.shape[0]
+    halves = lax.axis_size("tp")
+    high = w_qkv.shape[0]
+    q_cols, o_cols, f_cols = w_qkv.shape[1], w_out.shape[1], w_up.shape[1]
+    k_rows = w_time.shape[0]
+    t_all = w_time.shape[1] // halves
+    folds = high // k_rows
+    t_cols = t_all // folds
+    mine = lax.axis_index("tp")
+    me = jnp.stack([lax.axis_index("fsdp") * lax.axis_size("ctx") + lax.axis_index("ctx"), mine])
+    time_part = lax.dynamic_slice_in_dim(w_time, mine * t_all, t_all, 1)
+    time_part = time_part.reshape(k_rows, folds, t_cols).transpose(1, 0, 2).reshape(high, t_cols)
+    first = jnp.concatenate([w_qkv, time_part], axis=1).astype(jnp.bfloat16)
+    second = jnp.concatenate([w_out, w_up, w_down], axis=1).astype(jnp.bfloat16)
+    first = lax.all_gather(first, EVERY, axis=0, tiled=True).reshape(chunks, halves, high, -1)
+    second = lax.all_gather(second, EVERY, axis=0, tiled=True).reshape(chunks, halves, high, -1)
+
+    row_blocks = segment_ids.shape[1] // BLK
+    listed = listed_table(block_pairs, pair_counts, row_blocks, lax.axis_size("ctx"))
+    edges = jnp.concatenate([segment_ids[:, ::BLK], segment_ids[:, BLK - 1 :: BLK]], axis=1)
+    segc = segment_ids[:, :, None]
+    segr = segment_ids[:, None, :]
+
+    qkv, normed, scales = project(time_embed, tokens, first, k_rows, q_cols, t_cols)
+    qkv = lax.all_to_all(qkv, GROUP, 0, 0, tiled=True)
+    mixed_own, lse = attend(listed, edges, qkv, segc, segr)
+    mixed = lax.all_to_all(mixed_own, GROUP, 0, 0, tiled=True)
+    hidden, normed_mlp = outward(mixed, tokens, second, scales, o_cols)
+    up_keep, up_send, down_keep, down_send, layer_out, grad_hidden, grad_attn, gscale_mlp = mlp(
+        me, normed_mlp, cotangent, hidden, scales, second, o_cols, f_cols
+    )
+    grad_mixed = grad_mixed_of(grad_attn, second, mixed.shape, o_cols)
+    grad_mixed = lax.all_to_all(grad_mixed, GROUP, 0, 0, tiled=True)
+    out_keep, out_send = grad_proj_of(me, grad_attn, mixed, chunks, halves, o_cols)
+    grad_down = scatter_sum(down_keep, down_send, "xy")
+    grad_up = scatter_sum(up_keep, up_send, "yx")
+    grad_mixed, out_keep, out_send = lax.optimization_barrier((grad_mixed, out_keep, out_send))
+    grad_out = scatter_sum(out_keep, out_send, "yx")
+    grad_qkv = attend_back(listed, edges, qkv, grad_mixed, mixed_own, lse, segc, segr)
+    grad_qkv = lax.all_to_all(grad_qkv, GROUP, 0, 0, tiled=True)
+    grad_tokens, gscale_attn = first_norm_back(
+        grad_qkv, tokens, grad_hidden.reshape(tokens.shape), first, scales, q_cols
+    )
+    grad_scales = jnp.concatenate([gscale_attn, gscale_mlp], axis=1)
+    a_keep, a_send, b_keep, b_send, t_keep, t_send = grad_qkv_of(
+        me, normed, grad_qkv, time_embed, grad_scales, chunks, halves, k_rows, t_cols
+    )
+    grad_time = scatter_sum(t_keep, t_send, "yx").reshape(folds, k_rows, t_cols)
+    grad_time = grad_time.transpose(1, 0, 2).reshape(k_rows, t_all)
+    other = across(grad_time.astype(jnp.bfloat16), "tp", 1).astype(jnp.float32)
+    grad_time = jnp.concatenate(
+        [jnp.where(mine == 0, grad_time, other), jnp.where(mine == 0, other, grad_time)], axis=1
+    )
+    grad_w_qkv = jnp.concatenate(
+        [scatter_sum(a_keep, a_send, "yx"), scatter_sum(b_keep, b_send, "xy")], axis=1
+    )
+    return (
+        layer_out.reshape(tokens.shape),
+        grad_tokens,
+        grad_time,
+        grad_w_qkv,
+        grad_out,
+        grad_up,
+        grad_down,
+    )
+
+
+def choose(*args):
+    tokens, w_qkv, w_out, w_up = args[0], args[6], args[7], args[8]
+    group = lax.axis_size("ctx") * lax.axis_size("tp")
+    heads_pair = 6 * HEAD_DIM
+    fits = (
+        (lax.axis_size("fsdp"), lax.axis_size("ctx"), lax.axis_size("tp")) == (4, 4, 2)
+        and tokens.shape[1] == BLK
+        and group * BLK == args[2].shape[1]
+        and w_qkv.shape[1] * lax.axis_size("tp") == group * heads_pair
+        and w_out.shape[1] % 512 == 0
+        and w_up.shape[1] % 512 == 0
+        and w_qkv.shape[0] % args[5].shape[0] == 0
+    )
+    return spread_body(*args) if fits else body(*args)
+
+
 def solution(mesh):
     placed = (
         P("fsdp", ("ctx", "tp"), None),
@@ -337,7 +1238,7 @@
         P("fsdp", ("ctx", "tp"), None),
     )
     return jax.shard_map(
-        body,
+        choose,
         mesh=mesh,
         in_specs=placed,
         out_specs=(

time: 2220 us -> 830 us (0.37)
  waiting for transfers between devices: 1580 us -> 399 us
  matrix products: 334 us -> 0 us
  Pallas kernels: 0 us -> 310 us
  local copies, waits for them, and re-layouts: 105 us -> 9.26 us
  other arithmetic: 105 us -> 36.7 us
  starting transfers between devices: 1.72 us -> 47.2 us
  loops' own time: 39.8 us -> 0 us
    reduce_scatter x9 -> x0, waiting for transfers between devices: 1010 us -> none  [the longest x1 383 us: body(): lax.psum_scatter(jnp.stack(key_grads).astype(jnp.bfloat16), 'ctx', scatte...]
    all_gather x11 -> x2, waiting for transfers between devices: 478 us -> 75.9 us  [the longest x1 75.9 us: spread_body(): lax.all_gather(first, EVERY, axis=0, tiled=True)]
    dot_general x56 -> x0, matrix products: 334 us -> none  [the longest x12 49.7 us: block_scores(): jnp.einsum('qhe,khe->hqk', query_block, key_block, preferred_element_type...]
    pallas_call x0 -> x9, Pallas kernels: none -> 310 us  [the longest x1 95.3 us: attend_back(): pl.pallas_call(attend_back_kernel, grid_spec=pltpu.PrefetchScalarGridSpec...]
    ppermute x0 -> x34, waiting for transfers between devices: none -> 280 us  [across(): return lax.ppermute(values, axis, [(i, i ^ apart) for i in range(size)])]
    unnamed x24 -> x2, waiting for transfers between devices: 95.5 us -> 0.03 us
    another operation x11 -> x5, other arithmetic: 47.5 us -> 2.74 us  [the longest x3 18.5 us: body(): jnp.stack(key_grads).astype(jnp.bfloat16)]
    all_to_all x0 -> x4, waiting for transfers between devices: none -> 43.5 us  [the longest x1 25.1 us: spread_body(): mixed = lax.all_to_all(mixed_own, GROUP, 0, 0, tiled=True)]
  transfers between devices with their start and end apart: 22 -> 40, of which waited for: 20 -> 19; matrix products, arithmetic and copies ran while one was open for 12% -> 5% of each run, Pallas kernels for 0% -> 27%
where the time goes in v1:
time: 830 us; the launch traced here: 818 us
  waiting for transfers between devices  399 us (48%)
  Pallas kernels  310 us (37%)
  starting transfers between devices  47.2 us (6%)
  other arithmetic  36.7 us (4%)
  between operations  15 us (2%)
  local copies, waits for them, and re-layouts  9.26 us (1%)
    ppermute x34, waiting for transfers between devices, across(): return lax.ppermute(values, axis, [(i, i ^ apart) for i in range(size)])  280 us
    pallas_call x1, Pallas kernels, attend_back(): pl.pallas_call(attend_back_kernel, grid_spec=pltpu.PrefetchScalarGridSpec...  95.3 us
    pallas_call x1, Pallas kernels, mlp(): pl.pallas_call(mlp_kernel, grid_spec=pltpu.PrefetchScalarGridSpec(num_sca...  76.6 us
    all_gather x1, waiting for transfers between devices, spread_body(): lax.all_gather(first, EVERY, axis=0, tiled=True)  75.9 us
    pallas_call x1, Pallas kernels, attend(): pl.pallas_call(attend_kernel, grid_spec=pltpu.PrefetchScalarGridSpec(num_...  72.2 us
    ppermute x34, starting transfers between devices, across(): return lax.ppermute(values, axis, [(i, i ^ apart) for i in range(size)])  29.9 us
    all_to_all x1, waiting for transfers between devices, spread_body(): mixed = lax.all_to_all(mixed_own, GROUP, 0, 0, tiled=True)  25.1 us
    all_to_all x1, waiting for transfers between devices, spread_body(): grad_mixed = lax.all_to_all(grad_mixed, GROUP, 0, 0, tiled=True)  18.4 us
  transfers between devices with their start and end apart: 40, of which 19 were waited for; matrix products, arithmetic and copies ran while one was open for 5% of the time, Pallas kernels for 27%

profile of v1, /device:TPU:0, one launch (start us, length us, event | category | flops | bytes accessed | tf_op | source)
XLA Modules:
  0.0 818.0 jit_solution(8643212307787649269)
XLA Ops:
  8.1 1.0 convert.66
  9.9 1.1 convert.69
  11.9 75.9 %all-gather.3.cloned.1.call-done = bf16[2048,1792]{1,0:T(8,128)(2,1)} async-done(((bf16[64,1792]{1,0:T(8,128)(2,1)}), bf16[2048,1792]{1,0:T(8,128)(2,1)}) %all-gather.3.cloned.1.call-update) | async-done | bytes 7340048 | tf_op jit(solution)/shard_map/all_gather | solution.py:1157
  87.8 13.9 %project.1 = (bf16[8,2,512,384]{3,2,1,0:T(8,128)(2,1)}, bf16[2,512,1024]{2,1,0:T(8,128)(2,1)}, f32[2,2048]{1,0:T(2,128)}) custom-call(f32[2,256]{1,0:T(2,128)} %te_ref.1, bf16[2,512,1024]{2,1,0:T(8,128)(2,1)} %tok_ref.5, bf16[16,2,64,1792]{3,2,1,0:T(8,128)(2,1)} %bitcast.348), custom_call_target="tpu_custom_call" | custom-call | flops 6442450944 | bytes 17825792 | tf_op jit(solution)/shard_map/project/pallas_call | solution.py:432
  101.8 4.9 all-to-all-start
  107.4 1.7 collective-permute-start.1
  110.9 2.7 copy.44.segc_ref
  113.6 100.6 %collective-permute-done.1 = s32[2,1,31]{2,0,1:T(2,128)S(1)} collective-permute-done((s32[2,1,31]{2,0,1:T(2,128)S(1)}, s32[2,1,31]{2,0,1:T(2,128)S(1)}, u32[]{:S(2)}, u32[]{:S(2)}) %collective-permute-start.1) | collective-permute-done | bytes 280 | tf_op jit(solution)/shard_map/ppermute | solution.py:1092
  215.8 72.2 %attend.1 = (bf16[8,2,512,128]{3,2,1,0:T(8,128)(2,1)}, f32[2,2,4096]{2,1,0:T(2,128)}) custom-call(s32[2,64]{1,0:T(2,128)} %convert_element_type.665.listed_ref, s32[2,16]{1,0:T(2,128)} %pad_add_fusion.2.edge_ref, bf16[8,2,512,384]{3,2,1,0:T(8,128)(2,1)} %all-to-all-done.qkv_ref, s32[2,4096,1]{2,1,0:T(8,128)} %copy.44.segc_ref, ...), custom_call_target="tpu_custom_call" | custom-call | flops 30000001024 | bytes 12000000 | tf_op jit(solution)/shard_map/attend/pallas_call | solution.py:549
  288.0 3.8 all-to-all-start.1
  292.4 25.1 %all-to-all-done.1.mixed_ref = bf16[8,2,512,128]{3,2,1,0:T(8,128)(2,1)S(1)} async-done(((bf16[8,2,512,128]{3,2,1,0:T(8,128)(2,1)}), bf16[8,2,512,128]{3,2,1,0:T(8,128)(2,1)S(1)}, u32[]{:S(2)}, u32[]{:S(2)}) %all-to-all-start.1) | async-done | bytes 2097184 | tf_op jit(solution)/shard_map/all_to_all | solution.py:1169
  317.5 1.3 copy-done.2
  318.8 7.8 outward.1
  326.6 76.6 %mlp.1 = (bf16[2,2,4,64,2048]{4,3,2,1,0:T(8,128)(2,1)}, bf16[2,2,4,64,2048]{4,3,2,1,0:T(8,128)(2,1)}, bf16[2,2,4,64,2048]{4,3,2,1,0:T(8,128)(2,1)}, bf16[2,2,4,6...) custom-call(s32[2]{0:T(128)} %pad_add_fusion.3.me_ref, ...), custom_call_target="tpu_custom_call" | custom-call | flops 51539607552 | bytes 54525952 | tf_op jit(solution)/shard_map/mlp/pallas_call | solution.py:823
  403.2 6.3 grad_mixed.1
  409.5 3.6 all-to-all-start.2
  413.6 6.7 grad_proj.1
  420.3 18.4 %all-to-all-done.2.grad_ref = bf16[8,2,512,128]{3,2,1,0:T(8,128)(2,1)S(1)} async-done(((bf16[8,2,512,128]{3,2,1,0:T(8,128)(2,1)}), bf16[8,2,512,128]{3,2,1,0:T(8,128)(2,1)S(1)}, u32[]{:S(2)}, u32[]{:S(2)}) %all-to-all-start.2) | async-done | bytes 2097184 | tf_op jit(solution)/shard_map/all_to_all | solution.py:1175
  438.8 1.3 copy-done.4
  440.1 95.3 %attend_back.1 = bf16[8,2,512,384]{3,2,1,0:T(8,128)(2,1)} custom-call(s32[2,64]{1,0:T(2,128)} %convert_element_type.665.listed_ref, s32[2,16]{1,0:T(2,128)} %pad_add_fusion.2.edge_ref, bf16[8,2,512,384]{3,2,1,0:T(8,128)(2,1)} %all-to-all-done.qkv_ref, bf16[8,2,512,128]{3,2,1,0:T(8,128)(2,1)} %copy-done.4, ...), custom_call_target="tpu_custom_call" | custom-call | flops 70000001024 | bytes 20000000 | tf_op jit(solution)/shard_map/attend_back/pallas_call | solution.py:660
  535.4 4.9 all-to-all-start.3
  540.7 3.3 collective-permute-done.19
  544.1 1.7 collective-permute-start.20
  545.9 3.2 fusion.1
  549.0 1.6 collective-permute-start.30
  550.6 3.7 fusion
  554.9 67.7 %collective-permute-done.20 = bf16[2,4,64,512]{3,2,1,0:T(8,128)(2,1)S(1)} collective-permute-done((bf16[2,4,64,512]{3,2,1,0:T(8,128)(2,1)S(1)}, bf16[2,4,64,512]{3,2,1,0:T(8,128)(2,1)S(1)}, u32[]{:S(2)}, u32[]{:S(2)}) %collective-permute-start.20) | collective-permute-done | bytes 524320 | tf_op jit(solution)/shard_map/ppermute | solution.py:1092
  622.6 1.1 collective-permute-start.21
  623.8 37.8 %collective-permute-done.21 = bf16[4,64,512]{2,1,0:T(8,128)(2,1)S(1)} collective-permute-done((bf16[4,64,512]{2,1,0:T(8,128)(2,1)S(1)}, bf16[4,64,512]{2,1,0:T(8,128)(2,1)S(1)}, u32[]{:S(2)}, u32[]{:S(2)}) %collective-permute-start.21) | collective-permute-done | bytes 262176 | tf_op jit(solution)/shard_map/ppermute | solution.py:1092
  662.5 4.4 collective-permute-done.22
  666.9 0.9 fusion.30
  667.9 3.4 fusion.2
  671.4 1.5 collective-permute-start.31
  672.9 3.4 fusion.3
  676.8 14.1 %first_norm_back.1 = (bf16[2,512,1024]{2,1,0:T(8,128)(2,1)}, f32[2,1024]{1,0:T(2,128)}) custom-call(bf16[8,2,512,384]{3,2,1,0:T(8,128)(2,1)} %all-to-all-done.3.gq_ref, bf16[2,512,1024]{2,1,0:T(8,128)(2,1)} %tok_ref.5, f32[2,512,1024]{2,1,0:T(8,128)} %bitcast.354, bf16[16,2,64,1792]{3,2,1,0:T(8,128)(2,1)} %bitcast.349, f32[2,2048]{1,0:T(2,128)} %get-tuple-element.37.scales_ref), custom_call_target="tpu_custom_call" | custom-call | flops 6442450944 | bytes 28311552 | tf_op jit(solution)/shard_map/first_norm_back/pallas_call | solution.py:966
  690.9 1.3 pad_maximum_fusion.4.gs_ref
  692.2 17.6 %grad_qkv.1 = (bf16[2,2,4,64,768]{4,3,2,1,0:T(8,128)(2,1)}, bf16[2,2,4,64,768]{4,3,2,1,0:T(8,128)(2,1)}, bf16[2,2,4,64,768]{4,3,2,1,0:T(8,128)(2,1)}, bf16[2,2,4...) custom-call(s32[2]{0:T(128)} %pad_add_fusion.3.me_ref, ...), custom_call_target="tpu_custom_call" | custom-call | flops 6442450944 | bytes 6291456 | tf_op jit(solution)/shard_map/grad_qkv/pallas_call | solution.py:1061
  710.0 1.7 fusion.31
  711.6 1.7 fusion.5
  714.5 1.7 fusion.7
  716.2 1.8 collective-permute-start.27
  718.5 3.8 collective-permute-done.4
  722.3 1.6 collective-permute-start.5
  723.9 4.3 collective-permute-done.32
  728.1 1.3 fusion.13
  729.4 3.0 collective-permute-start.33
  732.8 12.2 %collective-permute-done.27 = bf16[2,64,2048]{2,1,0:T(8,128)(2,1)S(1)} collective-permute-done((bf16[2,64,2048]{2,1,0:T(8,128)(2,1)S(1)}, bf16[2,64,2048]{2,1,0:T(8,128)(2,1)S(1)}, u32[]{:S(2)}, u32[]{:S(2)}) %collective-permute-start.27) | collective-permute-done | bytes 524320 | tf_op jit(solution)/shard_map/ppermute | solution.py:1092
  745.0 1.3 fusion.15
  747.1 2.3 collective-permute-start.7
  749.4 2.1 fusion.14
  751.5 10.2 %collective-permute-done.7 = bf16[64,256]{1,0:T(8,128)(2,1)S(1)} collective-permute-done((bf16[64,256]{1,0:T(8,128)(2,1)S(1)}, bf16[64,256]{1,0:T(8,128)(2,1)S(1)}, u32[]{:S(2)}, u32[]{:S(2)}) %collective-permute-start.7) | collective-permute-done | bytes 32800 | tf_op jit(solution)/shard_map/ppermute | solution.py:1092
  762.6 1.5 collective-permute-start.10
  764.3 1.6 collective-permute-start.15
  765.9 2.1 fusion.16
  768.0 14.2 %collective-permute-done.10 = bf16[2,4,64,768]{3,2,1,0:T(8,128)(2,1)S(1)} collective-permute-done((bf16[2,4,64,768]{3,2,1,0:T(8,128)(2,1)S(1)}, bf16[2,4,64,768]{3,2,1,0:T(8,128)(2,1)S(1)}, u32[]{:S(2)}, u32[]{:S(2)}) %collective-permute-start.10) | collective-permute-done | bytes 786464 | tf_op jit(solution)/shard_map/ppermute | solution.py:1092
  782.4 1.5 collective-permute-start.11
  784.0 1.2 collective-permute-start.16
  785.9 6.8 collective-permute-done.11
  792.8 1.2 collective-permute-done.16
  795.0 6.0 collective-permute-done.12
  801.2 2.0 collective-permute-done.17
  803.2 1.0 collective-permute-start.18
  804.2 3.1 collective-permute-done.13
  807.4 2.5 collective-permute-done.18
  (143 shorter events, 17.9 us)
Async XLA Ops:
  7.2 0.9 copy-start
  7.2 3.8 copy-start.9
  7.2 3.8 copy-start.13
  7.2 80.6 %all-gather.3.cloned.1.call-start = ((), (), s32[]{:S(2)}) async-start(), calls=%async_computation.4 | async-start | bytes 7569408 | tf_op jit(solution)/shard_map/all_gather | solution.py:1157
  9.8 307.7 %all-gather.5.cloned.1.call-start = ((), (), s32[]{:S(2)}) async-start(), calls=%async_computation.5 | async-start | bytes 19464192 | tf_op jit(solution)/shard_map/all_gather | solution.py:1158
  101.7 4.9 copy-start.16
  101.7 5.1 copy-start.20
  101.7 7.4 copy-start.12
  101.8 114.1 %all-to-all-start = ((bf16[8,2,512,384]{3,2,1,0:T(8,128)(2,1)}), bf16[8,2,512,384]{3,2,1,0:T(8,128)(2,1)}, u32[]{:S(2)}, u32[]{:S(2)}) async-start(bf16[8,2,512,384]{3,2,1,0:T(8,128)(2,1)} %get-tuple-element.35), calls=%async_computation | async-start | bytes 12582912 | tf_op jit(solution)/shard_map/all_to_all | solution.py:1167
  107.0 6.6 collective-permute-start
  107.4 106.8 %collective-permute-start.1 = (s32[2,1,31]{2,0,1:T(2,128)S(1)}, s32[2,1,31]{2,0,1:T(2,128)S(1)}, u32[]{:S(2)}, u32[]{:S(2)}) collective-permute-start(s32[2,1,31]{2,0,1:T(2,128)S(1)} %pad_add_fusion.1), channel_id=1, source_target_pairs={{0,4},{2,6},{4,0},{6,2},{1,5},{3,7},{5,1},{7,3},{8,12},{10,14},{12... | collective-permute-start | bytes 752 | tf_op jit(solution)/shard_map/ppermute | solution.py:1092
  109.1 105.1 %collective-permute-start.2 = (s32[2,1,31]{2,0,1:T(2,128)S(1)}, s32[2,1,31]{2,0,1:T(2,128)S(1)}, u32[]{:S(2)}, u32[]{:S(2)}) collective-permute-start(s32[2,1,31]{2,0,1:T(2,128)S(1)} %pad_add_fusion.1), channel_id=1, source_target_pairs={{0,6},{2,4},{4,2},{6,0},{1,7},{3,5},{5,3},{7,1},{8,14},{10,12},{12... | collective-permute-start | bytes 752 | tf_op jit(solution)/shard_map/ppermute | solution.py:1092
  288.0 29.5 %all-to-all-start.1 = ((bf16[8,2,512,128]{3,2,1,0:T(8,128)(2,1)}), bf16[8,2,512,128]{3,2,1,0:T(8,128)(2,1)S(1)}, u32[]{:S(2)}, u32[]{:S(2)}) async-start(bf16[8,2,512,128]{3,2,1,0:T(8,128)(2,1)} %get-tuple-element.36.mixed_ref), calls=%async_computation.1 | async-start | bytes 4194304 | tf_op jit(solution)/shard_map/all_to_all | solution.py:1169
  317.5 1.3 copy-start.2
  409.5 29.3 %all-to-all-start.2 = ((bf16[8,2,512,128]{3,2,1,0:T(8,128)(2,1)}), bf16[8,2,512,128]{3,2,1,0:T(8,128)(2,1)S(1)}, u32[]{:S(2)}, u32[]{:S(2)}) async-start(bf16[8,2,512,128]{3,2,1,0:T(8,128)(2,1)} %grad_mixed.1), calls=%async_computation.2 | async-start | bytes 4194304 | tf_op jit(solution)/shard_map/all_to_all | solution.py:1175
  413.1 132.8 %collective-permute-start.29 = (bf16[2,2,4,64,2048]{4,3,2,1,0:T(8,128)(2,1)}, bf16[2,2,4,64,2048]{4,3,2,1,0:T(8,128)(2,1)}, u32[]{:S(2)}, u32[]{:S(2)}) collective-permute-start(bf16[2,2,4,64,2048]{4,3,2,1,0:T(8,128)(2,1)} %get-tuple-element.62), channel_id=1, source_target_pairs={{0,2},{2,0},{4,6},{6,4},{1,3},{3,1},{5,7},{7,5},{8,10},{10,8},{12,... | collective-permute-start | bytes 12582920 | tf_op jit(solution)/shard_map/ppermute | solution.py:1092
  413.5 137.1 %collective-permute-start.24 = (bf16[2,2,4,64,2048]{4,3,2,1,0:T(8,128)(2,1)}, bf16[2,2,4,64,2048]{4,3,2,1,0:T(8,128)(2,1)}, u32[]{:S(2)}, u32[]{:S(2)}) collective-permute-start(bf16[2,2,4,64,2048]{4,3,2,1,0:T(8,128)(2,1)} %get-tuple-element.60), channel_id=1, source_target_pairs={{0,2},{2,0},{4,6},{6,4},{1,3},{3,1},{5,7},{7,5},{8,10},{10,8},{12,... | collective-permute-start | bytes 12582920 | tf_op jit(solution)/shard_map/ppermute | solution.py:1092
  438.8 1.3 copy-start.4
  535.4 4.9 copy-start.19
  535.4 8.6 %copy-start.7 = (bf16[2,2,4,64,512]{4,3,2,1,0:T(8,128)(2,1)S(1)}, bf16[2,2,4,64,512]{4,3,2,1,0:T(8,128)(2,1)}, u32[]{:S(2)}) copy-start(bf16[2,2,4,64,512]{4,3,2,1,0:T(8,128)(2,1)} %get-tuple-element.57) | copy-start | bytes 3145732
  535.4 141.4 %all-to-all-start.3 = ((bf16[8,2,512,384]{3,2,1,0:T(8,128)(2,1)}), bf16[8,2,512,384]{3,2,1,0:T(8,128)(2,1)}, u32[]{:S(2)}, u32[]{:S(2)}) async-start(bf16[8,2,512,384]{3,2,1,0:T(8,128)(2,1)} %attend_back.1), calls=%async_computation.3 | async-start | bytes 12582912 | tf_op jit(solution)/shard_map/all_to_all | solution.py:1182
  540.3 3.6 collective-permute-start.19
  544.0 117.5 %copy-start.8 = (bf16[2,2,4,64,512]{4,3,2,1,0:T(8,128)(2,1)}, bf16[2,2,4,64,512]{4,3,2,1,0:T(8,128)(2,1)S(1)}, u32[]{:S(2)}) copy-start(bf16[2,2,4,64,512]{4,3,2,1,0:T(8,128)(2,1)S(1)} %collective-permute-done.19) | copy-start | bytes 3145732
  544.1 78.4 %collective-permute-start.20 = (bf16[2,4,64,512]{3,2,1,0:T(8,128)(2,1)S(1)}, bf16[2,4,64,512]{3,2,1,0:T(8,128)(2,1)S(1)}, u32[]{:S(2)}, u32[]{:S(2)}) collective-permute-start(bf16[2,4,64,512]{3,2,1,0:T(8,128)(2,1)S(1)} %fusion.12), channel_id=1, source_target_pairs={{0,1},{1,0},{2,3},{3,2},{4,5},{5,4},{6,7},{7,6},{8,9},{9,8},{10,11... | collective-permute-start | bytes 1572872 | tf_op jit(solution)/shard_map/ppermute | solution.py:1092
  545.9 4.7 copy-start.3
  549.0 118.9 %collective-permute-start.30 = (bf16[2,4,64,2048]{3,2,1,0:T(8,128)(2,1)S(1)}, bf16[2,4,64,2048]{3,2,1,0:T(8,128)(2,1)}, u32[]{:S(2)}, u32[]{:S(2)}) collective-permute-start(bf16[2,4,64,2048]{3,2,1,0:T(8,128)(2,1)S(1)} %fusion.1), channel_id=1, source_target_pairs={{0,4},{2,6},{4,0},{6,2},{1,5},{3,7},{5,1},{7,3},{8,12},{10,14},{12... | collective-permute-start | bytes 6291464 | tf_op jit(solution)/shard_map/ppermute | solution.py:1092
  550.6 111.1 %copy-start.15 = (f32[2,256]{1,0:T(2,128)S(1)}, f32[2,256]{1,0:T(2,128)}, u32[]{:S(2)}) copy-start(f32[2,256]{1,0:T(2,128)} %te_ref.1) | copy-start | bytes 6148
  554.3 118.5 %collective-permute-start.25 = (bf16[2,4,64,2048]{3,2,1,0:T(8,128)(2,1)}, bf16[2,4,64,2048]{3,2,1,0:T(8,128)(2,1)}, u32[]{:S(2)}, u32[]{:S(2)}) collective-permute-start(bf16[2,4,64,2048]{3,2,1,0:T(8,128)(2,1)} %fusion), channel_id=1, source_target_pairs={{0,1},{1,0},{2,3},{3,2},{4,5},{5,4},{6,7},{7,6},{8,9},{9,8},{10,11... | collective-permute-start | bytes 6291464 | tf_op jit(solution)/shard_map/ppermute | solution.py:1092
  622.5 39.0 %copy-start.11 = (bf16[2,4,64,512]{3,2,1,0:T(8,128)(2,1)}, bf16[2,4,64,512]{3,2,1,0:T(8,128)(2,1)S(1)}, u32[]{:S(2)}) copy-start(bf16[2,4,64,512]{3,2,1,0:T(8,128)(2,1)S(1)} %collective-permute-done.20) | copy-start | bytes 1572868
  622.6 38.9 %collective-permute-start.21 = (bf16[4,64,512]{2,1,0:T(8,128)(2,1)S(1)}, bf16[4,64,512]{2,1,0:T(8,128)(2,1)S(1)}, u32[]{:S(2)}, u32[]{:S(2)}) collective-permute-start(bf16[4,64,512]{2,1,0:T(8,128)(2,1)S(1)} %fusion.17), channel_id=1, source_target_pairs={{0,4},{2,6},{4,0},{6,2},{1,5},{3,7},{5,1},{7,3},{8,12},{10,14},{12... | collective-permute-start | bytes 786440 | tf_op jit(solution)/shard_map/ppermute | solution.py:1092
  661.6 5.3 collective-permute-start.22
  667.9 42.1 %collective-permute-start.23 = (bf16[64,512]{1,0:T(8,128)(2,1)S(1)}, bf16[64,512]{1,0:T(8,128)(2,1)S(1)}, u32[]{:S(2)}, u32[]{:S(2)}) collective-permute-start(bf16[64,512]{1,0:T(8,128)(2,1)S(1)} %fusion.30), channel_id=1, source_target_pairs={{0,16},{8,24},{16,0},{24,8},{1,17},{9,25},{17,1},{25,9},{2,18},{10... | collective-permute-start | bytes 196616 | tf_op jit(solution)/shard_map/ppermute | solution.py:1092
  671.4 40.3 %collective-permute-start.31 = (bf16[4,64,2048]{2,1,0:T(8,128)(2,1)}, bf16[4,64,2048]{2,1,0:T(8,128)(2,1)S(1)}, u32[]{:S(2)}, u32[]{:S(2)}) collective-permute-start(bf16[4,64,2048]{2,1,0:T(8,128)(2,1)} %fusion.2), channel_id=1, source_target_pairs={{0,1},{1,0},{2,3},{3,2},{4,5},{5,4},{6,7},{7,6},{8,9},{9,8},{10,11... | collective-permute-start | bytes 3145736 | tf_op jit(solution)/shard_map/ppermute | solution.py:1092
  676.3 38.2 %collective-permute-start.26 = (bf16[4,64,2048]{2,1,0:T(8,128)(2,1)}, bf16[4,64,2048]{2,1,0:T(8,128)(2,1)S(1)}, u32[]{:S(2)}, u32[]{:S(2)}) collective-permute-start(bf16[4,64,2048]{2,1,0:T(8,128)(2,1)} %fusion.3), channel_id=1, source_target_pairs={{0,4},{2,6},{4,0},{6,2},{1,5},{3,7},{5,1},{7,3},{8,12},{10,14},{12... | collective-permute-start | bytes 3145736 | tf_op jit(solution)/shard_map/ppermute | solution.py:1092
  676.8 14.1 %copy-start.14 = (f32[2,1024]{1,0:T(2,128)S(1)}, f32[2,1024]{1,0:T(2,128)}, u32[]{:S(2)}) copy-start(f32[2,1024]{1,0:T(2,128)} %get-tuple-element.50) | copy-start | bytes 24580
  709.9 3.8 copy-start.10
  709.9 3.8 collective-permute-start.3
  713.3 4.6 copy-start.18
  713.3 4.6 copy-start.17
  713.4 14.8 %collective-permute-start.32 = (bf16[2,64,2048]{2,1,0:T(8,128)(2,1)S(1)}, bf16[2,64,2048]{2,1,0:T(8,128)(2,1)S(1)}, u32[]{:S(2)}, u32[]{:S(2)}) collective-permute-start(bf16[2,64,2048]{2,1,0:T(8,128)(2,1)S(1)} %fusion.5), channel_id=1, source_target_pairs={{0,8},{8,0},{16,24},{24,16},{1,9},{9,1},{17,25},{25,17},{2,10},{10... | collective-permute-start | bytes 1572872 | tf_op jit(solution)/shard_map/ppermute | solution.py:1092
  713.8 8.5 %collective-permute-start.4 = (bf16[2,4,64,256]{3,2,1,0:T(8,128)(2,1)S(1)}, bf16[2,4,64,256]{3,2,1,0:T(8,128)(2,1)S(1)}, u32[]{:S(2)}, u32[]{:S(2)}) collective-permute-start(bf16[2,4,64,256]{3,2,1,0:T(8,128)(2,1)S(1)} %fusion.22), channel_id=1, source_target_pairs={{0,1},{1,0},{2,3},{3,2},{4,5},{5,4},{6,7},{7,6},{8,9},{9,8},{10,11... | collective-permute-start | bytes 786440 | tf_op jit(solution)/shard_map/ppermute | solution.py:1092
  716.2 28.8 %collective-permute-start.27 = (bf16[2,64,2048]{2,1,0:T(8,128)(2,1)S(1)}, bf16[2,64,2048]{2,1,0:T(8,128)(2,1)S(1)}, u32[]{:S(2)}, u32[]{:S(2)}) collective-permute-start(bf16[2,64,2048]{2,1,0:T(8,128)(2,1)S(1)} %fusion.7), channel_id=1, source_target_pairs={{0,8},{8,0},{16,24},{24,16},{1,9},{9,1},{17,25},{25,17},{2,10},{10... | collective-permute-start | bytes 1572872 | tf_op jit(solution)/shard_map/ppermute | solution.py:1092
  718.0 44.5 %collective-permute-start.9 = (bf16[2,2,4,64,768]{4,3,2,1,0:T(8,128)(2,1)S(1)}, bf16[2,2,4,64,768]{4,3,2,1,0:T(8,128)(2,1)S(1)}, u32[]{:S(2)}, u32[]{:S(2)}) collective-permute-start(bf16[2,2,4,64,768]{4,3,2,1,0:T(8,128)(2,1)S(1)} %copy-done.18), channel_id=1, source_target_pairs={{0,2},{2,0},{4,6},{6,4},{1,3},{3,1},{5,7},{7,5},{8,10},{10,8},{12,... | collective-permute-start | bytes 4718600 | tf_op jit(solution)/shard_map/ppermute | solution.py:1092
  718.0 46.1 %collective-permute-start.14 = (bf16[2,2,4,64,768]{4,3,2,1,0:T(8,128)(2,1)S(1)}, bf16[2,2,4,64,768]{4,3,2,1,0:T(8,128)(2,1)S(1)}, u32[]{:S(2)}, u32[]{:S(2)}) collective-permute-start(bf16[2,2,4,64,768]{4,3,2,1,0:T(8,128)(2,1)S(1)} %copy-done.17), channel_id=1, source_target_pairs={{0,2},{2,0},{4,6},{6,4},{1,3},{3,1},{5,7},{7,5},{8,10},{10,8},{12,... | collective-permute-start | bytes 4718600 | tf_op jit(solution)/shard_map/ppermute | solution.py:1092
  722.3 10.1 %collective-permute-start.5 = (bf16[4,64,256]{2,1,0:T(8,128)(2,1)S(1)}, bf16[4,64,256]{2,1,0:T(8,128)(2,1)S(1)}, u32[]{:S(2)}, u32[]{:S(2)}) collective-permute-start(bf16[4,64,256]{2,1,0:T(8,128)(2,1)S(1)} %fusion.25), channel_id=1, source_target_pairs={{0,4},{2,6},{4,0},{6,2},{1,5},{3,7},{5,1},{7,3},{8,12},{10,14},{12... | collective-permute-start | bytes 393224 | tf_op jit(solution)/shard_map/ppermute | solution.py:1092
  729.4 20.0 %collective-permute-start.33 = (bf16[64,2048]{1,0:T(8,128)(2,1)S(1)}, bf16[64,2048]{1,0:T(8,128)(2,1)S(1)}, u32[]{:S(2)}, u32[]{:S(2)}) collective-permute-start(bf16[64,2048]{1,0:T(8,128)(2,1)S(1)} %fusion.13), channel_id=1, source_target_pairs={{0,16},{8,24},{16,0},{24,8},{1,17},{9,25},{17,1},{25,9},{2,18},{10... | collective-permute-start | bytes 786440 | tf_op jit(solution)/shard_map/ppermute | solution.py:1092
  732.5 30.0 %copy-start.6 = (bf16[2,2,4,64,768]{4,3,2,1,0:T(8,128)(2,1)S(1)}, bf16[2,2,4,64,768]{4,3,2,1,0:T(8,128)(2,1)}, u32[]{:S(2)}) copy-start(bf16[2,2,4,64,768]{4,3,2,1,0:T(8,128)(2,1)} %get-tuple-element.53) | copy-start | bytes 4718596
  732.5 14.6 %collective-permute-start.6 = (bf16[2,64,256]{2,1,0:T(8,128)(2,1)S(1)}, bf16[2,64,256]{2,1,0:T(8,128)(2,1)S(1)}, u32[]{:S(2)}, u32[]{:S(2)}) collective-permute-start(bf16[2,64,256]{2,1,0:T(8,128)(2,1)S(1)} %fusion.33), channel_id=1, source_target_pairs={{0,8},{8,0},{16,24},{24,16},{1,9},{9,1},{17,25},{25,17},{2,10},{10... | collective-permute-start | bytes 196616 | tf_op jit(solution)/shard_map/ppermute | solution.py:1092
  746.3 19.6 %collective-permute-start.28 = (bf16[64,2048]{1,0:T(8,128)(2,1)S(1)}, bf16[64,2048]{1,0:T(8,128)(2,1)S(1)}, u32[]{:S(2)}, u32[]{:S(2)}) collective-permute-start(bf16[64,2048]{1,0:T(8,128)(2,1)S(1)} %fusion.15), channel_id=1, source_target_pairs={{0,16},{8,24},{16,0},{24,8},{1,17},{9,25},{17,1},{25,9},{2,18},{10... | collective-permute-start | bytes 786440 | tf_op jit(solution)/shard_map/ppermute | solution.py:1092
  747.1 17.0 %copy-start.5 = (bf16[2,2,4,64,768]{4,3,2,1,0:T(8,128)(2,1)S(1)}, bf16[2,2,4,64,768]{4,3,2,1,0:T(8,128)(2,1)}, u32[]{:S(2)}) copy-start(bf16[2,2,4,64,768]{4,3,2,1,0:T(8,128)(2,1)} %get-tuple-element.55) | copy-start | bytes 4718596
  747.1 14.6 %collective-permute-start.7 = (bf16[64,256]{1,0:T(8,128)(2,1)S(1)}, bf16[64,256]{1,0:T(8,128)(2,1)S(1)}, u32[]{:S(2)}, u32[]{:S(2)}) collective-permute-start(bf16[64,256]{1,0:T(8,128)(2,1)S(1)} %fusion.34), channel_id=1, source_target_pairs={{0,16},{8,24},{16,0},{24,8},{1,17},{9,25},{17,1},{25,9},{2,18},{10... | collective-permute-start | bytes 98312 | tf_op jit(solution)/shard_map/ppermute | solution.py:1092
  761.7 6.2 collective-permute-start.8
  762.6 19.6 %collective-permute-start.10 = (bf16[2,4,64,768]{3,2,1,0:T(8,128)(2,1)S(1)}, bf16[2,4,64,768]{3,2,1,0:T(8,128)(2,1)S(1)}, u32[]{:S(2)}, u32[]{:S(2)}) collective-permute-start(bf16[2,4,64,768]{3,2,1,0:T(8,128)(2,1)S(1)} %fusion.8), channel_id=1, source_target_pairs={{0,1},{1,0},{2,3},{3,2},{4,5},{5,4},{6,7},{7,6},{8,9},{9,8},{10,11... | collective-permute-start | bytes 2359304 | tf_op jit(solution)/shard_map/ppermute | solution.py:1092
  764.3 19.6 %collective-permute-start.15 = (bf16[2,4,64,768]{3,2,1,0:T(8,128)(2,1)S(1)}, bf16[2,4,64,768]{3,2,1,0:T(8,128)(2,1)S(1)}, u32[]{:S(2)}, u32[]{:S(2)}) collective-permute-start(bf16[2,4,64,768]{3,2,1,0:T(8,128)(2,1)S(1)} %fusion.9), channel_id=1, source_target_pairs={{0,4},{2,6},{4,0},{6,2},{1,5},{3,7},{5,1},{7,3},{8,12},{10,14},{12... | collective-permute-start | bytes 2359304 | tf_op jit(solution)/shard_map/ppermute | solution.py:1092
  782.4 10.3 %collective-permute-start.11 = (bf16[4,64,768]{2,1,0:T(8,128)(2,1)S(1)}, bf16[4,64,768]{2,1,0:T(8,128)(2,1)S(1)}, u32[]{:S(2)}, u32[]{:S(2)}) collective-permute-start(bf16[4,64,768]{2,1,0:T(8,128)(2,1)S(1)} %fusion.11), channel_id=1, source_target_pairs={{0,4},{2,6},{4,0},{6,2},{1,5},{3,7},{5,1},{7,3},{8,12},{10,14},{12... | collective-permute-start | bytes 1179656 | tf_op jit(solution)/shard_map/ppermute | solution.py:1092
  784.0 10.0 %collective-permute-start.16 = (bf16[4,64,768]{2,1,0:T(8,128)(2,1)S(1)}, bf16[4,64,768]{2,1,0:T(8,128)(2,1)S(1)}, u32[]{:S(2)}, u32[]{:S(2)}) collective-permute-start(bf16[4,64,768]{2,1,0:T(8,128)(2,1)S(1)} %fusion.10), channel_id=1, source_target_pairs={{0,1},{1,0},{2,3},{3,2},{4,5},{5,4},{6,7},{7,6},{8,9},{9,8},{10,11... | collective-permute-start | bytes 1179656 | tf_op jit(solution)/shard_map/ppermute | solution.py:1092
  792.6 18.1 %copy-start.1 = (f32[16,2048]{1,0:T(8,128)S(1)}, f32[16,2048]{1,0:T(8,128)}, u32[]{:S(2)}) copy-start(f32[16,2048]{1,0:T(8,128)} %param.16) | copy-start | bytes 393220
  792.8 8.3 %collective-permute-start.12 = (bf16[2,64,768]{2,1,0:T(8,128)(2,1)S(1)}, bf16[2,64,768]{2,1,0:T(8,128)(2,1)S(1)}, u32[]{:S(2)}, u32[]{:S(2)}) collective-permute-start(bf16[2,64,768]{2,1,0:T(8,128)(2,1)S(1)} %fusion.21), channel_id=1, source_target_pairs={{0,8},{8,0},{16,24},{24,16},{1,9},{9,1},{17,25},{25,17},{2,10},{10... | collective-permute-start | bytes 589832 | tf_op jit(solution)/shard_map/ppermute | solution.py:1092
  794.1 9.0 %collective-permute-start.17 = (bf16[2,64,768]{2,1,0:T(8,128)(2,1)S(1)}, bf16[2,64,768]{2,1,0:T(8,128)(2,1)S(1)}, u32[]{:S(2)}, u32[]{:S(2)}) collective-permute-start(bf16[2,64,768]{2,1,0:T(8,128)(2,1)S(1)} %fusion.19), channel_id=1, source_target_pairs={{0,8},{8,0},{16,24},{24,16},{1,9},{9,1},{17,25},{25,17},{2,10},{10... | collective-permute-start | bytes 589832 | tf_op jit(solution)/shard_map/ppermute | solution.py:1092
  801.1 6.2 collective-permute-start.13
  803.2 6.6 collective-permute-start.18
Sparse Core Ops, SparseCore 0:
  11.5 76.2 all-gather.2
  91.3 159.6 all-gather.4

commit v2 on v1

--- a/solution.py
+++ b/solution.py
@@ -387,68 +387,70 @@
     )
 
 
-def project_kernel(te_ref, tok_ref, w_ref, qkv_ref, normed_ref, scales_ref, *, tiles, k_rows, q_cols, t_cols):
-    step = pl.program_id(0)
-    chunks, halves = w_ref.shape[0], w_ref.shape[1]
-
-    @pl.when(step == 0)
+def time_scales(te_ref, w_ref, scales_ref, k_rows, q_cols, t_cols):
+    exact = te_ref[...]
+    high = exact.astype(jnp.bfloat16)
+    rest = exact - high.astype(jnp.float32)
+    middle = rest.astype(jnp.bfloat16)
+    last = (rest - middle.astype(jnp.float32)).astype(jnp.bfloat16)
+    chunks, halves, tall, _ = w_ref.shape
+    folds = tall // k_rows
+    for half in range(halves):
+        for fold in range(folds):
+            weights = w_ref[:, half, fold * k_rows : (fold + 1) * k_rows, q_cols : q_cols + t_cols]
+            weights = weights.reshape(chunks * k_rows, t_cols)
+            total = dot_nn(last, weights) + dot_nn(middle, weights) + dot_nn(high, weights)
+            at = (half * folds + fold) * t_cols
+            scales_ref[:, at : at + t_cols] = 1.0 + total
+
+
+def project_kernel(te_ref, tok_ref, w_ref, qkv_ref, normed_ref, scales_ref, *, row, k_rows, q_cols, t_cols):
+    @pl.when(pl.program_id(0) == 0)
     def _():
-        exact = te_ref[...]
-        high = exact.astype(jnp.bfloat16)
-        rest = exact - high.astype(jnp.float32)
-        middle = rest.astype(jnp.bfloat16)
-        last = (rest - middle.astype(jnp.float32)).astype(jnp.bfloat16)
-        folds = w_ref.shape[2] // k_rows
-        for half in range(halves):
-            for fold in range(folds):
-                weights = w_ref[:, half, fold * k_rows : (fold + 1) * k_rows, q_cols : q_cols + t_cols]
-                weights = weights.reshape(chunks * k_rows, t_cols)
-                total = dot_nn(last, weights) + dot_nn(middle, weights) + dot_nn(high, weights)
-                at = (half * folds + fold) * t_cols
-                scales_ref[:, at : at + t_cols] = 1.0 + total
-
-    row = step // tiles
+        time_scales(te_ref, w_ref, scales_ref, k_rows, q_cols, t_cols)
+
+    halves = w_ref.shape[1]
     values = tok_ref[0].astype(jnp.float32)
     width = values.shape[1]
     hat, _ = normalize(values)
-    normed = (hat * scales_ref[pl.ds(row, 1), :width]).astype(jnp.bfloat16)
-    normed_ref[0] = normed
+    normed = (hat * scales_ref[row : row + 1, :width]).astype(jnp.bfloat16)
+    normed_ref[...] = normed
     pair = 6 * HEAD_DIM
     for half in range(halves):
         weights = w_ref[:, half, :, :q_cols].reshape(width, q_cols)
         out = dot_nn(normed, weights)
         for group in range(q_cols // pair):
-            qkv_ref[half * (q_cols // pair) + group, 0] = pair_apart(
+            qkv_ref[half * (q_cols // pair) + group] = pair_apart(
                 out[:, group * pair : (group + 1) * pair]
             ).astype(jnp.bfloat16)
 
 
-def project(time_embed, tokens, w_all, k_rows, q_cols, t_cols):
+def project(row, time_embed, tokens, w_all, k_rows, q_cols, t_cols):
     rows, length, width = tokens.shape
     chunks, halves = w_all.shape[:2]
-    groups = halves * q_cols // (6 * HEAD_DIM)
+    pair = 6 * HEAD_DIM
+    groups = halves * q_cols // pair
     tile = 256
-    tiles = length // tile
     return pl.pallas_call(
-        functools.partial(project_kernel, tiles=tiles, k_rows=k_rows, q_cols=q_cols, t_cols=t_cols),
-        grid=(rows * tiles,),
+        functools.partial(project_kernel, row=row, k_rows=k_rows, q_cols=q_cols, t_cols=t_cols),
+        grid=(length // tile,),
         in_specs=[
             whole(time_embed.shape),
-            pl.BlockSpec((1, tile, width), lambda i: (i // tiles, i % tiles, 0)),
+            pl.BlockSpec((1, tile, width), lambda i: (row, i, 0)),
             whole(w_all.shape),
         ],
         out_specs=[
-            pl.BlockSpec((groups, 1, tile, 6 * HEAD_DIM), lambda i: (0, i // tiles, i % tiles, 0)),
-            pl.BlockSpec((1, tile, width), lambda i: (i // tiles, i % tiles, 0)),
+            pl.BlockSpec((groups, tile, pair), lambda i: (0, i, 0)),
+            pl.BlockSpec((tile, width), lambda i: (i, 0)),
             whole((rows, 2 * width)),
         ],
         out_shape=[
-            jax.ShapeDtypeStruct((groups, rows, length, 6 * HEAD_DIM), jnp.bfloat16),
-            jax.ShapeDtypeStruct(tokens.shape, jnp.bfloat16),
+            jax.ShapeDtypeStruct((groups, length, pair), jnp.bfloat16),
+            jax.ShapeDtypeStruct((length, width), jnp.bfloat16),
             jax.ShapeDtypeStruct((rows, 2 * width), jnp.float32),
         ],
         compiler_params=params(),
-        cost_estimate=cost(2 * rows * length * width * halves * q_cols, 2 * w_all.size + 10 * tokens.size),
+        cost_estimate=cost(2 * length * width * halves * q_cols, 2 * w_all.size + 10 * length * width),
         name="project",
     )(time_embed, tokens, w_all)
 
@@ -473,46 +475,49 @@
     return same & (key_block < query_block)
 
 
-def attend_kernel(listed_ref, edge_ref, qkv_ref, segc_ref, segr_ref, mixed_ref, lse_ref, vt_ref, qz_ref, acc_ref, stat_ref):
-    row = pl.program_id(0)
+def attend_kernel(
+    listed_ref, edge_ref, qkv_ref, segc_ref, segr_ref, mixed_ref, lse_ref,
+    vt_ref, qz_ref, acc_ref, stat_ref, *, row,
+):
     blocks = qkv_ref.shape[0]
 
     def turn(block, carried):
         at = pl.multiple_of(block * BLK, BLK)
-        vt_ref[:, pl.ds(at, BLK)] = transposed(qkv_ref[block, 0, :, 256:384])
+        vt_ref[:, pl.ds(at, BLK)] = transposed(qkv_ref[block, :, 256:384])
         return carried
 
     lax.fori_loop(0, blocks, turn, 0)
 
     def one_query(query_block, carried):
-        query = qkv_ref[query_block, 0, :, :128].astype(jnp.float32) * HEAD_DIM ** (-0.5)
+        query = qkv_ref[query_block, :, :128].astype(jnp.float32) * HEAD_DIM ** (-0.5)
         qz_ref[...] = split_heads(query.astype(jnp.bfloat16))
         stat_ref[0:1, :] = jnp.full((1, 2 * BLK), masked_out, jnp.float32)
         stat_ref[1:2, :] = jnp.zeros((1, 2 * BLK), jnp.float32)
         acc_ref[...] = jnp.zeros(acc_ref.shape, jnp.float32)
 
         def update(key_block, mask):
-            scores = dot_nt(qkv_ref[key_block, 0, :, 128:256], qz_ref[...])
+            keys = qkv_ref[key_block, :, 128:256]
+            at = pl.multiple_of(key_block * BLK, BLK)
+            parts = [slice(head * BLK, (head + 1) * BLK) for head in range(2)]
+            values = [vt_ref[h * HEAD_DIM : (h + 1) * HEAD_DIM, pl.ds(at, BLK)] for h in range(2)]
+            old_max = [stat_ref[0:1, part] for part in parts]
+            old_sum = [stat_ref[1:2, part] for part in parts]
+            old_acc = [acc_ref[:, part] for part in parts]
+            scores = [dot_nt(keys, qz_ref[part, :]) for part in parts]
             if mask is not None:
-                scores = jnp.concatenate(
-                    [
-                        jnp.where(mask, scores[:, :BLK], masked_out),
-                        jnp.where(mask, scores[:, BLK:], masked_out),
-                    ],
-                    axis=1,
-                )
-            old_max = stat_ref[0:1, :]
-            new_max = jnp.maximum(old_max, jnp.max(scores, axis=0, keepdims=True))
-            weights = jnp.exp(scores - new_max)
-            shrink = jnp.exp(old_max - new_max)
-            stat_ref[0:1, :] = new_max
-            stat_ref[1:2, :] = stat_ref[1:2, :] * shrink + jnp.sum(weights, axis=0, keepdims=True)
-            rounded = weights.astype(jnp.bfloat16)
-            at = pl.multiple_of(key_block * BLK, BLK)
+                scores = [jnp.where(mask, one, masked_out) for one in scores]
+            new_max, new_sum, new_acc = [], [], []
             for head in range(2):
-                part = slice(head * BLK, (head + 1) * BLK)
-                value = vt_ref[head * HEAD_DIM : (head + 1) * HEAD_DIM, pl.ds(at, BLK)]
-                acc_ref[:, part] = acc_ref[:, part] * shrink[:, part] + dot_nn(value, rounded[:, part])
+                top = jnp.maximum(old_max[head], jnp.max(scores[head], axis=0, keepdims=True))
+                weights = jnp.exp(scores[head] - top)
+                shrink = jnp.exp(old_max[head] - top)
+                new_max.append(top)
+                new_sum.append(old_sum[head] * shrink + jnp.sum(weights, axis=0, keepdims=True))
+                new_acc.append(old_acc[head] * shrink + dot_nn(values[head], weights.astype(jnp.bfloat16)))
+            for head, part in enumerate(parts):
+                stat_ref[0:1, part] = new_max[head]
+                stat_ref[1:2, part] = new_sum[head]
+                acc_ref[:, part] = new_acc[head]
 
         def one_key(key_block, carried):
             listed = listed_ref[row, query_block * blocks + key_block] != 0
@@ -532,34 +537,31 @@
         total = stat_ref[1:2, :]
         mixed = acc_ref[...] / total
         mixed = jnp.concatenate([mixed[:, :BLK], mixed[:, BLK:]], axis=0).T
-        mixed_ref[query_block, 0] = mixed.astype(jnp.bfloat16)
+        mixed_ref[query_block] = mixed.astype(jnp.bfloat16)
         log_total = stat_ref[0:1, :] + jnp.log(total)
         at = pl.multiple_of(query_block * BLK, BLK)
-        lse_ref[0, 0:1, pl.ds(at, BLK)] = log_total[:, :BLK]
-        lse_ref[0, 1:2, pl.ds(at, BLK)] = log_total[:, BLK:]
+        lse_ref[0:1, pl.ds(at, BLK)] = log_total[:, :BLK]
+        lse_ref[1:2, pl.ds(at, BLK)] = log_total[:, BLK:]
         return carried
 
     lax.fori_loop(0, blocks, one_query, 0)
 
 
-def attend(listed, edges, qkv, segc, segr):
-    blocks, rows, blk, width = qkv.shape
+def attend(row, listed, edges, qkv, segc, segr):
+    blocks, blk, width = qkv.shape
     length = blocks * blk
     pair = 2 * HEAD_DIM
     return pl.pallas_call(
-        attend_kernel,
+        functools.partial(attend_kernel, row=row),
         grid_spec=pltpu.PrefetchScalarGridSpec(
             num_scalar_prefetch=2,
-            grid=(rows,),
+            grid=(1,),
             in_specs=[
-                pl.BlockSpec((blocks, 1, blk, width), lambda r, *_: (0, r, 0, 0)),
-                pl.BlockSpec((1, length, 1), lambda r, *_: (r, 0, 0)),
-                pl.BlockSpec((1, 1, length), lambda r, *_: (r, 0, 0)),
+                whole(qkv.shape),
+                pl.BlockSpec((1, length, 1), lambda i, *_: (row, 0, 0)),
+                pl.BlockSpec((1, 1, length), lambda i, *_: (row, 0, 0)),
             ],
-            out_specs=[
-                pl.BlockSpec((blocks, 1, blk, pair), lambda r, *_: (0, r, 0, 0)),
-                pl.BlockSpec((1, 2, length), lambda r, *_: (r, 0, 0)),
-            ],
+            out_specs=[whole((blocks, blk, pair)), whole((2, length))],
             scratch_shapes=[
                 pltpu.VMEM((pair, length), jnp.bfloat16),
                 pltpu.VMEM((2 * blk, pair), jnp.bfloat16),
@@ -568,31 +570,30 @@
             ],
         ),
         out_shape=[
-            jax.ShapeDtypeStruct((blocks, rows, blk, pair), jnp.bfloat16),
-            jax.ShapeDtypeStruct((rows, 2, length), jnp.float32),
+            jax.ShapeDtypeStruct((blocks, blk, pair), jnp.bfloat16),
+            jax.ShapeDtypeStruct((2, length), jnp.float32),
         ],
         compiler_params=params(),
-        cost_estimate=cost(30e9, 12e6, 40e6),
+        cost_estimate=cost(20e9, 6e6, 20e6),
         name="attend",
     )(listed, edges, qkv, segc, segr)
 
 
 def attend_back_kernel(
     listed_ref, edge_ref, qkv_ref, grad_ref, mixed_ref, lse_ref, segc_ref, segr_ref, out_ref,
-    kt_ref, qz_ref, gz_ref, inner_ref, dq_ref, dk_ref, dv_ref,
+    kt_ref, qz_ref, gz_ref, inner_ref, dq_ref, dk_ref, dv_ref, *, row,
 ):
-    row = pl.program_id(0)
     blocks = qkv_ref.shape[0]
     scale = HEAD_DIM ** (-0.5)
 
     def prepare(block, carried):
         at = pl.multiple_of(block * BLK, BLK)
-        kt_ref[:, pl.ds(at, BLK)] = transposed(qkv_ref[block, 0, :, 128:256])
-        query = qkv_ref[block, 0, :, :128].astype(jnp.float32) * scale
+        kt_ref[:, pl.ds(at, BLK)] = transposed(qkv_ref[block, :, 128:256])
+        query = qkv_ref[block, :, :128].astype(jnp.float32) * scale
         qz_ref[block] = split_heads(query.astype(jnp.bfloat16))
-        grad = grad_ref[block, 0]
+        grad = grad_ref[block]
         gz_ref[block] = split_heads(grad)
-        product = (grad.astype(jnp.float32) * mixed_ref[block, 0].astype(jnp.float32)).T
+        product = (grad.astype(jnp.float32) * mixed_ref[block].astype(jnp.float32)).T
         for head in range(2):
             part = product[head * HEAD_DIM : (head + 1) * HEAD_DIM, :]
             inner_ref[head : head + 1, pl.ds(at, BLK)] = jnp.sum(part, axis=0, keepdims=True)
@@ -608,14 +609,14 @@
 
         def update(query_block, mask):
             query_at = pl.multiple_of(query_block * BLK, BLK)
-            keys = qkv_ref[key_block, 0, :, 128:256]
-            values = qkv_ref[key_block, 0, :, 256:384]
+            keys = qkv_ref[key_block, :, 128:256]
+            values = qkv_ref[key_block, :, 256:384]
             for head in range(2):
                 part = slice(head * BLK, (head + 1) * BLK)
                 query = qz_ref[query_block, part, :]
                 grad = gz_ref[query_block, part, :]
                 scores = dot_nt(keys, query)
-                probs = jnp.exp(scores - lse_ref[0, head : head + 1, pl.ds(query_at, BLK)])
+                probs = jnp.exp(scores - lse_ref[head : head + 1, pl.ds(query_at, BLK)])
                 if mask is not None:
                     probs = jnp.where(mask, probs, 0.0)
                 grad_probs = dot_nt(values, grad)
@@ -645,32 +646,30 @@
 
         lax.fori_loop(key_block, blocks, one_query, 0)
         grad_query = dq_ref[:, pl.ds(key_at, BLK)].T * scale
-        out_ref[key_block, 0] = pair_together(grad_query, dk_ref[...], dv_ref[...]).astype(jnp.bfloat16)
+        out_ref[key_block] = pair_together(grad_query, dk_ref[...], dv_ref[...]).astype(jnp.bfloat16)
         return carried
 
     lax.fori_loop(0, blocks, one_key, 0)
 
 
-def attend_back(listed, edges, qkv, grad, mixed, lse, segc, segr):
-    blocks, rows, blk, width = qkv.shape
+def attend_back(row, listed, edges, qkv, grad, mixed, lse, segc, segr):
+    blocks, blk, width = qkv.shape
     length = blocks * blk
     pair = 2 * HEAD_DIM
-    wide = pl.BlockSpec((blocks, 1, blk, width), lambda r, *_: (0, r, 0, 0))
-    narrow = pl.BlockSpec((blocks, 1, blk, pair), lambda r, *_: (0, r, 0, 0))
     return pl.pallas_call(
-        attend_back_kernel,
+        functools.partial(attend_back_kernel, row=row),
         grid_spec=pltpu.PrefetchScalarGridSpec(
             num_scalar_prefetch=2,
-            grid=(rows,),
+            grid=(1,),
             in_specs=[
-                wide,
-                narrow,
-                narrow,
-                pl.BlockSpec((1, 2, length), lambda r, *_: (r, 0, 0)),
-                pl.BlockSpec((1, length, 1), lambda r, *_: (r, 0, 0)),
-                pl.BlockSpec((1, 1, length), lambda r, *_: (r, 0, 0)),
+                whole(qkv.shape),
+                whole(grad.shape),
+                whole(mixed.shape),
+                whole(lse.shape),
+                pl.BlockSpec((1, length, 1), lambda i, *_: (row, 0, 0)),
+                pl.BlockSpec((1, 1, length), lambda i, *_: (row, 0, 0)),
             ],
-            out_specs=wide,
+            out_specs=whole(qkv.shape),
             scratch_shapes=[
                 pltpu.VMEM((pair, length), jnp.bfloat16),
                 pltpu.VMEM((blocks, 2 * blk, pair), jnp.bfloat16),
@@ -683,72 +682,72 @@
         ),
         out_shape=jax.ShapeDtypeStruct(qkv.shape, jnp.bfloat16),
         compiler_params=params(),
-        cost_estimate=cost(70e9, 20e6, 40e6),
+        cost_estimate=cost(50e9, 10e6, 20e6),
         name="attend_back",
     )(listed, edges, qkv, grad, mixed, lse, segc, segr)
 
 
 def joined(ref, first, count):
-    return jnp.concatenate([ref[first + i, 0] for i in range(count)], axis=1)
-
-
-def outward_kernel(mixed_ref, tok_ref, w_ref, scales_ref, hidden_ref, normed_ref, *, tiles):
-    row = pl.program_id(0) // tiles
+    return jnp.concatenate([ref[first + i] for i in range(count)], axis=1)
+
+
+def outward_kernel(mixed_ref, tok_ref, w_ref, scales_ref, hidden_ref, normed_ref, *, row):
     halves = w_ref.shape[1]
     per_half = mixed_ref.shape[0] // halves
     hidden = tok_ref[0].astype(jnp.float32)
     width = hidden.shape[1]
     for half in range(halves):
         hidden += dot_nt(joined(mixed_ref, half * per_half, per_half), w_ref[:, half].reshape(width, -1))
-    hidden_ref[0] = hidden
+    hidden_ref[...] = hidden
     hat, _ = normalize(hidden)
-    normed_ref[0] = (hat * scales_ref[pl.ds(row, 1), width:]).astype(jnp.bfloat16)
-
-
-def outward(mixed, tokens, w_all, scales, columns):
+    normed_ref[...] = (hat * scales_ref[row : row + 1, width:]).astype(jnp.bfloat16)
+
+
+def outward(row, mixed, tokens, w_all, scales, columns):
     rows, length, width = tokens.shape
-    groups, _, _, pair = mixed.shape
+    groups, _, pair = mixed.shape
     chunks, halves, high, _ = w_all.shape
     tile = 256
-    tiles = length // tile
-    one = pl.BlockSpec((1, tile, width), lambda i: (i // tiles, i % tiles, 0))
+    one = pl.BlockSpec((tile, width), lambda i: (i, 0))
     return pl.pallas_call(
-        functools.partial(outward_kernel, tiles=tiles),
-        grid=(rows * tiles,),
+        functools.partial(outward_kernel, row=row),
+        grid=(length // tile,),
         in_specs=[
-            pl.BlockSpec((groups, 1, tile, pair), lambda i: (0, i // tiles, i % tiles, 0)),
-            one,
+            pl.BlockSpec((groups, tile, pair), lambda i: (0, i, 0)),
+            pl.BlockSpec((1, tile, width), lambda i: (row, i, 0)),
             whole((chunks, halves, high, columns)),
             whole(scales.shape),
         ],
         out_specs=[one, one],
         out_shape=[
-            jax.ShapeDtypeStruct(tokens.shape, jnp.float32),
-            jax.ShapeDtypeStruct(tokens.shape, jnp.bfloat16),
+            jax.ShapeDtypeStruct((length, width), jnp.float32),
+            jax.ShapeDtypeStruct((length, width), jnp.bfloat16),
         ],
         compiler_params=params(),
-        cost_estimate=cost(2 * rows * length * width * width, 12 * tokens.size),
+        cost_estimate=cost(2 * length * width * width, 12 * length * width),
         name="outward",
     )(mixed, tokens, w_all, scales)
 
 
 def mlp_kernel(
-    me_ref, nm_ref, cot_ref, hidden_ref, scales_ref, up_ref, down_ref,
+    me_ref, nm0_ref, nm1_ref, cot_ref, hidden0_ref, hidden1_ref, scales_ref, up_ref, down_ref,
     up_keep_ref, up_send_ref, down_keep_ref, down_send_ref,
     layer_ref, grad_hidden_ref, grad_attn_ref, gscale_ref,
     nmt_ref, cott_ref, out_ref, gn_ref, act_ref, gpre_ref,
 ):
     tile = pl.program_id(0)
     phase = pl.program_id(1)
-    count, width = nm_ref.shape
-    chunk = 256
+    length, width = nm0_ref.shape
+    count = 2 * length
     root = 0.7978845608028654
     cube = 0.044715
 
     @pl.when((tile == 0) & (phase == 0))
     def _():
-        turned_apart(nmt_ref, nm_ref[...], me_ref[0], up_ref.shape[0])
-        turned_apart(cott_ref, cot_ref[...], me_ref[0], up_ref.shape[0])
+        chunks = up_ref.shape[0]
+        turned_apart(nmt_ref.at[:, :length], nm0_ref[...], me_ref[0], chunks)
+        turned_apart(nmt_ref.at[:, length:], nm1_ref[...], me_ref[0], chunks)
+        turned_apart(cott_ref, cot_ref[...], me_ref[0], chunks)
         out_ref[...] = jnp.zeros(out_ref.shape, jnp.float32)
         gn_ref[...] = jnp.zeros(gn_ref.shape, jnp.float32)
 
@@ -756,9 +755,9 @@
     def _():
         up = up_ref[:, 0].reshape(width, -1)
         down = down_ref[:, 0].reshape(width, -1)
-        for at in range(0, count, chunk):
-            part = slice(at, at + chunk)
-            pre = dot_nn(nm_ref[part, :], up)
+        for row, nm_ref in enumerate((nm0_ref, nm1_ref)):
+            part = slice(row * length, (row + 1) * length)
+            pre = dot_nn(nm_ref[...], up)
             grad_act = dot_nn(cot_ref[part, :], down)
             square = pre * pre
             bent = jnp.tanh(root * (pre + cube * pre * square))
@@ -784,14 +783,13 @@
 
     @pl.when((tile == pl.num_programs(0) - 1) & (phase == 1))
     def _():
-        rows = scales_ref.shape[0]
-        per_row = count // rows
-        for row in range(rows):
+        chunk = 256
+        for row, hidden_ref in enumerate((hidden0_ref, hidden1_ref)):
             scale = scales_ref[row : row + 1, width:]
             total = jnp.zeros((1, width), jnp.float32)
-            for at in range(row * per_row, (row + 1) * per_row, chunk):
-                part = slice(at, at + chunk)
-                hidden = hidden_ref[part, :]
+            for at in range(0, length, chunk):
+                part = slice(row * length + at, row * length + at + chunk)
+                hidden = hidden_ref[at : at + chunk, :]
                 layer_ref[part, :] = (hidden + out_ref[part, :]).astype(jnp.bfloat16)
                 hat, inverse = normalize(hidden)
                 grad = gn_ref[part, :]
@@ -803,7 +801,7 @@
 
 
 def mlp(me, normed, cotangent, hidden, scales, w_all, skip, hidden_cols):
-    rows, length, width = hidden.shape
+    rows, length, width = cotangent.shape
     count = rows * length
     chunks, halves, high, columns = w_all.shape
     tile = 512
@@ -826,9 +824,11 @@
             num_scalar_prefetch=1,
             grid=(halves * per_half, 2),
             in_specs=[
+                whole((length, width)),
+                whole((length, width)),
                 whole(flat),
-                whole(flat),
-                whole(flat),
+                whole((length, width)),
+                whole((length, width)),
                 whole(scales.shape),
                 pl.BlockSpec((chunks, 1, high, tile), up_at),
                 pl.BlockSpec((chunks, 1, high, tile), down_at),
@@ -854,73 +854,73 @@
         compiler_params=params(60),
         cost_estimate=cost(12 * count * width * halves * hidden_cols, 4 * w_all.size + 16 * count * width),
         name="mlp",
-    )(me, normed.reshape(flat), cotangent.reshape(flat), hidden.reshape(flat), scales, w_all, w_all)
+    )(me, *normed, cotangent.reshape(flat), *hidden, scales, w_all, w_all)
 
 
 def grad_mixed_kernel(grad_ref, w_ref, out_ref):
     halves = w_ref.shape[1]
     per_half = out_ref.shape[0] // halves
     grad = grad_ref[...]
-    pair = out_ref.shape[3]
+    pair = out_ref.shape[2]
     for half in range(halves):
         out = dot_nn(grad, w_ref[:, half].reshape(grad.shape[1], -1)).astype(jnp.bfloat16)
         for group in range(per_half):
-            out_ref[half * per_half + group, 0] = out[:, group * pair : (group + 1) * pair]
-
-
-def grad_mixed_of(grad_attn, w_all, mixed_shape, columns):
-    groups, rows, length, pair = mixed_shape
+            out_ref[half * per_half + group] = out[:, group * pair : (group + 1) * pair]
+
+
+def grad_mixed_of(row, grad_attn, w_all, mixed_shape, columns):
+    groups, length, pair = mixed_shape
     chunks, halves, high, _ = w_all.shape
     width = grad_attn.shape[1]
     tile = 256
     tiles = length // tile
     return pl.pallas_call(
         grad_mixed_kernel,
-        grid=(rows * tiles,),
+        grid=(tiles,),
         in_specs=[
-            pl.BlockSpec((tile, width), lambda i: (i, 0)),
+            pl.BlockSpec((tile, width), lambda i: (row * tiles + i, 0)),
             whole((chunks, halves, high, columns)),
         ],
-        out_specs=pl.BlockSpec((groups, 1, tile, pair), lambda i: (0, i // tiles, i % tiles, 0)),
+        out_specs=pl.BlockSpec((groups, tile, pair), lambda i: (0, i, 0)),
         out_shape=jax.ShapeDtypeStruct(mixed_shape, jnp.bfloat16),
         compiler_params=params(),
-        cost_estimate=cost(2 * rows * length * width * width, 8 * rows * length * width),
+        cost_estimate=cost(2 * length * width * width, 8 * length * width),
         name="grad_mixed",
     )(grad_attn, w_all)
 
 
-def grad_proj_kernel(me_ref, grad_ref, mixed_ref, keep_ref, send_ref, turned_ref):
-    count, width = grad_ref.shape
+def grad_proj_kernel(me_ref, grad_ref, *refs):
+    mixed_refs, (keep_ref, send_ref, turned_ref) = refs[:-3], refs[-3:]
+    width = grad_ref.shape[1]
 
     @pl.when(pl.program_id(0) == 0)
     def _():
         turned_apart(turned_ref, grad_ref[...], me_ref[0], 4 * keep_ref.shape[2])
 
-    pair = mixed_ref.shape[3]
-    mixed = jnp.concatenate(
-        [mixed_ref[i].reshape(count, pair) for i in range(mixed_ref.shape[0])], axis=1
-    )
-    grad = dot_nn(turned_ref[...], mixed).astype(jnp.bfloat16)
+    grad = 0.0
+    for row, mixed_ref in enumerate(mixed_refs):
+        length = mixed_ref.shape[1]
+        part = slice(row * length, (row + 1) * length)
+        grad += dot_nn(turned_ref[:, part], joined(mixed_ref, 0, mixed_ref.shape[0]))
+    grad = grad.astype(jnp.bfloat16)
     shape = keep_ref.shape[1:]
     keep_ref[0] = grad[: width // 2].reshape(shape)
     send_ref[0] = grad[width // 2 :].reshape(shape)
 
 
 def grad_proj_of(me, grad_attn, mixed, chunks, halves, columns):
-    groups, rows, length, pair = mixed.shape
+    groups, length, pair = mixed[0].shape
     count, width = grad_attn.shape
     high = width // chunks
     shape = (halves, 2, chunks // 4, high, columns)
     one = pl.BlockSpec((1,) + shape[1:], lambda h, me: (h ^ me[1], 0, 0, 0, 0))
+    given = pl.BlockSpec((groups // halves, length, pair), lambda h, me: (h, 0, 0))
     return pl.pallas_call(
         grad_proj_kernel,
         grid_spec=pltpu.PrefetchScalarGridSpec(
             num_scalar_prefetch=1,
             grid=(halves,),
-            in_specs=[
-                whole(grad_attn.shape),
-                pl.BlockSpec((groups // halves, rows, length, pair), lambda h, me: (h, 0, 0, 0)),
-            ],
+            in_specs=[whole(grad_attn.shape)] + [given] * len(mixed),
             out_specs=[one, one],
             scratch_shapes=[pltpu.VMEM((width, count), jnp.bfloat16)],
         ),
@@ -928,12 +928,11 @@
         compiler_params=params(),
         cost_estimate=cost(2 * count * width * width, 6 * count * width),
         name="grad_proj",
-    )(me, grad_attn, mixed)
-
-
-def first_norm_kernel(gq_ref, tok_ref, grad_hidden_ref, w_ref, scales_ref, out_ref, gscale_ref, *, tiles, q_cols):
+    )(me, grad_attn, *mixed)
+
+
+def first_norm_kernel(gq_ref, tok_ref, grad_hidden_ref, w_ref, scales_ref, out_ref, gscale_ref, *, row, q_cols):
     step = pl.program_id(0)
-    row = step // tiles
     halves = w_ref.shape[1]
     per_half = gq_ref.shape[0] // halves
     values = tok_ref[0].astype(jnp.float32)
@@ -945,146 +944,142 @@
     hat, inverse = normalize(values)
     total = jnp.sum(grad * hat, axis=0, keepdims=True)
 
-    @pl.when(step % tiles == 0)
+    @pl.when(step == 0)
     def _():
-        gscale_ref[pl.ds(row, 1), :] = total
-
-    @pl.when(step % tiles != 0)
+        gscale_ref[...] = total
+
+    @pl.when(step != 0)
     def _():
-        gscale_ref[pl.ds(row, 1), :] += total
-
-    back = normalize_back(grad * scales_ref[pl.ds(row, 1), :width], hat, inverse)
-    out_ref[0] = (grad_hidden_ref[0] + back).astype(jnp.bfloat16)
-
-
-def first_norm_back(grad_qkv, tokens, grad_hidden, w_all, scales, q_cols):
+        gscale_ref[...] += total
+
+    back = normalize_back(grad * scales_ref[row : row + 1, :width], hat, inverse)
+    out_ref[...] = (grad_hidden_ref[...] + back).astype(jnp.bfloat16)
+
+
+def first_norm_back(row, grad_qkv, tokens, grad_hidden, w_all, scales, q_cols):
     rows, length, width = tokens.shape
-    groups, _, _, pair = grad_qkv.shape
+    groups, _, pair = grad_qkv.shape
     tile = 256
     tiles = length // tile
-    one = pl.BlockSpec((1, tile, width), lambda i: (i // tiles, i % tiles, 0))
     return pl.pallas_call(
-        functools.partial(first_norm_kernel, tiles=tiles, q_cols=q_cols),
-        grid=(rows * tiles,),
+        functools.partial(first_norm_kernel, row=row, q_cols=q_cols),
+        grid=(tiles,),
         in_specs=[
-            pl.BlockSpec((groups, 1, tile, pair), lambda i: (0, i // tiles, i % tiles, 0)),
-            one,
-            one,
+            pl.BlockSpec((groups, tile, pair), lambda i: (0, i, 0)),
+            pl.BlockSpec((1, tile, width), lambda i: (row, i, 0)),
+            pl.BlockSpec((tile, width), lambda i: (row * tiles + i, 0)),
             whole(w_all.shape),
             whole(scales.shape),
         ],
-        out_specs=[one, whole((rows, width))],
+        out_specs=[pl.BlockSpec((tile, width), lambda i: (i, 0)), whole((1, width))],
         out_shape=[
-            jax.ShapeDtypeStruct(tokens.shape, jnp.bfloat16),
-            jax.ShapeDtypeStruct((rows, width), jnp.float32),
+            jax.ShapeDtypeStruct((length, width), jnp.bfloat16),
+            jax.ShapeDtypeStruct((1, width), jnp.float32),
         ],
         compiler_params=params(),
-        cost_estimate=cost(2 * rows * length * width * groups * pair, 2 * w_all.size + 20 * tokens.size),
+        cost_estimate=cost(2 * length * width * groups * pair, 2 * w_all.size + 20 * length * width),
         name="first_norm_back",
     )(grad_qkv, tokens, grad_hidden, w_all, scales)
 
 
-def grad_qkv_kernel(
-    me_ref, normed_ref, gq_ref, tet_ref, gs_ref,
-    a_keep_ref, a_send_ref, b_keep_ref, b_send_ref, t_keep_ref, t_send_ref,
-    turned_ref, tet_apart_ref, *, pairs, chunks, folds, t_cols,
-):
-    half = pl.program_id(0)
-    part = pl.program_id(1)
-    count, width = normed_ref.shape
-
-    @pl.when((half == 0) & (part == 0))
+def grad_qkv_kernel(me_ref, *refs, chunks, at_front):
+    rows = (len(refs) - 3) // 2
+    normed_refs, gq_refs, (keep_ref, send_ref, turned_ref) = refs[:rows], refs[rows:-3], refs[-3:]
+    length, width = normed_refs[0].shape
+
+    @pl.when((pl.program_id(0) == 0) & (pl.program_id(1) == 0))
     def _():
-        turned_apart(turned_ref, normed_ref[...], me_ref[0], chunks)
-        bits = chunks.bit_length() - 1
-        high = tet_ref.shape[0] // chunks
-        for chunk in range(chunks):
-            apart = chunk ^ me_ref[0]
-            place = 0
-            for bit in range(bits):
-                place += ((apart >> bit) & 1) << (bits - 1 - bit)
-            tet_apart_ref[pl.ds(pl.multiple_of(place * high, high), high), :] = tet_ref[
-                chunk * high : (chunk + 1) * high, :
-            ]
-
-    def grad():
-        return dot_nn(turned_ref[...], gq_ref[0].reshape(count, -1)).astype(jnp.bfloat16)
-
-    @pl.when(part < pairs // 2)
-    def _():
-        found = grad()
-        shape = a_keep_ref.shape[1:]
-        a_keep_ref[0] = found[: width // 2].reshape(shape)
-        a_send_ref[0] = found[width // 2 :].reshape(shape)
-
-    @pl.when((part >= pairs // 2) & (part < pairs))
-    def _():
-        found = grad()
-        shape = (b_keep_ref.shape[0],) + b_keep_ref.shape[2:]
-        b_keep_ref[:, 0] = found[: width // 2].reshape(shape)
-        b_send_ref[:, 0] = found[width // 2 :].reshape(shape)
-
-    @pl.when(part == pairs)
-    def _():
-        k_rows = tet_ref.shape[0] // chunks
-        shape = t_keep_ref.shape[1:3] + (k_rows, t_cols)
-        for fold in range(folds):
-            at = pl.multiple_of((half * folds + fold) * t_cols, t_cols)
-            total = jnp.zeros((chunks * k_rows, t_cols), jnp.float32)
-            for row in range(gs_ref.shape[0]):
-                total += tet_apart_ref[:, row : row + 1] * gs_ref[row : row + 1, pl.ds(at, t_cols)]
-            total = total.astype(jnp.bfloat16)
-            middle = chunks * k_rows // 2
-            t_keep_ref[0, :, :, fold * k_rows : (fold + 1) * k_rows, :] = total[:middle].reshape(shape)
-            t_send_ref[0, :, :, fold * k_rows : (fold + 1) * k_rows, :] = total[middle:].reshape(shape)
-
-
-def grad_qkv_of(me, normed, grad_qkv, time_embed, grad_scales, chunks, halves, k_rows, t_cols):
-    rows, length, width = normed.shape
-    groups, _, _, pair = grad_qkv.shape
+        for row in range(rows):
+            part = slice(row * length, (row + 1) * length)
+            turned_apart(turned_ref.at[:, part], normed_refs[row][...], me_ref[0], chunks)
+
+    found = 0.0
+    for row in range(rows):
+        found += dot_nn(turned_ref[:, row * length : (row + 1) * length], gq_refs[row][0])
+    found = found.astype(jnp.bfloat16)
+    if at_front:
+        shape = keep_ref.shape[1:]
+        keep_ref[0] = found[: width // 2].reshape(shape)
+        send_ref[0] = found[width // 2 :].reshape(shape)
+    else:
+        shape = (keep_ref.shape[0],) + keep_ref.shape[2:]
+        keep_ref[:, 0] = found[: width // 2].reshape(shape)
+        send_ref[:, 0] = found[width // 2 :].reshape(shape)
+
+
+def grad_qkv_of(me, normed, grad_qkv, chunks, halves, first, some, at_front):
+    length, width = normed[0].shape
+    rows = len(normed)
+    groups, _, pair = grad_qkv[0].shape
     pairs = groups // halves
     high = width // chunks
-    count = rows * length
     quarter = chunks // 4
-    some = pairs // 2
-    turned = time_embed.T
-    a_out = pl.BlockSpec(
-        (1, 2, quarter, high, pair), lambda h, j, me: (h ^ me[1], 0, 0, 0, jnp.minimum(j, some - 1))
-    )
-    b_out = pl.BlockSpec(
-        (2, 1, quarter, high, pair),
-        lambda h, j, me: (0, h ^ me[1], 0, 0, jnp.clip(j - some, 0, some - 1)),
-    )
-    t_out = pl.BlockSpec((1, 2, quarter, high, t_cols), lambda h, j, me: (h ^ me[1], 0, 0, 0, 0))
+    if at_front:
+        out = pl.BlockSpec((1, 2, quarter, high, pair), lambda h, j, me: (h ^ me[1], 0, 0, 0, j))
+    else:
+        out = pl.BlockSpec((2, 1, quarter, high, pair), lambda h, j, me: (0, h ^ me[1], 0, 0, j))
     wide = jax.ShapeDtypeStruct((halves, 2, quarter, high, some * pair), jnp.bfloat16)
-    thin = jax.ShapeDtypeStruct((halves, 2, quarter, high, t_cols), jnp.bfloat16)
+    given = pl.BlockSpec((1, length, pair), lambda h, j, me: (h * pairs + first + j, 0, 0))
     return pl.pallas_call(
-        functools.partial(
-            grad_qkv_kernel, pairs=pairs, chunks=chunks, folds=high // k_rows, t_cols=t_cols
-        ),
+        functools.partial(grad_qkv_kernel, chunks=chunks, at_front=at_front),
         grid_spec=pltpu.PrefetchScalarGridSpec(
             num_scalar_prefetch=1,
-            grid=(halves, pairs + 1),
-            in_specs=[
-                whole((count, width)),
-                pl.BlockSpec(
-                    (1, rows, length, pair),
-                    lambda h, j, me: (h * pairs + jnp.minimum(j, pairs - 1), 0, 0, 0),
-                ),
-                whole(turned.shape),
-                whole(grad_scales.shape),
-            ],
-            out_specs=[a_out, a_out, b_out, b_out, t_out, t_out],
-            scratch_shapes=[
-                pltpu.VMEM((width, count), jnp.bfloat16),
-                pltpu.VMEM(turned.shape, jnp.float32),
-            ],
+            grid=(halves, some),
+            in_specs=[whole((length, width))] * rows + [given] * rows,
+            out_specs=[out, out],
+            scratch_shapes=[pltpu.VMEM((width, rows * length), jnp.bfloat16)],
         ),
-        out_shape=[wide] * 4 + [thin] * 2,
+        out_shape=[wide] * 2,
         compiler_params=params(),
-        cost_estimate=cost(2 * count * width * groups * pair, 6 * count * width),
+        cost_estimate=cost(2 * rows * length * width * halves * some * pair, 6 * rows * length * width),
         name="grad_qkv",
-    )(me, normed.reshape(count, width), grad_qkv, turned, grad_scales)
+    )(me, *normed, *grad_qkv)
+
+
+def grad_time_kernel(me_ref, tet_ref, gs_ref, keep_ref, send_ref, apart_ref, *, chunks, folds, t_cols):
+    bits = chunks.bit_length() - 1
+    k_rows = tet_ref.shape[0] // chunks
+    for chunk in range(chunks):
+        apart = chunk ^ me_ref[0]
+        place = 0
+        for bit in range(bits):
+            place += ((apart >> bit) & 1) << (bits - 1 - bit)
+        apart_ref[pl.ds(pl.multiple_of(place * k_rows, k_rows), k_rows), :] = tet_ref[
+            chunk * k_rows : (chunk + 1) * k_rows, :
+        ]
+    half = pl.program_id(0)
+    shape = keep_ref.shape[1:3] + (k_rows, t_cols)
+    middle = chunks * k_rows // 2
+    for fold in range(folds):
+        at = pl.multiple_of((half * folds + fold) * t_cols, t_cols)
+        total = jnp.zeros((chunks * k_rows, t_cols), jnp.float32)
+        for row in range(gs_ref.shape[0]):
+            total += apart_ref[:, row : row + 1] * gs_ref[row : row + 1, pl.ds(at, t_cols)]
+        total = total.astype(jnp.bfloat16)
+        rows = slice(fold * k_rows, (fold + 1) * k_rows)
+        keep_ref[0, :, :, rows, :] = total[:middle].reshape(shape)
+        send_ref[0, :, :, rows, :] = total[middle:].reshape(shape)
+
+
+def grad_time_of(me, time_embed, grad_scales, chunks, halves, high, k_rows, t_cols):
+    turned = time_embed.T
+    quarter = chunks // 4
+    thin = jax.ShapeDtypeStruct((halves, 2, quarter, high, t_cols), jnp.bfloat16)
+    out = pl.BlockSpec((1, 2, quarter, high, t_cols), lambda h, me: (h ^ me[1], 0, 0, 0, 0))
+    return pl.pallas_call(
+        functools.partial(grad_time_kernel, chunks=chunks, folds=high // k_rows, t_cols=t_cols),
+        grid_spec=pltpu.PrefetchScalarGridSpec(
+            num_scalar_prefetch=1,
+            grid=(halves,),
+            in_specs=[whole(turned.shape), whole(grad_scales.shape)],
+            out_specs=[out, out],
+            scratch_shapes=[pltpu.VMEM(turned.shape, jnp.float32)],
+        ),
+        out_shape=[thin] * 2,
+        compiler_params=params(),
+        cost_estimate=cost(4 * turned.shape[0] * grad_scales.size, 4 * grad_scales.size),
+        name="grad_time",
+    )(me, turned, grad_scales)
 
 
 def across(values, axis, apart):
@@ -1099,20 +1094,38 @@
     return total
 
 
-STAGES = {"x": ("ctx", 2), "y": ("tp", 1)}
-
-
-def scatter_sum(keep, send, order):
-    parts = [keep, across(send, "ctx", 1)]
-    for name in order:
-        axis, apart = STAGES[name]
-        given = across(summed(parts, 1).astype(jnp.bfloat16), axis, apart)
-        parts = [part[0] for part in parts] + [given]
-    given = across(summed(parts, slice(2, 4)).astype(jnp.bfloat16), "fsdp", 1)
-    parts = [part[:2] for part in parts] + [given]
-    given = across(summed(parts, 1).astype(jnp.bfloat16), "fsdp", 2)
-    parts = [part[0] for part in parts] + [given]
-    return summed(parts, slice(None))
+HOPS = {"x": ("ctx", 2), "y": ("tp", 1), "near": ("fsdp", 1), "far": ("fsdp", 2)}
+
+
+class TreeSum:
+    def __init__(self, keep, send, order):
+        self.parts = [keep, across(send, "ctx", 1)]
+        self.left = list(order) + ["near", "far"]
+
+    def ready(self):
+        upper = slice(2, 4) if self.left[0] == "near" else 1
+        self.given = summed(self.parts, upper).astype(jnp.bfloat16)
+        return self.given
+
+    def go(self):
+        name = self.left.pop(0)
+        lower = slice(0, 2) if name == "near" else 0
+        self.parts = [part[lower] for part in self.parts] + [across(self.given, *HOPS[name])]
+
+    def finish(self):
+        while self.left:
+            self.ready()
+            self.go()
+        return summed(self.parts, slice(None))
+
+
+def together(value, trees):
+    given = [tree.ready() for tree in trees]
+    value, *given = lax.optimization_barrier((value, *given))
+    for tree, one in zip(trees, given):
+        tree.given = one
+        tree.go()
+    return value
 
 
 def listed_table(block_pairs, pair_counts, row_blocks, ctx_size):
@@ -1163,47 +1176,70 @@
     segc = segment_ids[:, :, None]
     segr = segment_ids[:, None, :]
 
-    qkv, normed, scales = project(time_embed, tokens, first, k_rows, q_cols, t_cols)
-    qkv = lax.all_to_all(qkv, GROUP, 0, 0, tiled=True)
-    mixed_own, lse = attend(listed, edges, qkv, segc, segr)
-    mixed = lax.all_to_all(mixed_own, GROUP, 0, 0, tiled=True)
-    hidden, normed_mlp = outward(mixed, tokens, second, scales, o_cols)
+    qkv, normed = [], []
+    for row in range(rows):
+        out, one, scales = project(row, time_embed, tokens, first, k_rows, q_cols, t_cols)
+        qkv.append(lax.all_to_all(out, GROUP, 0, 0, tiled=True))
+        normed.append(one)
+    mixed_own, lse, mixed = [], [], []
+    for row in range(rows):
+        out, one = attend(row, listed, edges, qkv[row], segc, segr)
+        mixed_own.append(out)
+        lse.append(one)
+        mixed.append(lax.all_to_all(out, GROUP, 0, 0, tiled=True))
+    hidden, normed_mlp = [], []
+    for row in range(rows):
+        out, one = outward(row, mixed[row], tokens, second, scales, o_cols)
+        hidden.append(out)
+        normed_mlp.append(one)
     up_keep, up_send, down_keep, down_send, layer_out, grad_hidden, grad_attn, gscale_mlp = mlp(
         me, normed_mlp, cotangent, hidden, scales, second, o_cols, f_cols
     )
-    grad_mixed = grad_mixed_of(grad_attn, second, mixed.shape, o_cols)
-    grad_mixed = lax.all_to_all(grad_mixed, GROUP, 0, 0, tiled=True)
+    down_tree = TreeSum(down_keep, down_send, "xy")
+    up_tree = TreeSum(up_keep, up_send, "yx")
+    grad_mixed = []
+    for row in range(rows):
+        out = grad_mixed_of(row, grad_attn, second, mixed[row].shape, o_cols)
+        grad_mixed.append(lax.all_to_all(out, GROUP, 0, 0, tiled=True))
     out_keep, out_send = grad_proj_of(me, grad_attn, mixed, chunks, halves, o_cols)
-    grad_down = scatter_sum(down_keep, down_send, "xy")
-    grad_up = scatter_sum(up_keep, up_send, "yx")
-    grad_mixed, out_keep, out_send = lax.optimization_barrier((grad_mixed, out_keep, out_send))
-    grad_out = scatter_sum(out_keep, out_send, "yx")
-    grad_qkv = attend_back(listed, edges, qkv, grad_mixed, mixed_own, lse, segc, segr)
-    grad_qkv = lax.all_to_all(grad_qkv, GROUP, 0, 0, tiled=True)
-    grad_tokens, gscale_attn = first_norm_back(
-        grad_qkv, tokens, grad_hidden.reshape(tokens.shape), first, scales, q_cols
-    )
-    grad_scales = jnp.concatenate([gscale_attn, gscale_mlp], axis=1)
-    a_keep, a_send, b_keep, b_send, t_keep, t_send = grad_qkv_of(
-        me, normed, grad_qkv, time_embed, grad_scales, chunks, halves, k_rows, t_cols
-    )
-    grad_time = scatter_sum(t_keep, t_send, "yx").reshape(folds, k_rows, t_cols)
+    out_tree = TreeSum(out_keep, out_send, "yx")
+    trees = [down_tree, up_tree, out_tree]
+    grad_qkv = []
+    for row in range(rows):
+        grad_mixed[row] = together(grad_mixed[row], trees)
+        out = attend_back(row, listed, edges, qkv[row], grad_mixed[row], mixed_own[row], lse[row], segc, segr)
+        grad_qkv.append(lax.all_to_all(out, GROUP, 0, 0, tiled=True))
+    grad_tokens, gscale_attn = [], []
+    for row in range(rows - 1):
+        out, one = first_norm_back(row, grad_qkv[row], tokens, grad_hidden, first, scales, q_cols)
+        grad_tokens.append(out)
+        gscale_attn.append(one)
+    some = q_cols // (6 * HEAD_DIM) // 2
+    a_keep, a_send = grad_qkv_of(me, normed, grad_qkv, chunks, halves, 0, some, True)
+    b_keep, b_send = grad_qkv_of(me, normed, grad_qkv, chunks, halves, some, some, False)
+    last, a_keep, b_keep = lax.optimization_barrier((grad_qkv[-1], a_keep, b_keep))
+    out, one = first_norm_back(rows - 1, last, tokens, grad_hidden, first, scales, q_cols)
+    grad_tokens.append(out)
+    gscale_attn.append(one)
+    grad_scales = jnp.concatenate([jnp.concatenate(gscale_attn, axis=0), gscale_mlp], axis=1)
+    t_keep, t_send = grad_time_of(me, time_embed, grad_scales, chunks, halves, high, k_rows, t_cols)
+    grad_time = TreeSum(t_keep, t_send, "yx").finish().reshape(folds, k_rows, t_cols)
     grad_time = grad_time.transpose(1, 0, 2).reshape(k_rows, t_all)
     other = across(grad_time.astype(jnp.bfloat16), "tp", 1).astype(jnp.float32)
     grad_time = jnp.concatenate(
         [jnp.where(mine == 0, grad_time, other), jnp.where(mine == 0, other, grad_time)], axis=1
     )
     grad_w_qkv = jnp.concatenate(
-        [scatter_sum(a_keep, a_send, "yx"), scatter_sum(b_keep, b_send, "xy")], axis=1
+        [TreeSum(a_keep, a_send, "yx").finish(), TreeSum(b_keep, b_send, "xy").finish()], axis=1
     )
     return (
         layer_out.reshape(tokens.shape),
-        grad_tokens,
+        jnp.stack(grad_tokens),
         grad_time,
         grad_w_qkv,
-        grad_out,
-        grad_up,
-        grad_down,
+        out_tree.finish(),
+        up_tree.finish(),
+        down_tree.finish(),
     )
 
 

time: 830 us -> 716 us (0.86)
  waiting for transfers between devices: 399 us -> 236 us
  starting transfers between devices: 47.2 us -> 68.1 us
  Pallas kernels: 310 us -> 329 us
    ppermute x34, waiting for transfers between devices: 280 us -> 104 us  [across(): return lax.ppermute(values, axis, [(i, i ^ apart) for i in range(size)])]
    all_gather x1, waiting for transfers between devices: 0.01 us -> 19.6 us  [spread_body(): lax.all_gather(second, EVERY, axis=0, tiled=True)]
    pallas_call x7 -> x15, Pallas kernels: 227 us -> 247 us  [the longest x2 99 us: attend_back(): pl.pallas_call(functools.partial(attend_back_kernel, row=row), grid_spec=...]
    all_to_all x4 -> x8, starting transfers between devices: 17.2 us -> 32.8 us  [the longest x2 8.52 us: spread_body(): grad_mixed.append(lax.all_to_all(out, GROUP, 0, 0, tiled=True))]
    all_to_all x4 -> x8, waiting for transfers between devices: 43.5 us -> 36.6 us  [the longest x2 35.6 us: spread_body(): qkv.append(lax.all_to_all(out, GROUP, 0, 0, tiled=True))]
  transfers between devices with their start and end apart: 40 -> 44, of which waited for: 19 -> 20; matrix products, arithmetic and copies ran while one was open for 5% -> 7% of each run, Pallas kernels for 27% -> 35%
where the time goes in v2:
time: 716 us; the launch traced here: 703 us
  Pallas kernels  329 us (46%)
  waiting for transfers between devices  236 us (33%)
  starting transfers between devices  68.1 us (10%)
  other arithmetic  43.2 us (6%)
  between operations  15 us (2%)
  local copies, waits for them, and re-layouts  10.9 us (2%)
    ppermute x34, waiting for transfers between devices, across(): return lax.ppermute(values, axis, [(i, i ^ apart) for i in range(size)])  104 us
    pallas_call x2, Pallas kernels, attend_back(): pl.pallas_call(functools.partial(attend_back_kernel, row=row), grid_spec=...  99 us
    pallas_call x1, Pallas kernels, mlp(): pl.pallas_call(mlp_kernel, grid_spec=pltpu.PrefetchScalarGridSpec(num_sca...  75.9 us
    all_gather x1, waiting for transfers between devices, spread_body(): lax.all_gather(first, EVERY, axis=0, tiled=True)  75.9 us
    pallas_call x2, Pallas kernels, attend(): pl.pallas_call(functools.partial(attend_kernel, row=row), grid_spec=pltpu...  69.7 us
    all_to_all x2, waiting for transfers between devices, spread_body(): qkv.append(lax.all_to_all(out, GROUP, 0, 0, tiled=True))  35.6 us
    ppermute x34, starting transfers between devices, across(): return lax.ppermute(values, axis, [(i, i ^ apart) for i in range(size)])  35.2 us
    convert_element_type x24, other arithmetic, ready(): self.given = summed(self.parts, upper).astype(jnp.bfloat16)  27.1 us
  transfers between devices with their start and end apart: 44, of which 20 were waited for; matrix products, arithmetic and copies ran while one was open for 7% of the time, Pallas kernels for 35%

profile of v2, /device:TPU:0, one launch (start us, length us, event | category | flops | bytes accessed | tf_op | source)
XLA Modules:
  0.0 702.7 jit_solution(11211645099937018425)
XLA Ops:
  11.9 75.9 %all-gather.3.cloned.1.call-done = bf16[2048,1792]{1,0:T(8,128)(2,1)} async-done(((bf16[64,1792]{1,0:T(8,128)(2,1)}), bf16[2048,1792]{1,0:T(8,128)(2,1)}) %all-gather.3.cloned.1.call-update) | async-done | bytes 7340048 | tf_op jit(solution)/shard_map/all_gather | solution.py:1170
  87.8 9.5 %project.2 = (bf16[8,512,384]{2,1,0:T(8,128)(2,1)}, bf16[512,1024]{1,0:T(8,128)(2,1)}, f32[2,2048]{1,0:T(2,128)}) custom-call(f32[2,256]{1,0:T(2,128)} %te_ref.3, bf16[2,512,1024]{2,1,0:T(8,128)(2,1)} %tok_ref.11, bf16[16,2,64,1792]{3,2,1,0:T(8,128)(2,1)} %bitcast.338), custom_call_target="tpu_custom_call" | custom-call | flops 3221225472 | bytes 12582912 | tf_op jit(solution)/shard_map/project/pallas_call | solution.py:434
  97.4 3.8 all-to-all-start
  101.6 1.7 collective-permute-start.2
  104.5 9.5 %project.3 = (bf16[8,512,384]{2,1,0:T(8,128)(2,1)}, bf16[512,1024]{1,0:T(8,128)(2,1)}, f32[2,2048]{1,0:T(2,128)}) custom-call(f32[2,256]{1,0:T(2,128)} %te_ref.3, bf16[2,512,1024]{2,1,0:T(8,128)(2,1)} %tok_ref.11, bf16[16,2,64,1792]{3,2,1,0:T(8,128)(2,1)} %bitcast.339), custom_call_target="tpu_custom_call" | custom-call | flops 3221225472 | bytes 12582912 | tf_op jit(solution)/shard_map/project/pallas_call | solution.py:434
  114.0 31.8 %all-to-all-done.qkv_ref = bf16[8,512,384]{2,1,0:T(8,128)(2,1)S(1)} async-done(((bf16[8,512,384]{2,1,0:T(8,128)(2,1)}), bf16[8,512,384]{2,1,0:T(8,128)(2,1)S(1)}, u32[]{:S(2)}, u32[]{:S(2)}) %all-to-all-start) | async-done | bytes 3145760 | tf_op jit(solution)/shard_map/all_to_all | solution.py:1182
  145.8 1.6 copy-done.7
  147.5 4.4 all-to-all-start.2
  152.8 2.7 copy.46.segc_ref
  157.1 43.5 %attend.2 = (bf16[8,512,128]{2,1,0:T(8,128)(2,1)}, f32[2,4096]{1,0:T(2,128)}) custom-call(s32[2,64]{1,0:T(2,128)} %convert_element_type.665.listed_ref, s32[2,16]{1,0:T(2,128)} %pad_add_fusion.2.edge_ref, bf16[8,512,384]{2,1,0:T(8,128)(2,1)} %copy-done.7, s32[2,4096,1]{2,1,0:T(8,128)} %copy.46.segc_ref, s32[2,1,4096]{2,1,0:T(1,128)} %broadcast_in_dim.19.segr_ref), custom_call_target="tpu_custom_call" | custom-call | flops 20000000000 | bytes 6000000 | tf_op jit(solution)/shard_map/attend/pallas_call | solution.py:554
  200.7 3.7 all-to-all-done.2.qkv_ref
  204.4 3.6 all-to-all-start.1
  208.0 26.2 %attend.3 = (bf16[8,512,128]{2,1,0:T(8,128)(2,1)}, f32[2,4096]{1,0:T(2,128)}) custom-call(s32[2,64]{1,0:T(2,128)} %convert_element_type.665.listed_ref, s32[2,16]{1,0:T(2,128)} %pad_add_fusion.2.edge_ref, bf16[8,512,384]{2,1,0:T(8,128)(2,1)} %all-to-all-done.2.qkv_ref, s32[2,4096,1]{2,1,0:T(8,128)} %copy.46.segc_ref, s32[2,1,4096]{2,1,0:T(1,128)} %broadcast_in_dim.19.segr_ref), custom_call_target="tpu_custom_call" | custom-call | flops 20000000000 | bytes 6000000 | tf_op jit(solution)/shard_map/attend/pallas_call | solution.py:554
  234.2 4.1 all-to-all-start.3
  238.8 19.6 %all-gather.5.cloned.1.call-done = bf16[2048,4608]{1,0:T(8,128)(2,1)} async-done(((bf16[64,4608]{1,0:T(8,128)(2,1)}), bf16[2048,4608]{1,0:T(8,128)(2,1)}) %all-gather.5.cloned.1.call-update) | async-done | bytes 18874384 | tf_op jit(solution)/shard_map/all_gather | solution.py:1171
  258.5 4.8 outward.2
  264.3 4.8 outward.3
  269.1 75.9 %mlp.1 = (bf16[2,2,4,64,2048]{4,3,2,1,0:T(8,128)(2,1)}, bf16[2,2,4,64,2048]{4,3,2,1,0:T(8,128)(2,1)}, bf16[2,2,4,64,2048]{4,3,2,1,0:T(8,128)(2,1)}, bf16[2,2,4,6...) custom-call(s32[2]{0:T(128)} %pad_add_fusion.3.me_ref, ...), custom_call_target="tpu_custom_call" | custom-call | flops 51539607552 | bytes 54525952 | tf_op jit(solution)/shard_map/mlp/pallas_call | solution.py:821
  345.6 6.9 grad_proj.1
  352.8 4.0 grad_mixed.2
  356.8 4.3 all-to-all-start.4
  361.1 4.2 grad_mixed.3
  365.3 2.0 fusion.12
  367.3 4.0 fusion
  371.3 3.7 fusion.1
  375.6 4.3 all-to-all-start.6
  379.9 1.9 collective-permute-start.6
  383.8 62.5 %attend_back.2 = bf16[8,512,384]{2,1,0:T(8,128)(2,1)} custom-call(s32[2,64]{1,0:T(2,128)} %convert_element_type.665.listed_ref, s32[2,16]{1,0:T(2,128)} %pad_add_fusion.2.edge_ref, bf16[8,512,384]{2,1,0:T(8,128)(2,1)} %copy-done.7, bf16[8,512,128]{2,1,0:T(8,128)(2,1)} %all-to-all-done.4.grad_ref, bf16[8,512,128]{2,1,0:T(8,128)(2,1)} %get-tuple-element.52.mixed_ref, ...), custom_call_target="tpu_custom_call" | custom-call | flops 49999998976 | bytes 10000000 | tf_op jit(solution)/shard_map/attend_back/pallas_call | solution.py:659
  446.3 4.1 collective-permute-done.8
  451.6 3.9 fusion.3
  455.5 3.4 fusion.2
  458.9 3.9 all-to-all-start.5
  462.8 36.5 %attend_back.3 = bf16[8,512,384]{2,1,0:T(8,128)(2,1)} custom-call(s32[2,64]{1,0:T(2,128)} %convert_element_type.665.listed_ref, s32[2,16]{1,0:T(2,128)} %pad_add_fusion.2.edge_ref, bf16[8,512,384]{2,1,0:T(8,128)(2,1)} %all-to-all-done.2.qkv_ref, bf16[8,512,128]{2,1,0:T(8,128)(2,1)} %all-to-all-done.6.grad_ref, ...), custom_call_target="tpu_custom_call" | custom-call | flops 49999998976 | bytes 10000000 | tf_op jit(solution)/shard_map/attend_back/pallas_call | solution.py:659
  499.7 1.6 copy-done.2
  501.4 4.4 all-to-all-start.7
  505.8 1.9 collective-permute-start.25
  507.9 40.9 %collective-permute-done.25 = bf16[4,64,512]{2,1,0:T(8,128)(2,1)S(1)} collective-permute-done((bf16[4,64,512]{2,1,0:T(8,128)(2,1)S(1)}, bf16[4,64,512]{2,1,0:T(8,128)(2,1)S(1)}, u32[]{:S(2)}, u32[]{:S(2)}) %collective-permute-start.25) | collective-permute-done | bytes 262176 | tf_op jit(solution)/shard_map/ppermute | solution.py:1087
  551.1 3.8 collective-permute-done.26
  559.7 2.1 collective-permute-done.27
  561.8 1.6 fusion.31
  563.4 9.4 %first_norm_back.2 = (bf16[512,1024]{1,0:T(8,128)(2,1)}, f32[1,1024]{1,0:T(1,128)}) custom-call(bf16[8,512,384]{2,1,0:T(8,128)(2,1)} %copy-done.2, bf16[2,512,1024]{2,1,0:T(8,128)(2,1)} %tok_ref.11, f32[1024,1024]{1,0:T(8,128)} %get-tuple-element.70.grad_hidden_ref, bf16[16,2,64,1792]{3,2,1,0:T(8,128)(2,1)} %bitcast.340, f32[2,2048]{1,0:T(2,128)} %get-tuple-element.53.scales_ref), custom_call_target="tpu_custom_call" | custom-call | flops 3221225472 | bytes 17825792 | tf_op jit(solution)/shard_map/first_norm_back/pallas_call | solution.py:964
  572.9 1.7 fusion.7
  575.2 9.2 %grad_qkv.2 = (bf16[2,2,4,64,768]{4,3,2,1,0:T(8,128)(2,1)}, bf16[2,2,4,64,768]{4,3,2,1,0:T(8,128)(2,1)}) custom-call(s32[2]{0:T(128)} %pad_add_fusion.3.me_ref, bf16[512,1024]{1,0:T(8,128)(2,1)} %get-tuple-element.77.refs_0_, bf16[512,1024]{1,0:T(8,128)(2,1)} %get-tuple-element.78.refs_1_, bf16[8,512,384]{2,1,0:T(8,128)(2,1)} %copy-done.2, ...), custom_call_target="tpu_custom_call" | custom-call | flops 3221225472 | bytes 6291456 | tf_op jit(solution)/shard_map/grad_qkv/pallas_call | solution.py:1023
  584.4 9.4 %grad_qkv.3 = (bf16[2,2,4,64,768]{4,3,2,1,0:T(8,128)(2,1)}, bf16[2,2,4,64,768]{4,3,2,1,0:T(8,128)(2,1)}) custom-call(s32[2]{0:T(128)} %pad_add_fusion.3.me_ref, bf16[512,1024]{1,0:T(8,128)(2,1)} %get-tuple-element.77.refs_0_, bf16[512,1024]{1,0:T(8,128)(2,1)} %get-tuple-element.78.refs_1_, bf16[8,512,384]{2,1,0:T(8,128)(2,1)} %copy-done.2, ...), custom_call_target="tpu_custom_call" | custom-call | flops 3221225472 | bytes 6291456 | tf_op jit(solution)/shard_map/grad_qkv/pallas_call | solution.py:1023
  593.8 9.6 %first_norm_back.3 = (bf16[512,1024]{1,0:T(8,128)(2,1)}, f32[1,1024]{1,0:T(1,128)}) custom-call(bf16[8,512,384]{2,1,0:T(8,128)(2,1)} %all-to-all-done.7.refs_3_.gq_ref, bf16[2,512,1024]{2,1,0:T(8,128)(2,1)} %tok_ref.11, f32[1024,1024]{1,0:T(8,128)} %get-tuple-element.70.grad_hidden_ref, bf16[16,2,64,1792]{3,2,1,0:T(8,128)(2,1)} %bitcast.341, ...), custom_call_target="tpu_custom_call" | custom-call | flops 3221225472 | bytes 17825792 | tf_op jit(solution)/shard_map/first_norm_back/pallas_call | solution.py:964
  604.7 3.5 grad_time.1
  608.3 1.6 fusion.5
  615.2 14.7 %collective-permute-done.32 = bf16[2,64,2048]{2,1,0:T(8,128)(2,1)S(1)} collective-permute-done((bf16[2,64,2048]{2,1,0:T(8,128)(2,1)S(1)}, bf16[2,64,2048]{2,1,0:T(8,128)(2,1)S(1)}, u32[]{:S(2)}, u32[]{:S(2)}) %collective-permute-start.32) | collective-permute-done | bytes 524320 | tf_op jit(solution)/shard_map/ppermute | solution.py:1087
  632.0 2.2 fusion.16
  634.3 3.1 collective-permute-done.11
  637.4 2.2 collective-permute-start.12
  639.6 5.0 collective-permute-done.33
  644.6 2.0 fusion.14
  647.5 1.9 collective-permute-start.16
  649.3 2.2 collective-permute-done.13
  654.7 12.8 %collective-permute-done.14 = bf16[16,1024]{1,0:T(8,128)(2,1)S(1)} collective-permute-done((bf16[16,1024]{1,0:T(8,128)(2,1)S(1)}, bf16[16,1024]{1,0:T(8,128)(2,1)S(1)}, u32[]{:S(2)}, u32[]{:S(2)}) %collective-permute-start.14) | collective-permute-done | bytes 32800 | tf_op jit(solution)/shard_map/ppermute | solution.py:1087
  667.6 1.8 collective-permute-start.22
  669.6 1.6 collective-permute-start.17
  671.8 5.9 collective-permute-done.22
  677.8 2.1 collective-permute-start.23
  681.4 4.4 collective-permute-done.23
  685.8 1.9 collective-permute-start.24
  689.0 1.8 collective-permute-start.19
  691.5 3.1 collective-permute-done.19
  (174 shorter events, 41.5 us)
Async XLA Ops:
  7.2 80.6 %all-gather.3.cloned.1.call-start = ((), (), s32[]{:S(2)}) async-start(), calls=%async_computation.8 | async-start | bytes 7569408 | tf_op jit(solution)/shard_map/all_gather | solution.py:1170
  9.8 248.6 %all-gather.5.cloned.1.call-start = ((), (), s32[]{:S(2)}) async-start(), calls=%async_computation.9 | async-start | bytes 19464192 | tf_op jit(solution)/shard_map/all_gather | solution.py:1171
  97.3 4.0 copy-start.24
  97.4 6.3 copy-start.19
  97.4 48.5 %all-to-all-start = ((bf16[8,512,384]{2,1,0:T(8,128)(2,1)}), bf16[8,512,384]{2,1,0:T(8,128)(2,1)S(1)}, u32[]{:S(2)}, u32[]{:S(2)}) async-start(bf16[8,512,384]{2,1,0:T(8,128)(2,1)} %get-tuple-element.51), calls=%async_computation | async-start | bytes 6291456 | tf_op jit(solution)/shard_map/all_to_all | solution.py:1182
  101.6 53.9 %collective-permute-start.2 = (s32[2,1,31]{2,0,1:T(2,128)S(1)}, s32[2,1,31]{2,0,1:T(2,128)S(1)}, u32[]{:S(2)}, u32[]{:S(2)}) collective-permute-start(s32[2,1,31]{2,0,1:T(2,128)S(1)} %pad_add_fusion.1), channel_id=1, source_target_pairs={{0,6},{2,4},{4,2},{6,0},{1,7},{3,5},{5,3},{7,1},{8,14},{10,12},{12... | collective-permute-start | bytes 752 | tf_op jit(solution)/shard_map/ppermute | solution.py:1087
  103.3 52.3 %collective-permute-start.1 = (s32[2,1,31]{2,0,1:T(2,128)S(1)}, s32[2,1,31]{2,0,1:T(2,128)S(1)}, u32[]{:S(2)}, u32[]{:S(2)}) collective-permute-start(s32[2,1,31]{2,0,1:T(2,128)S(1)} %pad_add_fusion.1), channel_id=1, source_target_pairs={{0,4},{2,6},{4,0},{6,2},{1,5},{3,7},{5,1},{7,3},{8,12},{10,14},{12... | collective-permute-start | bytes 752 | tf_op jit(solution)/shard_map/ppermute | solution.py:1087
  103.6 51.9 %collective-permute-start = (s32[2,1,31]{2,0,1:T(2,128)S(1)}, s32[2,1,31]{2,0,1:T(2,128)S(1)}, u32[]{:S(2)}, u32[]{:S(2)}) collective-permute-start(s32[2,1,31]{2,0,1:T(2,128)S(1)} %pad_add_fusion.1), channel_id=1, source_target_pairs={{0,2},{2,0},{4,6},{6,4},{1,3},{3,1},{5,7},{7,5},{8,10},{10,8},{12,... | collective-permute-start | bytes 752 | tf_op jit(solution)/shard_map/ppermute | solution.py:1087
  147.5 57.0 %all-to-all-start.2 = ((bf16[8,512,384]{2,1,0:T(8,128)(2,1)}), bf16[8,512,384]{2,1,0:T(8,128)(2,1)}, u32[]{:S(2)}, u32[]{:S(2)}) async-start(bf16[8,512,384]{2,1,0:T(8,128)(2,1)} %get-tuple-element.55), calls=%async_computation.2 | async-start | bytes 6291456 | tf_op jit(solution)/shard_map/all_to_all | solution.py:1182
  204.4 29.8 %all-to-all-start.1 = ((bf16[8,512,128]{2,1,0:T(8,128)(2,1)}), bf16[8,512,128]{2,1,0:T(8,128)(2,1)S(1)}, u32[]{:S(2)}, u32[]{:S(2)}) async-start(bf16[8,512,128]{2,1,0:T(8,128)(2,1)} %get-tuple-element.52.mixed_ref), calls=%async_computation.1 | async-start | bytes 2097152 | tf_op jit(solution)/shard_map/all_to_all | solution.py:1189
  234.2 24.3 %copy-start.3 = (bf16[8,512,128]{2,1,0:T(8,128)(2,1)}, bf16[8,512,128]{2,1,0:T(8,128)(2,1)S(1)}, u32[]{:S(2)}) copy-start(bf16[8,512,128]{2,1,0:T(8,128)(2,1)S(1)} %all-to-all-done.1.mixed_ref.refs_0_) | copy-start | bytes 3145732
  234.2 29.1 %all-to-all-start.3 = ((bf16[8,512,128]{2,1,0:T(8,128)(2,1)}), bf16[8,512,128]{2,1,0:T(8,128)(2,1)S(1)}, u32[]{:S(2)}, u32[]{:S(2)}) async-start(bf16[8,512,128]{2,1,0:T(8,128)(2,1)} %get-tuple-element.56.mixed_ref), calls=%async_computation.3 | async-start | bytes 2097152 | tf_op jit(solution)/shard_map/all_to_all | solution.py:1189
  345.1 22.2 %collective-permute-start.3 = (bf16[2,2,4,64,2048]{4,3,2,1,0:T(8,128)(2,1)}, bf16[2,2,4,64,2048]{4,3,2,1,0:T(8,128)(2,1)}, u32[]{:S(2)}, u32[]{:S(2)}) collective-permute-start(bf16[2,2,4,64,2048]{4,3,2,1,0:T(8,128)(2,1)} %get-tuple-element.63), channel_id=1, source_target_pairs={{0,2},{2,0},{4,6},{6,4},{1,3},{3,1},{5,7},{7,5},{8,10},{10,8},{12,... | collective-permute-start | bytes 12582920 | tf_op jit(solution)/shard_map/ppermute | solution.py:1087
  345.4 25.9 %collective-permute-start.4 = (bf16[2,2,4,64,2048]{4,3,2,1,0:T(8,128)(2,1)}, bf16[2,2,4,64,2048]{4,3,2,1,0:T(8,128)(2,1)}, u32[]{:S(2)}, u32[]{:S(2)}) collective-permute-start(bf16[2,2,4,64,2048]{4,3,2,1,0:T(8,128)(2,1)} %get-tuple-element.65), channel_id=1, source_target_pairs={{0,2},{2,0},{4,6},{6,4},{1,3},{3,1},{5,7},{7,5},{8,10},{10,8},{12,... | collective-permute-start | bytes 12582920 | tf_op jit(solution)/shard_map/ppermute | solution.py:1087
  352.5 12.8 %collective-permute-start.5 = (bf16[2,2,4,64,512]{4,3,2,1,0:T(8,128)(2,1)}, bf16[2,2,4,64,512]{4,3,2,1,0:T(8,128)(2,1)}, u32[]{:S(2)}, u32[]{:S(2)}) collective-permute-start(bf16[2,2,4,64,512]{4,3,2,1,0:T(8,128)(2,1)} %get-tuple-element.67), channel_id=1, source_target_pairs={{0,2},{2,0},{4,6},{6,4},{1,3},{3,1},{5,7},{7,5},{8,10},{10,8},{12,... | collective-permute-start | bytes 3145736 | tf_op jit(solution)/shard_map/ppermute | solution.py:1087
  356.8 18.8 %all-to-all-start.4 = ((bf16[8,512,128]{2,1,0:T(8,128)(2,1)}), bf16[8,512,128]{2,1,0:T(8,128)(2,1)}, u32[]{:S(2)}, u32[]{:S(2)}) async-start(bf16[8,512,128]{2,1,0:T(8,128)(2,1)} %grad_mixed.2), calls=%async_computation.4 | async-start | bytes 2097152 | tf_op jit(solution)/shard_map/all_to_all | solution.py:1203
  361.1 4.2 copy-start.13
  361.1 6.2 copy-start.5
  367.3 4.0 copy-start.6
  375.0 4.9 copy-start.8
  375.6 83.3 %all-to-all-start.6 = ((bf16[8,512,128]{2,1,0:T(8,128)(2,1)}), bf16[8,512,128]{2,1,0:T(8,128)(2,1)}, u32[]{:S(2)}, u32[]{:S(2)}) async-start(bf16[8,512,128]{2,1,0:T(8,128)(2,1)} %grad_mixed.3), calls=%async_computation.6 | async-start | bytes 2097152 | tf_op jit(solution)/shard_map/all_to_all | solution.py:1203
  379.9 71.7 %collective-permute-start.6 = (bf16[2,4,64,2048]{3,2,1,0:T(8,128)(2,1)S(1)}, bf16[2,4,64,2048]{3,2,1,0:T(8,128)(2,1)S(1)}, u32[]{:S(2)}, u32[]{:S(2)}) collective-permute-start(bf16[2,4,64,2048]{3,2,1,0:T(8,128)(2,1)S(1)} %copy-done.8), channel_id=1, source_target_pairs={{0,4},{2,6},{4,0},{6,2},{1,5},{3,7},{5,1},{7,3},{8,12},{10,14},{12... | collective-permute-start | bytes 6291464 | tf_op jit(solution)/shard_map/ppermute | solution.py:1087
  381.8 73.7 %collective-permute-start.7 = (bf16[2,4,64,2048]{3,2,1,0:T(8,128)(2,1)}, bf16[2,4,64,2048]{3,2,1,0:T(8,128)(2,1)}, u32[]{:S(2)}, u32[]{:S(2)}) collective-permute-start(bf16[2,4,64,2048]{3,2,1,0:T(8,128)(2,1)} %fusion.1), channel_id=1, source_target_pairs={{0,1},{1,0},{2,3},{3,2},{4,5},{5,4},{6,7},{7,6},{8,9},{9,8},{10,11... | collective-permute-start | bytes 6291464 | tf_op jit(solution)/shard_map/ppermute | solution.py:1087
  383.3 67.1 %collective-permute-start.8 = (bf16[2,4,64,512]{3,2,1,0:T(8,128)(2,1)}, bf16[2,4,64,512]{3,2,1,0:T(8,128)(2,1)S(1)}, u32[]{:S(2)}, u32[]{:S(2)}) collective-permute-start(bf16[2,4,64,512]{3,2,1,0:T(8,128)(2,1)} %fusion.12), channel_id=1, source_target_pairs={{0,1},{1,0},{2,3},{3,2},{4,5},{5,4},{6,7},{7,6},{8,9},{9,8},{10,11... | collective-permute-start | bytes 1572872 | tf_op jit(solution)/shard_map/ppermute | solution.py:1087
  450.4 5.1 copy-start.18
  458.9 40.8 %all-to-all-start.5 = ((bf16[8,512,384]{2,1,0:T(8,128)(2,1)}), bf16[8,512,384]{2,1,0:T(8,128)(2,1)S(1)}, u32[]{:S(2)}, u32[]{:S(2)}) async-start(bf16[8,512,384]{2,1,0:T(8,128)(2,1)} %attend_back.2), calls=%async_computation.5 | async-start | bytes 6291456 | tf_op jit(solution)/shard_map/all_to_all | solution.py:1211
  499.3 58.1 %copy-start.23 = (f32[2,256]{1,0:T(2,128)S(1)}, f32[2,256]{1,0:T(2,128)}, u32[]{:S(2)}) copy-start(f32[2,256]{1,0:T(2,128)} %te_ref.3) | copy-start | bytes 6148
  501.4 73.8 %all-to-all-start.7 = ((bf16[8,512,384]{2,1,0:T(8,128)(2,1)}), bf16[8,512,384]{2,1,0:T(8,128)(2,1)}, u32[]{:S(2)}, u32[]{:S(2)}) async-start(bf16[8,512,384]{2,1,0:T(8,128)(2,1)} %attend_back.3), calls=%async_computation.7 | async-start | bytes 6291456 | tf_op jit(solution)/shard_map/all_to_all | solution.py:1211
  505.8 43.0 %collective-permute-start.25 = (bf16[4,64,512]{2,1,0:T(8,128)(2,1)S(1)}, bf16[4,64,512]{2,1,0:T(8,128)(2,1)S(1)}, u32[]{:S(2)}, u32[]{:S(2)}) collective-permute-start(bf16[4,64,512]{2,1,0:T(8,128)(2,1)S(1)} %fusion.17), channel_id=1, source_target_pairs={{0,4},{2,6},{4,0},{6,2},{1,5},{3,7},{5,1},{7,3},{8,12},{10,14},{12... | collective-permute-start | bytes 786440 | tf_op jit(solution)/shard_map/ppermute | solution.py:1087
  507.7 65.2 %collective-permute-start.28 = (bf16[4,64,2048]{2,1,0:T(8,128)(2,1)}, bf16[4,64,2048]{2,1,0:T(8,128)(2,1)S(1)}, u32[]{:S(2)}, u32[]{:S(2)}) collective-permute-start(bf16[4,64,2048]{2,1,0:T(8,128)(2,1)} %fusion.2), channel_id=1, source_target_pairs={{0,4},{2,6},{4,0},{6,2},{1,5},{3,7},{5,1},{7,3},{8,12},{10,14},{12... | collective-permute-start | bytes 3145736 | tf_op jit(solution)/shard_map/ppermute | solution.py:1087
  549.9 5.0 collective-permute-start.26
  555.9 5.9 collective-permute-start.27
  558.3 50.0 %collective-permute-start.31 = (bf16[4,64,2048]{2,1,0:T(8,128)(2,1)}, bf16[4,64,2048]{2,1,0:T(8,128)(2,1)S(1)}, u32[]{:S(2)}, u32[]{:S(2)}) collective-permute-start(bf16[4,64,2048]{2,1,0:T(8,128)(2,1)} %fusion.3), channel_id=1, source_target_pairs={{0,1},{1,0},{2,3},{3,2},{4,5},{5,4},{6,7},{7,6},{8,9},{9,8},{10,11... | collective-permute-start | bytes 3145736 | tf_op jit(solution)/shard_map/ppermute | solution.py:1087
  574.6 36.8 %collective-permute-start.29 = (bf16[2,64,2048]{2,1,0:T(8,128)(2,1)S(1)}, bf16[2,64,2048]{2,1,0:T(8,128)(2,1)S(1)}, u32[]{:S(2)}, u32[]{:S(2)}) collective-permute-start(bf16[2,64,2048]{2,1,0:T(8,128)(2,1)S(1)} %fusion.7), channel_id=1, source_target_pairs={{0,8},{8,0},{16,24},{24,16},{1,9},{9,1},{17,25},{25,17},{2,10},{10... | collective-permute-start | bytes 1572872 | tf_op jit(solution)/shard_map/ppermute | solution.py:1087
  593.7 9.6 %copy-start.21 = (f32[2,1024]{1,0:T(2,128)S(1)}, f32[2,1024]{1,0:T(2,128)}, u32[]{:S(2)}) copy-start(f32[2,1024]{1,0:T(2,128)} %get-tuple-element.85) | copy-start | bytes 24580
  593.7 9.6 %copy-start.22 = (f32[1,1024]{1,0:T(1,128)S(1)}, f32[1,1024]{1,0:T(1,128)}, u32[]{:S(2)}) copy-start(f32[1,1024]{1,0:T(1,128)} %get-tuple-element.83) | copy-start | bytes 12292
  593.7 14.5 %copy-start.10 = (bf16[2,4,64,2048]{3,2,1,0:T(8,128)(2,1)S(1)}, bf16[2,4,64,2048]{3,2,1,0:T(8,128)(2,1)}, u32[]{:S(2)}) copy-start(bf16[2,4,64,2048]{3,2,1,0:T(8,128)(2,1)} %copy-done.9) | copy-start | bytes 6291460
  608.1 5.4 copy-start.17
  608.2 5.4 collective-permute-start.9
  609.8 21.2 %copy-start.26 = (bf16[2,2,4,64,768]{4,3,2,1,0:T(8,128)(2,1)S(1)}, bf16[2,2,4,64,768]{4,3,2,1,0:T(8,128)(2,1)}, u32[]{:S(2)}) copy-start(bf16[2,2,4,64,768]{4,3,2,1,0:T(8,128)(2,1)} %get-tuple-element.91) | copy-start | bytes 4718596
  609.9 21.3 %copy-start.25 = (bf16[2,2,4,64,768]{4,3,2,1,0:T(8,128)(2,1)S(1)}, bf16[2,2,4,64,768]{4,3,2,1,0:T(8,128)(2,1)}, u32[]{:S(2)}) copy-start(bf16[2,2,4,64,768]{4,3,2,1,0:T(8,128)(2,1)} %get-tuple-element.89) | copy-start | bytes 4718596
  609.9 19.9 %collective-permute-start.32 = (bf16[2,64,2048]{2,1,0:T(8,128)(2,1)S(1)}, bf16[2,64,2048]{2,1,0:T(8,128)(2,1)S(1)}, u32[]{:S(2)}, u32[]{:S(2)}) collective-permute-start(bf16[2,64,2048]{2,1,0:T(8,128)(2,1)S(1)} %fusion.5), channel_id=1, source_target_pairs={{0,8},{8,0},{16,24},{24,16},{1,9},{9,1},{17,25},{25,17},{2,10},{10... | collective-permute-start | bytes 1572872 | tf_op jit(solution)/shard_map/ppermute | solution.py:1087
  612.7 19.3 %collective-permute-start.30 = (bf16[64,2048]{1,0:T(8,128)(2,1)S(1)}, bf16[64,2048]{1,0:T(8,128)(2,1)S(1)}, u32[]{:S(2)}, u32[]{:S(2)}) collective-permute-start(bf16[64,2048]{1,0:T(8,128)(2,1)S(1)} %fusion.15), channel_id=1, source_target_pairs={{0,16},{8,24},{16,0},{24,8},{1,17},{9,25},{17,1},{25,9},{2,18},{10... | collective-permute-start | bytes 786440 | tf_op jit(solution)/shard_map/ppermute | solution.py:1087
  613.6 18.1 %collective-permute-start.10 = (bf16[2,4,64,256]{3,2,1,0:T(8,128)(2,1)S(1)}, bf16[2,4,64,256]{3,2,1,0:T(8,128)(2,1)S(1)}, u32[]{:S(2)}, u32[]{:S(2)}) collective-permute-start(bf16[2,4,64,256]{3,2,1,0:T(8,128)(2,1)S(1)} %fusion.22), channel_id=1, source_target_pairs={{0,1},{1,0},{2,3},{3,2},{4,5},{5,4},{6,7},{7,6},{8,9},{9,8},{10,11... | collective-permute-start | bytes 786440 | tf_op jit(solution)/shard_map/ppermute | solution.py:1087
  631.0 13.6 %collective-permute-start.33 = (bf16[64,2048]{1,0:T(8,128)(2,1)S(1)}, bf16[64,2048]{1,0:T(8,128)(2,1)S(1)}, u32[]{:S(2)}, u32[]{:S(2)}) collective-permute-start(bf16[64,2048]{1,0:T(8,128)(2,1)S(1)} %fusion.13), channel_id=1, source_target_pairs={{0,16},{8,24},{16,0},{24,8},{1,17},{9,25},{17,1},{25,9},{2,18},{10... | collective-permute-start | bytes 786440 | tf_op jit(solution)/shard_map/ppermute | solution.py:1087
  631.1 15.7 %collective-permute-start.20 = (bf16[2,2,4,64,768]{4,3,2,1,0:T(8,128)(2,1)S(1)}, bf16[2,2,4,64,768]{4,3,2,1,0:T(8,128)(2,1)S(1)}, u32[]{:S(2)}, u32[]{:S(2)}) collective-permute-start(bf16[2,2,4,64,768]{4,3,2,1,0:T(8,128)(2,1)S(1)} %copy-done.26), channel_id=1, source_target_pairs={{0,2},{2,0},{4,6},{6,4},{1,3},{3,1},{5,7},{7,5},{8,10},{10,8},{12,... | collective-permute-start | bytes 4718600 | tf_op jit(solution)/shard_map/ppermute | solution.py:1087
  631.2 16.1 %collective-permute-start.15 = (bf16[2,2,4,64,768]{4,3,2,1,0:T(8,128)(2,1)S(1)}, bf16[2,2,4,64,768]{4,3,2,1,0:T(8,128)(2,1)S(1)}, u32[]{:S(2)}, u32[]{:S(2)}) collective-permute-start(bf16[2,2,4,64,768]{4,3,2,1,0:T(8,128)(2,1)S(1)} %copy-done.25), channel_id=1, source_target_pairs={{0,2},{2,0},{4,6},{6,4},{1,3},{3,1},{5,7},{7,5},{8,10},{10,8},{12,... | collective-permute-start | bytes 4718600 | tf_op jit(solution)/shard_map/ppermute | solution.py:1087
  631.7 15.0 %copy-start.12 = (bf16[2,2,4,64,768]{4,3,2,1,0:T(8,128)(2,1)S(1)}, bf16[2,2,4,64,768]{4,3,2,1,0:T(8,128)(2,1)}, u32[]{:S(2)}) copy-start(bf16[2,2,4,64,768]{4,3,2,1,0:T(8,128)(2,1)} %get-tuple-element.90) | copy-start | bytes 4718596
  631.8 5.6 collective-permute-start.11
  637.3 9.9 %copy-start.11 = (bf16[2,2,4,64,768]{4,3,2,1,0:T(8,128)(2,1)S(1)}, bf16[2,2,4,64,768]{4,3,2,1,0:T(8,128)(2,1)}, u32[]{:S(2)}) copy-start(bf16[2,2,4,64,768]{4,3,2,1,0:T(8,128)(2,1)} %get-tuple-element.88) | copy-start | bytes 4718596
  637.4 9.3 %collective-permute-start.12 = (bf16[2,64,256]{2,1,0:T(8,128)(2,1)S(1)}, bf16[2,64,256]{2,1,0:T(8,128)(2,1)S(1)}, u32[]{:S(2)}, u32[]{:S(2)}) collective-permute-start(bf16[2,64,256]{2,1,0:T(8,128)(2,1)S(1)} %fusion.33), channel_id=1, source_target_pairs={{0,8},{8,0},{16,24},{24,16},{1,9},{9,1},{17,25},{25,17},{2,10},{10... | collective-permute-start | bytes 196616 | tf_op jit(solution)/shard_map/ppermute | solution.py:1087
  646.7 6.5 copy-start.14
  646.7 6.5 copy-start.15
  646.7 4.9 collective-permute-start.13
  647.0 20.5 %collective-permute-start.21 = (bf16[2,4,64,768]{3,2,1,0:T(8,128)(2,1)S(1)}, bf16[2,4,64,768]{3,2,1,0:T(8,128)(2,1)S(1)}, u32[]{:S(2)}, u32[]{:S(2)}) collective-permute-start(bf16[2,4,64,768]{3,2,1,0:T(8,128)(2,1)S(1)} %fusion.9), channel_id=1, source_target_pairs={{0,4},{2,6},{4,0},{6,2},{1,5},{3,7},{5,1},{7,3},{8,12},{10,14},{12... | collective-permute-start | bytes 2359304 | tf_op jit(solution)/shard_map/ppermute | solution.py:1087
  647.5 21.9 %collective-permute-start.16 = (bf16[2,4,64,768]{3,2,1,0:T(8,128)(2,1)S(1)}, bf16[2,4,64,768]{3,2,1,0:T(8,128)(2,1)S(1)}, u32[]{:S(2)}, u32[]{:S(2)}) collective-permute-start(bf16[2,4,64,768]{3,2,1,0:T(8,128)(2,1)S(1)} %fusion.8), channel_id=1, source_target_pairs={{0,1},{1,0},{2,3},{3,2},{4,5},{5,4},{6,7},{7,6},{8,9},{9,8},{10,11... | collective-permute-start | bytes 2359304 | tf_op jit(solution)/shard_map/ppermute | solution.py:1087
  651.6 15.8 %collective-permute-start.14 = (bf16[16,1024]{1,0:T(8,128)(2,1)S(1)}, bf16[16,1024]{1,0:T(8,128)(2,1)S(1)}, u32[]{:S(2)}, u32[]{:S(2)}) collective-permute-start(bf16[16,1024]{1,0:T(8,128)(2,1)S(1)} %convert_element_type.726), channel_id=1, source_target_pairs={{0,1},{1,0},{2,3},{3,2},{4,5},{5,4},{6,7},{7,6},{8,9},{9,8},{10,11... | collective-permute-start | bytes 98312 | tf_op jit(solution)/shard_map/ppermute | solution.py:1087
  667.6 10.0 %collective-permute-start.22 = (bf16[4,64,768]{2,1,0:T(8,128)(2,1)S(1)}, bf16[4,64,768]{2,1,0:T(8,128)(2,1)S(1)}, u32[]{:S(2)}, u32[]{:S(2)}) collective-permute-start(bf16[4,64,768]{2,1,0:T(8,128)(2,1)S(1)} %fusion.10), channel_id=1, source_target_pairs={{0,1},{1,0},{2,3},{3,2},{4,5},{5,4},{6,7},{7,6},{8,9},{9,8},{10,11... | collective-permute-start | bytes 1179656 | tf_op jit(solution)/shard_map/ppermute | solution.py:1087
  669.6 10.3 %collective-permute-start.17 = (bf16[4,64,768]{2,1,0:T(8,128)(2,1)S(1)}, bf16[4,64,768]{2,1,0:T(8,128)(2,1)S(1)}, u32[]{:S(2)}, u32[]{:S(2)}) collective-permute-start(bf16[4,64,768]{2,1,0:T(8,128)(2,1)S(1)} %fusion.11), channel_id=1, source_target_pairs={{0,4},{2,6},{4,0},{6,2},{1,5},{3,7},{5,1},{7,3},{8,12},{10,14},{12... | collective-permute-start | bytes 1179656 | tf_op jit(solution)/shard_map/ppermute | solution.py:1087
  677.6 17.8 %copy-start.1 = (f32[16,2048]{1,0:T(8,128)S(1)}, f32[16,2048]{1,0:T(8,128)}, u32[]{:S(2)}) copy-start(f32[16,2048]{1,0:T(8,128)} %param.16) | copy-start | bytes 393220
  677.8 8.0 %collective-permute-start.23 = (bf16[2,64,768]{2,1,0:T(8,128)(2,1)S(1)}, bf16[2,64,768]{2,1,0:T(8,128)(2,1)S(1)}, u32[]{:S(2)}, u32[]{:S(2)}) collective-permute-start(bf16[2,64,768]{2,1,0:T(8,128)(2,1)S(1)} %fusion.19), channel_id=1, source_target_pairs={{0,8},{8,0},{16,24},{24,16},{1,9},{9,1},{17,25},{25,17},{2,10},{10... | collective-permute-start | bytes 589832 | tf_op jit(solution)/shard_map/ppermute | solution.py:1087
  680.0 9.0 %collective-permute-start.18 = (bf16[2,64,768]{2,1,0:T(8,128)(2,1)S(1)}, bf16[2,64,768]{2,1,0:T(8,128)(2,1)S(1)}, u32[]{:S(2)}, u32[]{:S(2)}) collective-permute-start(bf16[2,64,768]{2,1,0:T(8,128)(2,1)S(1)} %fusion.21), channel_id=1, source_target_pairs={{0,8},{8,0},{16,24},{24,16},{1,9},{9,1},{17,25},{25,17},{2,10},{10... | collective-permute-start | bytes 589832 | tf_op jit(solution)/shard_map/ppermute | solution.py:1087
  685.8 5.6 collective-permute-start.24
  689.0 5.6 collective-permute-start.19
  (8 other events, 20.5 us)
Sparse Core Ops, SparseCore 0:
  11.5 76.2 all-gather.2
  91.3 167.0 all-gather.4

commit v3 on v2

--- a/solution.py
+++ b/solution.py
@@ -1,4 +1,5 @@
 import functools
+import math
 
 import jax
 import jax.numpy as jnp
@@ -455,12 +456,14 @@
     )(time_embed, tokens, w_all)
 
 
-def tile_mask(segc_ref, segr_ref, key_block, query_block):
-    key_at = pl.multiple_of(key_block * BLK, BLK)
-    query_at = pl.multiple_of(query_block * BLK, BLK)
-    same = segc_ref[0, pl.ds(key_at, BLK), :] == segr_ref[0, :, pl.ds(query_at, BLK)]
-    key_pos = key_at + lax.broadcasted_iota(jnp.int32, (BLK, BLK), 0)
-    query_pos = query_at + lax.broadcasted_iota(jnp.int32, (BLK, BLK), 1)
+HALF = BLK // 2
+
+
+def tile_mask(segc_ref, segr_ref, key_at, query_at, size):
+    key_at, query_at = pl.multiple_of(key_at, size), pl.multiple_of(query_at, size)
+    same = segc_ref[0, pl.ds(key_at, size), :] == segr_ref[0, :, pl.ds(query_at, size)]
+    key_pos = key_at + lax.broadcasted_iota(jnp.int32, (size, size), 0)
+    query_pos = query_at + lax.broadcasted_iota(jnp.int32, (size, size), 1)
     return same & (key_pos <= query_pos)
 
 
@@ -470,9 +473,32 @@
     return jnp.concatenate([jnp.where(low, values, zero), jnp.where(low, zero, values)], axis=0)
 
 
-def is_full(edge_ref, row, blocks, key_block, query_block):
-    same = edge_ref[row, key_block] == edge_ref[row, blocks + query_block]
+def is_full(edge_ref, row, key_block, query_block):
+    ends = edge_ref.shape[1] // 2
+    same = edge_ref[row, 2 * key_block] == edge_ref[row, ends + 2 * query_block + 1]
     return same & (key_block < query_block)
+
+
+def over_quarters(edge_ref, row, key_block, query_block, update):
+    ends = edge_ref.shape[1] // 2
+
+    def quarter(number, carried):
+        key_half = 2 * key_block + number % 2
+        query_half = 2 * query_block + number // 2
+        shared = edge_ref[row, ends + key_half] >= edge_ref[row, query_half]
+
+        @pl.when(shared & (key_half <= query_half))
+        def _():
+            update(pl.multiple_of(key_half * HALF, HALF), pl.multiple_of(query_half * HALF, HALF))
+
+        return carried
+
+    lax.fori_loop(0, 4, quarter, 0)
+
+
+def largest(values, head):
+    part = jnp.where(low_lanes(values.shape) == (head == 0), values, 0.0)
+    return jnp.max(jnp.sum(part * part, axis=1, keepdims=True))
 
 
 def attend_kernel(
@@ -480,62 +506,97 @@
     vt_ref, qz_ref, acc_ref, stat_ref, *, row,
 ):
     blocks = qkv_ref.shape[0]
-
-    def turn(block, carried):
+    tall = HEAD_DIM + 16
+
+    def turn(block, tops):
         at = pl.multiple_of(block * BLK, BLK)
-        vt_ref[:, pl.ds(at, BLK)] = transposed(qkv_ref[block, :, 256:384])
-        return carried
-
-    lax.fori_loop(0, blocks, turn, 0)
+        turned = transposed(qkv_ref[block, :, 256:384])
+        ones = jnp.ones((16, BLK), jnp.bfloat16)
+        for head in range(2):
+            vt_ref[head * tall : head * tall + HEAD_DIM, pl.ds(at, BLK)] = turned[
+                head * HEAD_DIM : (head + 1) * HEAD_DIM
+            ]
+            vt_ref[head * tall + HEAD_DIM : (head + 1) * tall, pl.ds(at, BLK)] = ones
+        keys = qkv_ref[block, :, 128:256].astype(jnp.float32)
+        return tuple(jnp.maximum(tops[head], largest(keys, head)) for head in range(2))
+
+    key_tops = lax.fori_loop(0, blocks, turn, (0.0, 0.0))
 
     def one_query(query_block, carried):
         query = qkv_ref[query_block, :, :128].astype(jnp.float32) * HEAD_DIM ** (-0.5)
         qz_ref[...] = split_heads(query.astype(jnp.bfloat16))
-        stat_ref[0:1, :] = jnp.full((1, 2 * BLK), masked_out, jnp.float32)
-        stat_ref[1:2, :] = jnp.zeros((1, 2 * BLK), jnp.float32)
         acc_ref[...] = jnp.zeros(acc_ref.shape, jnp.float32)
-
-        def update(key_block, mask):
-            keys = qkv_ref[key_block, :, 128:256]
-            at = pl.multiple_of(key_block * BLK, BLK)
-            parts = [slice(head * BLK, (head + 1) * BLK) for head in range(2)]
-            values = [vt_ref[h * HEAD_DIM : (h + 1) * HEAD_DIM, pl.ds(at, BLK)] for h in range(2)]
-            old_max = [stat_ref[0:1, part] for part in parts]
-            old_sum = [stat_ref[1:2, part] for part in parts]
-            old_acc = [acc_ref[:, part] for part in parts]
-            scores = [dot_nt(keys, qz_ref[part, :]) for part in parts]
-            if mask is not None:
-                scores = [jnp.where(mask, one, masked_out) for one in scores]
-            new_max, new_sum, new_acc = [], [], []
-            for head in range(2):
-                top = jnp.maximum(old_max[head], jnp.max(scores[head], axis=0, keepdims=True))
-                weights = jnp.exp(scores[head] - top)
-                shrink = jnp.exp(old_max[head] - top)
-                new_max.append(top)
-                new_sum.append(old_sum[head] * shrink + jnp.sum(weights, axis=0, keepdims=True))
-                new_acc.append(old_acc[head] * shrink + dot_nn(values[head], weights.astype(jnp.bfloat16)))
-            for head, part in enumerate(parts):
-                stat_ref[0:1, part] = new_max[head]
-                stat_ref[1:2, part] = new_sum[head]
-                acc_ref[:, part] = new_acc[head]
-
-        def one_key(key_block, carried):
-            listed = listed_ref[row, query_block * blocks + key_block] != 0
-            full = is_full(edge_ref, row, blocks, key_block, query_block)
-
-            @pl.when(listed & full)
-            def _():
+        shift = []
+        for head in range(2):
+            both = jnp.full((1, BLK), largest(query, head) * key_tops[head], jnp.float32)
+            shift.append(jnp.sqrt(both) * 1.01)
+        small = (jnp.max(shift[0]) < 40.0) & (jnp.max(shift[1]) < 40.0)
+
+        def over_keys(full_update, part_update):
+            def one_key(key_block, carried):
+                listed = listed_ref[row, query_block * blocks + key_block] != 0
+                full = is_full(edge_ref, row, key_block, query_block)
+
+                @pl.when(listed & full)
+                def _():
+                    full_update(key_block)
+
+                @pl.when(listed & jnp.logical_not(full))
+                def _():
+                    part_update(key_block)
+
+                return carried
+
+            lax.fori_loop(0, query_block + 1, one_key, 0)
+
+        @pl.when(small)
+        def _():
+            def update(key_block, mask):
+                at = pl.multiple_of(key_block * BLK, BLK)
+                keys = qkv_ref[key_block, :, 128:256]
+                parts = [slice(head * BLK, (head + 1) * BLK) for head in range(2)]
+                scores = [dot_nt(keys, qz_ref[part, :]) for part in parts]
+                for head, part in enumerate(parts):
+                    one = scores[head] - shift[head]
+                    if mask is not None:
+                        one = jnp.where(mask, one, masked_out)
+                    value = vt_ref[head * tall : (head + 1) * tall, pl.ds(at, BLK)]
+                    acc_ref[:, part] += dot_nn(value, jnp.exp(one).astype(jnp.bfloat16))
+
+            def part_update(key_block):
+                update(key_block, tile_mask(segc_ref, segr_ref, key_block * BLK, query_block * BLK, BLK))
+
+            def full_update(key_block):
                 update(key_block, None)
 
-            @pl.when(listed & jnp.logical_not(full))
-            def _():
-                update(key_block, tile_mask(segc_ref, segr_ref, key_block, query_block))
-
-            return carried
-
-        lax.fori_loop(0, query_block + 1, one_key, 0)
-        total = stat_ref[1:2, :]
-        mixed = acc_ref[...] / total
+            over_keys(full_update, part_update)
+            stat_ref[0:1, :] = jnp.concatenate(shift, axis=1)
+
+        @pl.when(jnp.logical_not(small))
+        def _():
+            stat_ref[0:1, :] = jnp.full((1, 2 * BLK), masked_out, jnp.float32)
+
+            def part_update(key_at, query_at):
+                keys = qkv_ref[key_at // BLK, pl.ds(pl.multiple_of(key_at % BLK, HALF), HALF), 128:256]
+                mask = tile_mask(segc_ref, segr_ref, key_at, query_at, HALF)
+                for head in range(2):
+                    part = pl.ds(pl.multiple_of(head * BLK + query_at % BLK, HALF), HALF)
+                    scores = jnp.where(mask, dot_nt(keys, qz_ref[part, :]), masked_out)
+                    old_max = stat_ref[0:1, part]
+                    new_max = jnp.maximum(old_max, jnp.max(scores, axis=0, keepdims=True))
+                    weights = jnp.where(mask, jnp.exp(scores - new_max), 0.0)
+                    value = vt_ref[head * tall : (head + 1) * tall, pl.ds(key_at, HALF)]
+                    shrink = jnp.exp(old_max - new_max)
+                    acc_ref[:, part] = acc_ref[:, part] * shrink + dot_nn(value, weights.astype(jnp.bfloat16))
+                    stat_ref[0:1, part] = new_max
+
+            def full_update(key_block):
+                over_quarters(edge_ref, row, key_block, query_block, part_update)
+
+            over_keys(full_update, full_update)
+
+        total = acc_ref[HEAD_DIM : HEAD_DIM + 1, :]
+        mixed = acc_ref[:HEAD_DIM, :] / total
         mixed = jnp.concatenate([mixed[:, :BLK], mixed[:, BLK:]], axis=0).T
         mixed_ref[query_block] = mixed.astype(jnp.bfloat16)
         log_total = stat_ref[0:1, :] + jnp.log(total)
@@ -563,10 +624,10 @@
             ],
             out_specs=[whole((blocks, blk, pair)), whole((2, length))],
             scratch_shapes=[
-                pltpu.VMEM((pair, length), jnp.bfloat16),
+                pltpu.VMEM((pair + 32, length), jnp.bfloat16),
                 pltpu.VMEM((2 * blk, pair), jnp.bfloat16),
-                pltpu.VMEM((HEAD_DIM, 2 * blk), jnp.float32),
-                pltpu.VMEM((2, 2 * blk), jnp.float32),
+                pltpu.VMEM((HEAD_DIM + 16, 2 * blk), jnp.float32),
+                pltpu.VMEM((1, 2 * blk), jnp.float32),
             ],
         ),
         out_shape=[
@@ -607,40 +668,44 @@
         dv_ref[...] = jnp.zeros(dv_ref.shape, jnp.float32)
         key_at = pl.multiple_of(key_block * BLK, BLK)
 
-        def update(query_block, mask):
+        def accumulate(head, key_at, query_at, keys, values, query, grad, mask):
+            keys_here = pl.ds(pl.multiple_of(key_at % BLK, HALF), keys.shape[0])
+            queries_here = pl.ds(query_at, query.shape[0])
+            scores = dot_nt(keys, query)
+            probs = jnp.exp(scores - lse_ref[head : head + 1, queries_here])
+            if mask is not None:
+                probs = jnp.where(mask, probs, 0.0)
+            grad_probs = dot_nt(values, grad)
+            grad_scores = probs * (grad_probs - inner_ref[head : head + 1, queries_here])
+            probs = probs.astype(jnp.bfloat16)
+            grad_scores = grad_scores.astype(jnp.bfloat16)
+            dv_ref[keys_here, :] += dot_nn(probs, grad)
+            dk_ref[keys_here, :] += dot_nn(grad_scores, query)
+            lanes = slice(head * HEAD_DIM, (head + 1) * HEAD_DIM)
+            dq_ref[lanes, queries_here] += dot_nn(
+                kt_ref[lanes, pl.ds(key_at, keys.shape[0])], grad_scores
+            )
+
+        def full_update(query_block, mask):
             query_at = pl.multiple_of(query_block * BLK, BLK)
             keys = qkv_ref[key_block, :, 128:256]
             values = qkv_ref[key_block, :, 256:384]
             for head in range(2):
                 part = slice(head * BLK, (head + 1) * BLK)
-                query = qz_ref[query_block, part, :]
-                grad = gz_ref[query_block, part, :]
-                scores = dot_nt(keys, query)
-                probs = jnp.exp(scores - lse_ref[head : head + 1, pl.ds(query_at, BLK)])
-                if mask is not None:
-                    probs = jnp.where(mask, probs, 0.0)
-                grad_probs = dot_nt(values, grad)
-                grad_scores = probs * (grad_probs - inner_ref[head : head + 1, pl.ds(query_at, BLK)])
-                probs = probs.astype(jnp.bfloat16)
-                grad_scores = grad_scores.astype(jnp.bfloat16)
-                dv_ref[...] += dot_nn(probs, grad)
-                dk_ref[...] += dot_nn(grad_scores, query)
-                lanes = slice(head * HEAD_DIM, (head + 1) * HEAD_DIM)
-                dq_ref[lanes, pl.ds(query_at, BLK)] += dot_nn(
-                    kt_ref[lanes, pl.ds(key_at, BLK)], grad_scores
-                )
+                query, grad = qz_ref[query_block, part, :], gz_ref[query_block, part, :]
+                accumulate(head, key_at, query_at, keys, values, query, grad, mask)
 
         def one_query(query_block, carried):
             listed = listed_ref[row, query_block * blocks + key_block] != 0
-            full = is_full(edge_ref, row, blocks, key_block, query_block)
+            full = is_full(edge_ref, row, key_block, query_block)
 
             @pl.when(listed & full)
             def _():
-                update(query_block, None)
+                full_update(query_block, None)
 
             @pl.when(listed & jnp.logical_not(full))
             def _():
-                update(query_block, tile_mask(segc_ref, segr_ref, key_block, query_block))
+                full_update(query_block, tile_mask(segc_ref, segr_ref, key_block * BLK, query_block * BLK, BLK))
 
             return carried
 
@@ -730,9 +795,8 @@
 
 
 def mlp_kernel(
-    me_ref, nm0_ref, nm1_ref, cot_ref, hidden0_ref, hidden1_ref, scales_ref, up_ref, down_ref,
-    up_keep_ref, up_send_ref, down_keep_ref, down_send_ref,
-    layer_ref, grad_hidden_ref, grad_attn_ref, gscale_ref,
+    nm0_ref, nm1_ref, cot_ref, hidden0_ref, hidden1_ref, scales_ref, up_ref, down_ref,
+    grads_ref, layer_ref, grad_hidden_ref, grad_attn_ref, gscale_ref,
     nmt_ref, cott_ref, out_ref, gn_ref, act_ref, gpre_ref,
 ):
     tile = pl.program_id(0)
@@ -744,10 +808,9 @@
 
     @pl.when((tile == 0) & (phase == 0))
     def _():
-        chunks = up_ref.shape[0]
-        turned_apart(nmt_ref.at[:, :length], nm0_ref[...], me_ref[0], chunks)
-        turned_apart(nmt_ref.at[:, length:], nm1_ref[...], me_ref[0], chunks)
-        turned_apart(cott_ref, cot_ref[...], me_ref[0], chunks)
+        nmt_ref[:, :length] = transposed(nm0_ref[...])
+        nmt_ref[:, length:] = transposed(nm1_ref[...])
+        cott_ref[...] = transposed(cot_ref[...])
         out_ref[...] = jnp.zeros(out_ref.shape, jnp.float32)
         gn_ref[...] = jnp.zeros(gn_ref.shape, jnp.float32)
 
@@ -766,9 +829,7 @@
             slope = half + (0.5 * root) * pre * (1.0 - bent * bent) * (1.0 + (3.0 * cube) * square)
             gpre_ref[part, :] = (grad_act * slope).astype(jnp.bfloat16)
         grad = dot_nn(nmt_ref[...], gpre_ref[...]).astype(jnp.bfloat16)
-        shape = up_keep_ref.shape[1:]
-        up_keep_ref[0] = grad[: width // 2].reshape(shape)
-        up_send_ref[0] = grad[width // 2 :].reshape(shape)
+        grads_ref[:, 0] = grad.reshape(grads_ref.shape[0], grads_ref.shape[2], -1)
 
     @pl.when(phase == 1)
     def _():
@@ -777,9 +838,7 @@
         out_ref[...] += dot_nt(act_ref[...], down)
         gn_ref[...] += dot_nt(gpre_ref[...], up)
         grad = dot_nn(cott_ref[...], act_ref[...]).astype(jnp.bfloat16)
-        shape = (down_keep_ref.shape[0],) + down_keep_ref.shape[2:]
-        down_keep_ref[:, 0] = grad[: width // 2].reshape(shape)
-        down_send_ref[:, 0] = grad[width // 2 :].reshape(shape)
+        grads_ref[:, 0] = grad.reshape(grads_ref.shape[0], grads_ref.shape[2], -1)
 
     @pl.when((tile == pl.num_programs(0) - 1) & (phase == 1))
     def _():
@@ -800,61 +859,55 @@
             gscale_ref[row : row + 1, :] = total
 
 
-def mlp(me, normed, cotangent, hidden, scales, w_all, skip, hidden_cols):
+def mlp(normed, cotangent, hidden, scales, w_all, skip, hidden_cols):
     rows, length, width = cotangent.shape
     count = rows * length
     chunks, halves, high, columns = w_all.shape
     tile = 512
     per_half = hidden_cols // tile
     first = skip // tile
-    quarter = chunks // 4
     flat = (count, width)
-    up_at = lambda f, s, me: (0, f // per_half, 0, first + f % per_half)
-    down_at = lambda f, s, me: (0, f // per_half, 0, first + per_half + f % per_half)
-    up_out = pl.BlockSpec(
-        (1, 2, quarter, high, tile), lambda f, s, me: ((f // per_half) ^ me[1], 0, 0, 0, f % per_half)
-    )
-    down_out = pl.BlockSpec(
-        (2, 1, quarter, high, tile), lambda f, s, me: (0, (f // per_half) ^ me[1], 0, 0, f % per_half)
-    )
-    grads = jax.ShapeDtypeStruct((2, 2, quarter, high, hidden_cols), jnp.bfloat16)
+    one = (length, width)
+    block = (chunks, 1, high, tile)
     return pl.pallas_call(
         mlp_kernel,
-        grid_spec=pltpu.PrefetchScalarGridSpec(
-            num_scalar_prefetch=1,
-            grid=(halves * per_half, 2),
-            in_specs=[
-                whole((length, width)),
-                whole((length, width)),
-                whole(flat),
-                whole((length, width)),
-                whole((length, width)),
-                whole(scales.shape),
-                pl.BlockSpec((chunks, 1, high, tile), up_at),
-                pl.BlockSpec((chunks, 1, high, tile), down_at),
-            ],
-            out_specs=[up_out, up_out, down_out, down_out]
-            + [whole(flat), whole(flat), whole(flat), whole((rows, width))],
-            scratch_shapes=[
-                pltpu.VMEM((width, count), jnp.bfloat16),
-                pltpu.VMEM((width, count), jnp.bfloat16),
-                pltpu.VMEM(flat, jnp.float32),
-                pltpu.VMEM(flat, jnp.float32),
-                pltpu.VMEM((count, tile), jnp.bfloat16),
-                pltpu.VMEM((count, tile), jnp.bfloat16),
-            ],
-        ),
-        out_shape=[grads] * 4
-        + [
+        grid=(halves * per_half, 2),
+        in_specs=[
+            whole(one),
+            whole(one),
+            whole(flat),
+            whole(one),
+            whole(one),
+            whole(scales.shape),
+            pl.BlockSpec(block, lambda f, s: (0, f // per_half, 0, first + f % per_half)),
+            pl.BlockSpec(block, lambda f, s: (0, f // per_half, 0, first + per_half + f % per_half)),
+        ],
+        out_specs=[
+            pl.BlockSpec(block, lambda f, s: (0, f // per_half, 0, first + s * per_half + f % per_half)),
+            whole(flat),
+            whole(flat),
+            whole(flat),
+            whole((rows, width)),
+        ],
+        out_shape=[
+            jax.ShapeDtypeStruct(w_all.shape, jnp.bfloat16),
             jax.ShapeDtypeStruct(flat, jnp.bfloat16),
             jax.ShapeDtypeStruct(flat, jnp.float32),
             jax.ShapeDtypeStruct(flat, jnp.bfloat16),
             jax.ShapeDtypeStruct((rows, width), jnp.float32),
         ],
+        scratch_shapes=[
+            pltpu.VMEM((width, count), jnp.bfloat16),
+            pltpu.VMEM((width, count), jnp.bfloat16),
+            pltpu.VMEM(flat, jnp.float32),
+            pltpu.VMEM(flat, jnp.float32),
+            pltpu.VMEM((count, tile), jnp.bfloat16),
+            pltpu.VMEM((count, tile), jnp.bfloat16),
+        ],
         compiler_params=params(60),
         cost_estimate=cost(12 * count * width * halves * hidden_cols, 4 * w_all.size + 16 * count * width),
         name="mlp",
-    )(me, *normed, cotangent.reshape(flat), *hidden, scales, w_all, w_all)
+    )(*normed, cotangent.reshape(flat), *hidden, scales, w_all, w_all)
 
 
 def grad_mixed_kernel(grad_ref, w_ref, out_ref):
@@ -889,46 +942,34 @@
     )(grad_attn, w_all)
 
 
-def grad_proj_kernel(me_ref, grad_ref, *refs):
-    mixed_refs, (keep_ref, send_ref, turned_ref) = refs[:-3], refs[-3:]
-    width = grad_ref.shape[1]
-
+def grad_proj_kernel(grad_ref, mixed0_ref, mixed1_ref, into_ref, out_ref, turned_ref):
     @pl.when(pl.program_id(0) == 0)
     def _():
-        turned_apart(turned_ref, grad_ref[...], me_ref[0], 4 * keep_ref.shape[2])
-
-    grad = 0.0
-    for row, mixed_ref in enumerate(mixed_refs):
-        length = mixed_ref.shape[1]
-        part = slice(row * length, (row + 1) * length)
-        grad += dot_nn(turned_ref[:, part], joined(mixed_ref, 0, mixed_ref.shape[0]))
-    grad = grad.astype(jnp.bfloat16)
-    shape = keep_ref.shape[1:]
-    keep_ref[0] = grad[: width // 2].reshape(shape)
-    send_ref[0] = grad[width // 2 :].reshape(shape)
-
-
-def grad_proj_of(me, grad_attn, mixed, chunks, halves, columns):
+        turned_ref[...] = transposed(grad_ref[...])
+
+    groups, length, _ = mixed0_ref.shape
+    grad = dot_nn(turned_ref[:, :length], joined(mixed0_ref, 0, groups))
+    grad += dot_nn(turned_ref[:, length:], joined(mixed1_ref, 0, groups))
+    out_ref[:, 0] = grad.astype(jnp.bfloat16).reshape(out_ref.shape[0], out_ref.shape[2], -1)
+
+
+def grad_proj_into(grads, grad_attn, mixed, columns):
     groups, length, pair = mixed[0].shape
+    chunks, halves, high, _ = grads.shape
     count, width = grad_attn.shape
-    high = width // chunks
-    shape = (halves, 2, chunks // 4, high, columns)
-    one = pl.BlockSpec((1,) + shape[1:], lambda h, me: (h ^ me[1], 0, 0, 0, 0))
-    given = pl.BlockSpec((groups // halves, length, pair), lambda h, me: (h, 0, 0))
+    given = pl.BlockSpec((groups // halves, length, pair), lambda h: (h, 0, 0))
     return pl.pallas_call(
         grad_proj_kernel,
-        grid_spec=pltpu.PrefetchScalarGridSpec(
-            num_scalar_prefetch=1,
-            grid=(halves,),
-            in_specs=[whole(grad_attn.shape)] + [given] * len(mixed),
-            out_specs=[one, one],
-            scratch_shapes=[pltpu.VMEM((width, count), jnp.bfloat16)],
-        ),
-        out_shape=[jax.ShapeDtypeStruct(shape, jnp.bfloat16)] * 2,
+        grid=(halves,),
+        in_specs=[whole(grad_attn.shape), given, given, pl.BlockSpec(memory_space=pl.ANY)],
+        out_specs=pl.BlockSpec((chunks, 1, high, columns), lambda h: (0, h, 0, 0)),
+        out_shape=jax.ShapeDtypeStruct(grads.shape, jnp.bfloat16),
+        scratch_shapes=[pltpu.VMEM((width, count), jnp.bfloat16)],
+        input_output_aliases={3: 0},
         compiler_params=params(),
         cost_estimate=cost(2 * count * width * width, 6 * count * width),
         name="grad_proj",
-    )(me, grad_attn, *mixed)
+    )(grad_attn, *mixed, grads)
 
 
 def first_norm_kernel(gq_ref, tok_ref, grad_hidden_ref, w_ref, scales_ref, out_ref, gscale_ref, *, row, q_cols):
@@ -982,58 +1023,58 @@
     )(grad_qkv, tokens, grad_hidden, w_all, scales)
 
 
-def grad_qkv_kernel(me_ref, *refs, chunks, at_front):
-    rows = (len(refs) - 3) // 2
-    normed_refs, gq_refs, (keep_ref, send_ref, turned_ref) = refs[:rows], refs[rows:-3], refs[-3:]
-    length, width = normed_refs[0].shape
-
-    @pl.when((pl.program_id(0) == 0) & (pl.program_id(1) == 0))
+def grad_qkv_kernel(me_ref, normed_ref, gq_ref, *refs, chunks):
+    *base_refs, keep_ref, send_ref, turned_ref = refs
+    width = normed_ref.shape[1]
+
+    @pl.when(pl.program_id(0) == 0)
     def _():
-        for row in range(rows):
-            part = slice(row * length, (row + 1) * length)
-            turned_apart(turned_ref.at[:, part], normed_refs[row][...], me_ref[0], chunks)
-
-    found = 0.0
-    for row in range(rows):
-        found += dot_nn(turned_ref[:, row * length : (row + 1) * length], gq_refs[row][0])
-    found = found.astype(jnp.bfloat16)
-    if at_front:
-        shape = keep_ref.shape[1:]
-        keep_ref[0] = found[: width // 2].reshape(shape)
-        send_ref[0] = found[width // 2 :].reshape(shape)
-    else:
-        shape = (keep_ref.shape[0],) + keep_ref.shape[2:]
-        keep_ref[:, 0] = found[: width // 2].reshape(shape)
-        send_ref[:, 0] = found[width // 2 :].reshape(shape)
-
-
-def grad_qkv_of(me, normed, grad_qkv, chunks, halves, first, some, at_front):
-    length, width = normed[0].shape
-    rows = len(normed)
-    groups, _, pair = grad_qkv[0].shape
+        turned_apart(turned_ref, normed_ref[...], me_ref[0], chunks)
+
+    pair = gq_ref.shape[2]
+    for one in range(gq_ref.shape[0]):
+        found = dot_nn(turned_ref[...], gq_ref[one])
+        lanes = slice(one * pair, (one + 1) * pair)
+        if keep_ref.shape[0] == 1:
+            at = (0, slice(None), slice(None), slice(None), lanes)
+        else:
+            at = (slice(None), 0, slice(None), slice(None), lanes)
+        for number, out_ref in enumerate((keep_ref, send_ref)):
+            part = found[number * width // 2 : (number + 1) * width // 2]
+            part = part.reshape(2, chunks // 4, width // chunks, pair)
+            for base_ref in base_refs[number : number + 1]:
+                part += base_ref[at]
+            out_ref[at] = part.astype(out_ref.dtype)
+
+
+def grad_qkv_of(me, normed, grad_qkv, chunks, halves, first, some, at_front, base=()):
+    length, width = normed.shape
+    groups, _, pair = grad_qkv.shape
     pairs = groups // halves
     high = width // chunks
     quarter = chunks // 4
+    columns = some * pair
     if at_front:
-        out = pl.BlockSpec((1, 2, quarter, high, pair), lambda h, j, me: (h ^ me[1], 0, 0, 0, j))
+        out = pl.BlockSpec((1, 2, quarter, high, columns), lambda h, me: (h ^ me[1], 0, 0, 0, 0))
     else:
-        out = pl.BlockSpec((2, 1, quarter, high, pair), lambda h, j, me: (0, h ^ me[1], 0, 0, j))
-    wide = jax.ShapeDtypeStruct((halves, 2, quarter, high, some * pair), jnp.bfloat16)
-    given = pl.BlockSpec((1, length, pair), lambda h, j, me: (h * pairs + first + j, 0, 0))
+        out = pl.BlockSpec((2, 1, quarter, high, columns), lambda h, me: (0, h ^ me[1], 0, 0, 0))
+    dtype = jnp.bfloat16 if base else jnp.float32
+    wide = jax.ShapeDtypeStruct((halves, 2, quarter, high, columns), dtype)
+    given = pl.BlockSpec((some, length, pair), lambda h, me: ((h * pairs + first) // some, 0, 0))
     return pl.pallas_call(
-        functools.partial(grad_qkv_kernel, chunks=chunks, at_front=at_front),
+        functools.partial(grad_qkv_kernel, chunks=chunks),
         grid_spec=pltpu.PrefetchScalarGridSpec(
             num_scalar_prefetch=1,
-            grid=(halves, some),
-            in_specs=[whole((length, width))] * rows + [given] * rows,
+            grid=(halves,),
+            in_specs=[whole((length, width)), given] + [out] * len(base),
             out_specs=[out, out],
-            scratch_shapes=[pltpu.VMEM((width, rows * length), jnp.bfloat16)],
+            scratch_shapes=[pltpu.VMEM((width, length), jnp.bfloat16)],
         ),
         out_shape=[wide] * 2,
         compiler_params=params(),
-        cost_estimate=cost(2 * rows * length * width * halves * some * pair, 6 * rows * length * width),
+        cost_estimate=cost(2 * length * width * halves * some * pair, 6 * length * width),
         name="grad_qkv",
-    )(me, *normed, *grad_qkv)
+    )(me, normed, grad_qkv, *base)
 
 
 def grad_time_kernel(me_ref, tet_ref, gs_ref, keep_ref, send_ref, apart_ref, *, chunks, folds, t_cols):
@@ -1083,7 +1124,7 @@
 
 
 def across(values, axis, apart):
-    size = lax.axis_size(axis)
+    size = math.prod(lax.axis_size(name) for name in ([axis] if isinstance(axis, str) else axis))
     return lax.ppermute(values, axis, [(i, i ^ apart) for i in range(size)])
 
 
@@ -1094,23 +1135,33 @@
     return total
 
 
-HOPS = {"x": ("ctx", 2), "y": ("tp", 1), "near": ("fsdp", 1), "far": ("fsdp", 2)}
+HOPS = {"x": ("ctx", 2), "y": ("tp", 1)}
 
 
 class TreeSum:
-    def __init__(self, keep, send, order):
+    def __init__(self, keep, send, order, stages):
         self.parts = [keep, across(send, "ctx", 1)]
-        self.left = list(order) + ["near", "far"]
+        self.order = order
+        self.left = list(stages)
 
     def ready(self):
-        upper = slice(2, 4) if self.left[0] == "near" else 1
-        self.given = summed(self.parts, upper).astype(jnp.bfloat16)
+        name = self.left[0]
+        if name in HOPS:
+            places = {1: HOPS[name]}
+        elif name == "xy":
+            first, second = HOPS[self.order[0]], HOPS[self.order[1]]
+            both = (GROUP, 2 * lax.axis_size("tp") + 1)
+            places = {(1, 1): both, (1, 0): first, (0, 1): second}
+        else:
+            places = {3: ("fsdp", 3), 1: ("fsdp", 2), 2: ("fsdp", 1)}
+        self.hops = list(places.values())
+        self.given = [summed(self.parts, place).astype(jnp.bfloat16) for place in places]
         return self.given
 
     def go(self):
-        name = self.left.pop(0)
-        lower = slice(0, 2) if name == "near" else 0
-        self.parts = [part[lower] for part in self.parts] + [across(self.given, *HOPS[name])]
+        lower = (0, 0) if self.left.pop(0) == "xy" else 0
+        got = [across(one, *hop) for one, hop in zip(self.given, self.hops)]
+        self.parts = [part[lower] for part in self.parts] + got
 
     def finish(self):
         while self.left:
@@ -1121,10 +1172,15 @@
 
 def together(value, trees):
     given = [tree.ready() for tree in trees]
-    value, *given = lax.optimization_barrier((value, *given))
-    for tree, one in zip(trees, given):
-        tree.given = one
+    value, given = lax.optimization_barrier((value, given))
+    for tree, some in zip(trees, given):
+        tree.given = some
         tree.go()
+    return value
+
+
+def after(value, tree):
+    value, tree.parts = lax.optimization_barrier((value, tree.parts))
     return value
 
 
@@ -1172,10 +1228,13 @@
 
     row_blocks = segment_ids.shape[1] // BLK
     listed = listed_table(block_pairs, pair_counts, row_blocks, lax.axis_size("ctx"))
-    edges = jnp.concatenate([segment_ids[:, ::BLK], segment_ids[:, BLK - 1 :: BLK]], axis=1)
+    edges = jnp.concatenate([segment_ids[:, ::HALF], segment_ids[:, HALF - 1 :: HALF]], axis=1)
     segc = segment_ids[:, :, None]
     segr = segment_ids[:, None, :]
 
+    time_embed, listed, edges, segc, segr = lax.optimization_barrier(
+        (time_embed, listed, edges, segc, segr)
+    )
     qkv, normed = [], []
     for row in range(rows):
         out, one, scales = project(row, time_embed, tokens, first, k_rows, q_cols, t_cols)
@@ -1192,54 +1251,65 @@
         out, one = outward(row, mixed[row], tokens, second, scales, o_cols)
         hidden.append(out)
         normed_mlp.append(one)
-    up_keep, up_send, down_keep, down_send, layer_out, grad_hidden, grad_attn, gscale_mlp = mlp(
-        me, normed_mlp, cotangent, hidden, scales, second, o_cols, f_cols
-    )
-    down_tree = TreeSum(down_keep, down_send, "xy")
-    up_tree = TreeSum(up_keep, up_send, "yx")
-    grad_mixed = []
-    for row in range(rows):
+    grads, layer_out, grad_hidden, grad_attn, gscale_mlp = mlp(
+        normed_mlp, cotangent, hidden, scales, second, o_cols, f_cols
+    )
+    grad_mixed = {}
+    for row in reversed(range(rows)):
         out = grad_mixed_of(row, grad_attn, second, mixed[row].shape, o_cols)
-        grad_mixed.append(lax.all_to_all(out, GROUP, 0, 0, tiled=True))
-    out_keep, out_send = grad_proj_of(me, grad_attn, mixed, chunks, halves, o_cols)
-    out_tree = TreeSum(out_keep, out_send, "yx")
-    trees = [down_tree, up_tree, out_tree]
-    grad_qkv = []
-    for row in range(rows):
-        grad_mixed[row] = together(grad_mixed[row], trees)
+        grad_mixed[row] = lax.all_to_all(out, GROUP, 0, 0, tiled=True)
+    grads = grad_proj_into(grads, grad_attn, mixed, o_cols)
+    last = rows - 1
+    grad_mixed[last], grads = lax.optimization_barrier((grad_mixed[last], grads))
+    grads = lax.psum_scatter(grads.reshape(-1, grads.shape[3]), EVERY, scatter_dimension=0, tiled=True)
+    grad_qkv = {}
+    for row in reversed(range(rows)):
         out = attend_back(row, listed, edges, qkv[row], grad_mixed[row], mixed_own[row], lse[row], segc, segr)
-        grad_qkv.append(lax.all_to_all(out, GROUP, 0, 0, tiled=True))
-    grad_tokens, gscale_attn = [], []
-    for row in range(rows - 1):
-        out, one = first_norm_back(row, grad_qkv[row], tokens, grad_hidden, first, scales, q_cols)
-        grad_tokens.append(out)
-        gscale_attn.append(one)
+        grad_qkv[row] = lax.all_to_all(out, GROUP, 0, 0, tiled=True)
     some = q_cols // (6 * HEAD_DIM) // 2
-    a_keep, a_send = grad_qkv_of(me, normed, grad_qkv, chunks, halves, 0, some, True)
-    b_keep, b_send = grad_qkv_of(me, normed, grad_qkv, chunks, halves, some, some, False)
-    last, a_keep, b_keep = lax.optimization_barrier((grad_qkv[-1], a_keep, b_keep))
-    out, one = first_norm_back(rows - 1, last, tokens, grad_hidden, first, scales, q_cols)
-    grad_tokens.append(out)
-    gscale_attn.append(one)
-    grad_scales = jnp.concatenate([jnp.concatenate(gscale_attn, axis=0), gscale_mlp], axis=1)
+    held, _ = lax.optimization_barrier((grad_qkv[last], out))
+    a_base = grad_qkv_of(me, normed[last], held, chunks, halves, 0, some, True)
+    b_base = grad_qkv_of(me, normed[last], held, chunks, halves, some, some, False)
+    grad_tokens, gscale_attn = {}, {}
+    grad_tokens[last], gscale_attn[last] = first_norm_back(
+        last, held, tokens, grad_hidden, first, scales, q_cols
+    )
+    held, gscale_attn[last], a_base, b_base = lax.optimization_barrier(
+        (grad_qkv[0], gscale_attn[last], a_base, b_base)
+    )
+    a_keep, a_send = grad_qkv_of(me, normed[0], held, chunks, halves, 0, some, True, a_base)
+    a_tree = TreeSum(a_keep, a_send, "yx", ["xy", "z"])
+    held, a_keep = lax.optimization_barrier((held, a_keep))
+    b_keep, b_send = grad_qkv_of(me, normed[0], held, chunks, halves, some, some, False, b_base)
+    b_tree = TreeSum(b_keep, b_send, "xy", ["xy", "z"])
+    held, b_keep = lax.optimization_barrier((held, b_keep))
+    held = together(held, [a_tree])
+    grad_tokens[0], gscale_attn[0] = first_norm_back(0, held, tokens, grad_hidden, first, scales, q_cols)
+    gscale_attn = jnp.concatenate([gscale_attn[row] for row in range(rows)], axis=0)
+    grad_scales = jnp.concatenate([gscale_attn, gscale_mlp], axis=1)
+    grad_scales = together(grad_scales, [b_tree])
     t_keep, t_send = grad_time_of(me, time_embed, grad_scales, chunks, halves, high, k_rows, t_cols)
-    grad_time = TreeSum(t_keep, t_send, "yx").finish().reshape(folds, k_rows, t_cols)
+    t_tree = TreeSum(t_keep, t_send, "yx", ["xy", "z"])
+    t_tree.parts = together(t_tree.parts, [a_tree])
+    b_tree.parts = together(b_tree.parts, [t_tree])
+    a_sum = a_tree.finish()
+    t_tree.parts = together(t_tree.parts, [b_tree])
+    grad_time = t_tree.finish().reshape(folds, k_rows, t_cols)
     grad_time = grad_time.transpose(1, 0, 2).reshape(k_rows, t_all)
     other = across(grad_time.astype(jnp.bfloat16), "tp", 1).astype(jnp.float32)
+    b_sum = b_tree.finish()
     grad_time = jnp.concatenate(
         [jnp.where(mine == 0, grad_time, other), jnp.where(mine == 0, other, grad_time)], axis=1
     )
-    grad_w_qkv = jnp.concatenate(
-        [TreeSum(a_keep, a_send, "yx").finish(), TreeSum(b_keep, b_send, "xy").finish()], axis=1
-    )
+    f32 = jnp.float32
     return (
         layer_out.reshape(tokens.shape),
-        jnp.stack(grad_tokens),
+        jnp.stack([grad_tokens[row] for row in range(rows)]),
         grad_time,
-        grad_w_qkv,
-        out_tree.finish(),
-        up_tree.finish(),
-        down_tree.finish(),
+        jnp.concatenate([a_sum, b_sum], axis=1),
+        grads[:, :o_cols].astype(f32),
+        grads[:, o_cols : o_cols + f_cols].astype(f32),
+        grads[:, o_cols + f_cols :].astype(f32),
     )
 
 

time: 716 us -> 685 us (0.957)
  waiting for transfers between devices: 236 us -> 213 us
  other arithmetic: 43.2 us -> 21.3 us
  starting transfers between devices: 68.1 us -> 84.5 us
    ppermute x34 -> x25, waiting for transfers between devices: 104 us -> 41.2 us  [across(): return lax.ppermute(values, axis, [(i, i ^ apart) for i in range(size)])]
    all_to_all x4, waiting for transfers between devices: 1.05 us -> 35.1 us  [the longest x2 26.9 us: spread_body(): grad_qkv[row] = lax.all_to_all(out, GROUP, 0, 0, tiled=True)]
    all_to_all x2, waiting for transfers between devices: 35.6 us -> 59.3 us  [spread_body(): qkv.append(lax.all_to_all(out, GROUP, 0, 0, tiled=True))]
    ppermute x34 -> x25, starting transfers between devices: 35.2 us -> 53.5 us  [across(): return lax.ppermute(values, axis, [(i, i ^ apart) for i in range(size)])]
    convert_element_type x24 -> x8, other arithmetic: 27.1 us -> 9.03 us  [the longest x6 5.43 us: ready(): summed(self.parts, place).astype(jnp.bfloat16)]
    all_gather x1, waiting for transfers between devices: 19.6 us -> 10 us  [spread_body(): lax.all_gather(second, EVERY, axis=0, tiled=True)]
    all_gather x1, waiting for transfers between devices: 75.9 us -> 67 us  [spread_body(): lax.all_gather(first, EVERY, axis=0, tiled=True)]
    pallas_call x2, Pallas kernels: 69.7 us -> 61 us  [attend(): pl.pallas_call(functools.partial(attend_kernel, row=row), grid_spec=pltpu...]
  transfers between devices with their start and end apart: 44 -> 36, of which waited for: 20 -> 18; matrix products, arithmetic and copies ran while one was open for 7% -> 3% of each run, Pallas kernels for 35% -> 36%
where the time goes in v3:
time: 685 us; the launch traced here: 678 us
  Pallas kernels  329 us (48%)
  waiting for transfers between devices  213 us (31%)
  starting transfers between devices  84.5 us (12%)
  other arithmetic  21.3 us (3%)
  local copies, waits for them, and re-layouts  16.2 us (2%)
  between operations  14.4 us (2%)
    pallas_call x2, Pallas kernels, attend_back(): pl.pallas_call(functools.partial(attend_back_kernel, row=row), grid_spec=...  99.6 us
    pallas_call x1, Pallas kernels, mlp(): pl.pallas_call(mlp_kernel, grid=(halves * per_half, 2), in_specs=[whole(o...  73.5 us
    all_gather x1, waiting for transfers between devices, spread_body(): lax.all_gather(first, EVERY, axis=0, tiled=True)  67 us
    pallas_call x2, Pallas kernels, attend(): pl.pallas_call(functools.partial(attend_kernel, row=row), grid_spec=pltpu...  61 us
    all_to_all x2, waiting for transfers between devices, spread_body(): qkv.append(lax.all_to_all(out, GROUP, 0, 0, tiled=True))  59.3 us
    ppermute x25, starting transfers between devices, across(): return lax.ppermute(values, axis, [(i, i ^ apart) for i in range(size)])  53.5 us
    ppermute x25, waiting for transfers between devices, across(): return lax.ppermute(values, axis, [(i, i ^ apart) for i in range(size)])  41.2 us
    pallas_call x4, Pallas kernels, grad_qkv_of(): pl.pallas_call(functools.partial(grad_qkv_kernel, chunks=chunks), grid_sp...  28.5 us
  transfers between devices with their start and end apart: 36, of which 18 were waited for; matrix products, arithmetic and copies ran while one was open for 3% of the time, Pallas kernels for 36%

profile of v3, /device:TPU:0, one launch (start us, length us, event | category | flops | bytes accessed | tf_op | source)
XLA Modules:
  0.0 678.5 jit_solution(17080678784307729913)
XLA Ops:
  13.2 2.4 collective-permute-start.2
  20.8 67.0 %all-gather.3.cloned.1.call-done = bf16[2048,1792]{1,0:T(8,128)(2,1)} async-done(((bf16[64,1792]{1,0:T(8,128)(2,1)}), bf16[2048,1792]{1,0:T(8,128)(2,1)}) %all-gather.3.cloned.1.call-update) | async-done | bytes 7340048 | tf_op jit(solution)/shard_map/all_gather | solution.py:1226
  87.8 9.5 %project.3 = (bf16[8,512,384]{2,1,0:T(8,128)(2,1)}, bf16[512,1024]{1,0:T(8,128)(2,1)}, f32[2,2048]{1,0:T(2,128)}) custom-call(f32[2,256]{1,0:T(2,128)} %te_ref.1, bf16[2,512,1024]{2,1,0:T(8,128)(2,1)} %tok_ref.11, bf16[16,2,64,1792]{3,2,1,0:T(8,128)(2,1)} %bitcast.158), custom_call_target="tpu_custom_call" | custom-call | flops 3221225472 | bytes 12582912 | tf_op jit(solution)/shard_map/project/pallas_call | solution.py:435
  97.3 3.7 all-to-all-start.2
  101.0 9.5 %project.2 = (bf16[8,512,384]{2,1,0:T(8,128)(2,1)}, bf16[512,1024]{1,0:T(8,128)(2,1)}, f32[2,2048]{1,0:T(2,128)}) custom-call(f32[2,256]{1,0:T(2,128)} %te_ref.1, bf16[2,512,1024]{2,1,0:T(8,128)(2,1)} %tok_ref.11, bf16[16,2,64,1792]{3,2,1,0:T(8,128)(2,1)} %bitcast.159), custom_call_target="tpu_custom_call" | custom-call | flops 3221225472 | bytes 12582912 | tf_op jit(solution)/shard_map/project/pallas_call | solution.py:435
  110.5 35.0 %all-to-all-done.2.qkv_ref = bf16[8,512,384]{2,1,0:T(8,128)(2,1)S(1)} async-done(((bf16[8,512,384]{2,1,0:T(8,128)(2,1)}), bf16[8,512,384]{2,1,0:T(8,128)(2,1)S(1)}, u32[]{:S(2)}, u32[]{:S(2)}) %all-to-all-start.2) | async-done | bytes 3145760 | tf_op jit(solution)/shard_map/all_to_all | solution.py:1241
  145.5 1.7 copy-done.7
  147.2 3.6 all-to-all-start
  150.8 2.7 copy.47.segc_ref
  153.6 25.4 %attend.3 = (bf16[8,512,128]{2,1,0:T(8,128)(2,1)}, f32[2,4096]{1,0:T(2,128)}) custom-call(s32[2,64]{1,0:T(2,128)} %convert_element_type.480.listed_ref, s32[2,32]{1,0:T(2,128)} %pad_add_fusion.2.edge_ref, bf16[8,512,384]{2,1,0:T(8,128)(2,1)} %copy-done.7, s32[2,4096,1]{2,1,0:T(8,128)} %copy.47.segc_ref, s32[2,1,4096]{2,1,0:T(1,128)} %broadcast_in_dim.19.segr_ref), custom_call_target="tpu_custom_call" | custom-call | flops 20000000000 | bytes 6000000 | tf_op jit(solution)/shard_map/attend/pallas_call | solution.py:615
  179.0 24.3 %all-to-all-done.qkv_ref = bf16[8,512,384]{2,1,0:T(8,128)(2,1)S(1)} async-done(((bf16[8,512,384]{2,1,0:T(8,128)(2,1)}), bf16[8,512,384]{2,1,0:T(8,128)(2,1)S(1)}, u32[]{:S(2)}, u32[]{:S(2)}) %all-to-all-start) | async-done | bytes 3145760 | tf_op jit(solution)/shard_map/all_to_all | solution.py:1241
  203.3 1.6 copy-done.6
  204.9 3.6 all-to-all-start.3
  208.5 35.6 %attend.2 = (bf16[8,512,128]{2,1,0:T(8,128)(2,1)}, f32[2,4096]{1,0:T(2,128)}) custom-call(s32[2,64]{1,0:T(2,128)} %convert_element_type.480.listed_ref, s32[2,32]{1,0:T(2,128)} %pad_add_fusion.2.edge_ref, bf16[8,512,384]{2,1,0:T(8,128)(2,1)} %copy-done.6, s32[2,4096,1]{2,1,0:T(8,128)} %copy.47.segc_ref, s32[2,1,4096]{2,1,0:T(1,128)} %broadcast_in_dim.19.segr_ref), custom_call_target="tpu_custom_call" | custom-call | flops 20000000000 | bytes 6000000 | tf_op jit(solution)/shard_map/attend/pallas_call | solution.py:615
  244.0 4.4 all-to-all-start.1
  248.4 10.0 %all-gather.5.cloned.1.call-done = bf16[2048,4608]{1,0:T(8,128)(2,1)} async-done(((bf16[64,4608]{1,0:T(8,128)(2,1)}), bf16[2048,4608]{1,0:T(8,128)(2,1)}) %all-gather.5.cloned.1.call-update) | async-done | bytes 18874384 | tf_op jit(solution)/shard_map/all_gather | solution.py:1227
  258.4 4.9 outward.3
  264.3 4.8 outward.2
  269.1 73.5 %mlp.1 = (bf16[16,2,64,4608]{3,2,1,0:T(8,128)(2,1)}, bf16[1024,1024]{1,0:T(8,128)(2,1)}, f32[1024,1024]{1,0:T(8,128)}, bf16[1024,1024]{1,0:T(8,128)(2,1)}, f32[2,1024]{1,0:T(2,128)}) custom-call(bf16[512,1024]{1,0:T(8,128)(2,1)} %get-tuple-element.92.nm0_ref, bf16[512,1024]{1,0:T(8,128)(2,1)} %get-tuple-element.95.nm1_ref, bf16[1024,1024]{1,0:T(8,128)(2,1)} %bitcast.174, ...), custom_call_target="tpu_custom_call" | custom-call | flops 51539607552 | bytes 54525952 | tf_op jit(solution)/shard_map/mlp/pallas_call | solution.py:872
  342.6 4.4 grad_mixed.3
  347.1 3.6 all-to-all-start.6
  350.7 6.2 grad_proj.1
  356.9 8.2 %all-to-all-done.6.grad_ref = bf16[8,512,128]{2,1,0:T(8,128)(2,1)S(1)} async-done(((bf16[8,512,128]{2,1,0:T(8,128)(2,1)}), bf16[8,512,128]{2,1,0:T(8,128)(2,1)S(1)}, u32[]{:S(2)}, u32[]{:S(2)}) %all-to-all-start.6) | async-done | bytes 1048608 | tf_op jit(solution)/shard_map/all_to_all | solution.py:1260
  366.1 4.0 grad_mixed.2
  370.1 3.6 all-to-all-start.4
  373.7 37.1 %attend_back.3 = bf16[8,512,384]{2,1,0:T(8,128)(2,1)} custom-call(s32[2,64]{1,0:T(2,128)} %convert_element_type.480.listed_ref, s32[2,32]{1,0:T(2,128)} %pad_add_fusion.2.edge_ref, bf16[8,512,384]{2,1,0:T(8,128)(2,1)} %copy-done.7, bf16[8,512,128]{2,1,0:T(8,128)(2,1)} %copy-done.10, bf16[8,512,128]{2,1,0:T(8,128)(2,1)} %get-tuple-element.94.mixed_ref, ...), custom_call_target="tpu_custom_call" | custom-call | flops 49999998976 | bytes 10000000 | tf_op jit(solution)/shard_map/attend_back/pallas_call | solution.py:724
  411.8 4.1 all-to-all-start.7
  415.9 62.4 %attend_back.2 = bf16[8,512,384]{2,1,0:T(8,128)(2,1)} custom-call(s32[2,64]{1,0:T(2,128)} %convert_element_type.480.listed_ref, s32[2,32]{1,0:T(2,128)} %pad_add_fusion.2.edge_ref, bf16[8,512,384]{2,1,0:T(8,128)(2,1)} %copy-done.6, bf16[8,512,128]{2,1,0:T(8,128)(2,1)} %copy-done.11, bf16[8,512,128]{2,1,0:T(8,128)(2,1)} %get-tuple-element.90.mixed_ref, ...), custom_call_target="tpu_custom_call" | custom-call | flops 49999998976 | bytes 10000000 | tf_op jit(solution)/shard_map/attend_back/pallas_call | solution.py:724
  478.3 1.6 copy-done.3
  479.9 4.4 all-to-all-start.5
  485.0 6.9 %grad_qkv.5 = (f32[2,2,4,64,768]{4,3,2,1,0:T(8,128)}, f32[2,2,4,64,768]{4,3,2,1,0:T(8,128)}) custom-call(s32[2]{0:T(128)} %pad_add_fusion.3.me_ref, bf16[512,1024]{1,0:T(8,128)(2,1)} %get-tuple-element.107.normed_ref, bf16[8,512,384]{2,1,0:T(8,128)(2,1)} %copy-done.3), custom_call_target="tpu_custom_call" | custom-call | flops 1610612736 | bytes 3145728 | tf_op jit(solution)/shard_map/grad_qkv/pallas_call | solution.py:1064
  491.9 6.6 grad_qkv.4
  498.5 9.9 %first_norm_back.2 = (bf16[512,1024]{1,0:T(8,128)(2,1)}, f32[1,1024]{1,0:T(1,128)}) custom-call(bf16[8,512,384]{2,1,0:T(8,128)(2,1)} %copy-done.3, bf16[2,512,1024]{2,1,0:T(8,128)(2,1)} %tok_ref.11, f32[1024,1024]{1,0:T(8,128)} %get-tuple-element.105.grad_hidden_ref, bf16[16,2,64,1792]{3,2,1,0:T(8,128)(2,1)} %bitcast.160, f32[2,2048]{1,0:T(2,128)} %get-tuple-element.91.scales_ref), custom_call_target="tpu_custom_call" | custom-call | flops 3221225472 | bytes 17825792 | tf_op jit(solution)/shard_map/first_norm_back/pallas_call | solution.py:1005
  508.4 26.9 %all-to-all-done.5.gq_ref = bf16[8,512,384]{2,1,0:T(8,128)(2,1)S(1)} async-done(((bf16[8,512,384]{2,1,0:T(8,128)(2,1)}), bf16[8,512,384]{2,1,0:T(8,128)(2,1)S(1)}, u32[]{:S(2)}, u32[]{:S(2)}) %all-to-all-start.5) | async-done | bytes 3145760 | tf_op jit(solution)/shard_map/all_to_all | solution.py:1268
  535.4 1.6 copy-done.2
  537.0 7.6 %grad_qkv.6 = (bf16[2,2,4,64,768]{4,3,2,1,0:T(8,128)(2,1)}, bf16[2,2,4,64,768]{4,3,2,1,0:T(8,128)(2,1)}) custom-call(s32[2]{0:T(128)} %pad_add_fusion.3.me_ref, bf16[512,1024]{1,0:T(8,128)(2,1)} %get-tuple-element.113.normed_ref, bf16[8,512,384]{2,1,0:T(8,128)(2,1)} %copy-done.2, f32[2,2,4,64,768]{4,3,2,1,0:T(8,128)} %get-tuple-element.114.refs_0_, ...), custom_call_target="tpu_custom_call" | custom-call | flops 1610612736 | bytes 3145728 | tf_op jit(solution)/shard_map/grad_qkv/pallas_call | solution.py:1064
  544.6 7.4 %grad_qkv.7 = (bf16[2,2,4,64,768]{4,3,2,1,0:T(8,128)(2,1)}, bf16[2,2,4,64,768]{4,3,2,1,0:T(8,128)(2,1)}) custom-call(s32[2]{0:T(128)} %pad_add_fusion.3.me_ref, bf16[512,1024]{1,0:T(8,128)(2,1)} %get-tuple-element.113.normed_ref, bf16[8,512,384]{2,1,0:T(8,128)(2,1)} %copy-done.2, f32[2,2,4,64,768]{4,3,2,1,0:T(8,128)} %get-tuple-element.118.refs_0_, ...), custom_call_target="tpu_custom_call" | custom-call | flops 1610612736 | bytes 3145728 | tf_op jit(solution)/shard_map/grad_qkv/pallas_call | solution.py:1064
  553.4 2.4 fusion.2
  555.8 10.1 %first_norm_back.3 = (bf16[512,1024]{1,0:T(8,128)(2,1)}, f32[1,1024]{1,0:T(1,128)}) custom-call(bf16[8,512,384]{2,1,0:T(8,128)(2,1)} %copy-done.2, bf16[2,512,1024]{2,1,0:T(8,128)(2,1)} %tok_ref.11, f32[1024,1024]{1,0:T(8,128)} %get-tuple-element.105.grad_hidden_ref, bf16[16,2,64,1792]{3,2,1,0:T(8,128)(2,1)} %bitcast.161, f32[2,2048]{1,0:T(2,128)} %get-tuple-element.91.scales_ref), custom_call_target="tpu_custom_call" | custom-call | flops 3221225472 | bytes 17825792 | tf_op jit(solution)/shard_map/first_norm_back/pallas_call | solution.py:1005
  568.3 3.8 collective-permute-start.6
  573.0 1.5 collective-permute-start.8
  574.4 3.4 grad_time.1
  578.0 1.5 collective-permute-start.9
  579.6 2.9 collective-permute-done.6
  582.4 2.3 collective-permute-start.10
  584.7 7.1 %collective-permute-done.7 = bf16[4,64,768]{2,1,0:T(8,128)(2,1)} collective-permute-done((bf16[4,64,768]{2,1,0:T(8,128)(2,1)}, bf16[4,64,768]{2,1,0:T(8,128)(2,1)}, u32[]{:S(2)}, u32[]{:S(2)}) %collective-permute-start.7) | collective-permute-done | bytes 393248 | tf_op jit(solution)/shard_map/ppermute | solution.py:1128
  591.8 10.0 %collective-permute-start.11 = (bf16[4,64,768]{2,1,0:T(8,128)(2,1)}, bf16[4,64,768]{2,1,0:T(8,128)(2,1)S(1)}, u32[]{:S(2)}, u32[]{:S(2)}) collective-permute-start(bf16[4,64,768]{2,1,0:T(8,128)(2,1)} %get-tuple-element.140), channel_id=1, source_target_pairs={{0,1},{1,0},{2,3},{3,2},{4,5},{5,4},{6,7},{7,6},{8,9},{9,8},{10,11... | collective-permute-start | bytes 1179656 | tf_op jit(solution)/shard_map/ppermute | solution.py:1128
  601.8 1.5 fusion.9
  603.5 5.5 collective-permute-done.10
  609.1 6.6 collective-permute-done.11
  615.7 2.4 collective-permute-start.12
  619.7 2.2 collective-permute-done.12
  621.9 2.4 collective-permute-done.13
  625.3 15.5 %collective-permute-start.17 = (bf16[64,256]{1,0:T(8,128)(2,1)S(1)}, bf16[64,256]{1,0:T(8,128)(2,1)S(1)}, u32[]{:S(2)}, u32[]{:S(2)}) collective-permute-start(bf16[64,256]{1,0:T(8,128)(2,1)S(1)} %get-tuple-element.177), channel_id=1, source_target_pairs={{0,8},{8,0},{16,24},{24,16},{1,9},{9,1},{17,25},{25,17},{2,10},{10... | collective-permute-start | bytes 98312 | tf_op jit(solution)/shard_map/ppermute | solution.py:1128
  640.9 1.5 pad_maximum_fusion
  642.4 2.4 collective-permute-start.19
  646.8 4.2 collective-permute-done.16
  651.1 1.6 collective-permute-start.18
  652.7 3.8 collective-permute-done.20
  658.2 3.9 collective-permute-start.24
  662.8 2.5 collective-permute-done.22
  665.3 1.9 collective-permute-done.23
  668.1 1.5 slice_convert_fusion.2
  669.6 2.1 slice_convert_fusion
  (133 shorter events, 27.6 us)
Async XLA Ops:
  7.2 0.9 copy-start
  7.2 4.7 copy-start.14
  7.2 80.6 %all-gather.3.cloned.1.call-start = ((), (), s32[]{:S(2)}) async-start(), calls=%async_computation.9 | async-start | bytes 7569408 | tf_op jit(solution)/shard_map/all_gather | solution.py:1226
  9.1 3.7 copy-start.21
  9.1 3.8 copy-start.20
  9.1 7.2 %copy-start.16 = (s32[2,4096]{1,0:T(2,128)S(1)}, s32[2,4096]{1,0:T(2,128)}, u32[]{:S(2)}) copy-start(s32[2,4096]{1,0:T(2,128)} %param.13) | copy-start | bytes 98308
  9.9 248.5 %all-gather.5.cloned.1.call-start = ((), (), s32[]{:S(2)}) async-start(), calls=%async_computation.10 | async-start | bytes 19464192 | tf_op jit(solution)/shard_map/all_gather | solution.py:1227
  13.2 4.8 collective-permute-start.2
  15.6 3.6 collective-permute-start.1
  16.3 2.9 collective-permute-start
  97.3 48.2 %all-to-all-start.2 = ((bf16[8,512,384]{2,1,0:T(8,128)(2,1)}), bf16[8,512,384]{2,1,0:T(8,128)(2,1)S(1)}, u32[]{:S(2)}, u32[]{:S(2)}) async-start(bf16[8,512,384]{2,1,0:T(8,128)(2,1)} %get-tuple-element.93), calls=%async_computation.2 | async-start | bytes 6291456 | tf_op jit(solution)/shard_map/all_to_all | solution.py:1241
  145.5 1.7 copy-start.7
  147.2 56.1 %all-to-all-start = ((bf16[8,512,384]{2,1,0:T(8,128)(2,1)}), bf16[8,512,384]{2,1,0:T(8,128)(2,1)S(1)}, u32[]{:S(2)}, u32[]{:S(2)}) async-start(bf16[8,512,384]{2,1,0:T(8,128)(2,1)} %get-tuple-element.87), calls=%async_computation | async-start | bytes 6291456 | tf_op jit(solution)/shard_map/all_to_all | solution.py:1241
  203.3 1.6 copy-start.6
  204.9 39.1 %all-to-all-start.3 = ((bf16[8,512,128]{2,1,0:T(8,128)(2,1)}), bf16[8,512,128]{2,1,0:T(8,128)(2,1)S(1)}, u32[]{:S(2)}, u32[]{:S(2)}) async-start(bf16[8,512,128]{2,1,0:T(8,128)(2,1)} %get-tuple-element.94.mixed_ref), calls=%async_computation.3 | async-start | bytes 2097152 | tf_op jit(solution)/shard_map/all_to_all | solution.py:1248
  244.0 14.4 %copy-start.4 = (bf16[8,512,128]{2,1,0:T(8,128)(2,1)}, bf16[8,512,128]{2,1,0:T(8,128)(2,1)S(1)}, u32[]{:S(2)}) copy-start(bf16[8,512,128]{2,1,0:T(8,128)(2,1)S(1)} %all-to-all-done.3.mixed_ref.mixed1_ref) | copy-start | bytes 3145732
  244.0 19.3 %all-to-all-start.1 = ((bf16[8,512,128]{2,1,0:T(8,128)(2,1)}), bf16[8,512,128]{2,1,0:T(8,128)(2,1)S(1)}, u32[]{:S(2)}, u32[]{:S(2)}) async-start(bf16[8,512,128]{2,1,0:T(8,128)(2,1)} %get-tuple-element.90.mixed_ref), calls=%async_computation.1 | async-start | bytes 2097152 | tf_op jit(solution)/shard_map/all_to_all | solution.py:1248
  263.3 1.0 copy-start.5
  347.1 18.0 %all-to-all-start.6 = ((bf16[8,512,128]{2,1,0:T(8,128)(2,1)}), bf16[8,512,128]{2,1,0:T(8,128)(2,1)S(1)}, u32[]{:S(2)}, u32[]{:S(2)}) async-start(bf16[8,512,128]{2,1,0:T(8,128)(2,1)} %grad_mixed.3), calls=%async_computation.6 | async-start | bytes 2097152 | tf_op jit(solution)/shard_map/all_to_all | solution.py:1260
  350.6 317.5 %reduce-scatter.2.cloned.1.call-start = ((), (), s32[]{:S(2)}) async-start(), calls=%async_computation.11 | async-start | bytes 19464192 | tf_op jit(solution)/shard_map/reduce_scatter | solution.py:1264
  365.1 1.0 copy-start.10
  370.1 40.7 %all-to-all-start.4 = ((bf16[8,512,128]{2,1,0:T(8,128)(2,1)}), bf16[8,512,128]{2,1,0:T(8,128)(2,1)S(1)}, u32[]{:S(2)}, u32[]{:S(2)}) async-start(bf16[8,512,128]{2,1,0:T(8,128)(2,1)} %grad_mixed.2), calls=%async_computation.4 | async-start | bytes 2097152 | tf_op jit(solution)/shard_map/all_to_all | solution.py:1260
  410.8 1.0 copy-start.11
  411.8 66.5 %all-to-all-start.7 = ((bf16[8,512,384]{2,1,0:T(8,128)(2,1)}), bf16[8,512,384]{2,1,0:T(8,128)(2,1)S(1)}, u32[]{:S(2)}, u32[]{:S(2)}) async-start(bf16[8,512,384]{2,1,0:T(8,128)(2,1)} %attend_back.3), calls=%async_computation.7 | async-start | bytes 6291456 | tf_op jit(solution)/shard_map/all_to_all | solution.py:1268
  478.3 1.6 copy-start.3
  479.9 55.4 %all-to-all-start.5 = ((bf16[8,512,384]{2,1,0:T(8,128)(2,1)}), bf16[8,512,384]{2,1,0:T(8,128)(2,1)S(1)}, u32[]{:S(2)}, u32[]{:S(2)}) async-start(bf16[8,512,384]{2,1,0:T(8,128)(2,1)} %attend_back.2), calls=%async_computation.5 | async-start | bytes 6291456 | tf_op jit(solution)/shard_map/all_to_all | solution.py:1268
  535.4 1.6 copy-start.2
  544.6 8.8 %collective-permute-start.3 = (bf16[2,2,4,64,768]{4,3,2,1,0:T(8,128)(2,1)}, bf16[2,2,4,64,768]{4,3,2,1,0:T(8,128)(2,1)}, u32[]{:S(2)}, u32[]{:S(2)}) collective-permute-start(bf16[2,2,4,64,768]{4,3,2,1,0:T(8,128)(2,1)} %get-tuple-element.122), channel_id=1, source_target_pairs={{0,2},{2,0},{4,6},{6,4},{1,3},{3,1},{5,7},{7,5},{8,10},{10,8},{12,... | collective-permute-start | bytes 4718600 | tf_op jit(solution)/shard_map/ppermute | solution.py:1128
  544.6 8.0 %copy-start.19 = (f32[2,256]{1,0:T(2,128)S(1)}, f32[2,256]{1,0:T(2,128)}, u32[]{:S(2)}) copy-start(f32[2,256]{1,0:T(2,128)} %te_ref.1) | copy-start | bytes 6148
  544.6 8.7 %copy-start.9 = (bf16[2,2,4,64,768]{4,3,2,1,0:T(8,128)(2,1)S(1)}, bf16[2,2,4,64,768]{4,3,2,1,0:T(8,128)(2,1)}, u32[]{:S(2)}) copy-start(bf16[2,2,4,64,768]{4,3,2,1,0:T(8,128)(2,1)} %get-tuple-element.116) | copy-start | bytes 4718596
  552.1 15.1 %collective-permute-start.4 = (bf16[2,2,4,64,768]{4,3,2,1,0:T(8,128)(2,1)}, bf16[2,2,4,64,768]{4,3,2,1,0:T(8,128)(2,1)S(1)}, u32[]{:S(2)}, u32[]{:S(2)}) collective-permute-start(bf16[2,2,4,64,768]{4,3,2,1,0:T(8,128)(2,1)} %get-tuple-element.129), channel_id=1, source_target_pairs={{0,2},{2,0},{4,6},{6,4},{1,3},{3,1},{5,7},{7,5},{8,10},{10,8},{12,... | collective-permute-start | bytes 4718600 | tf_op jit(solution)/shard_map/ppermute | solution.py:1128
  555.8 10.1 %copy-start.17 = (f32[2,1024]{1,0:T(2,128)S(1)}, f32[2,1024]{1,0:T(2,128)}, u32[]{:S(2)}) copy-start(f32[2,1024]{1,0:T(2,128)} %get-tuple-element.128) | copy-start | bytes 24580
  555.8 10.1 %copy-start.18 = (f32[1,1024]{1,0:T(1,128)S(1)}, f32[1,1024]{1,0:T(1,128)}, u32[]{:S(2)}) copy-start(f32[1,1024]{1,0:T(1,128)} %get-tuple-element.127) | copy-start | bytes 12292
  555.8 11.4 %copy-start.8 = (bf16[2,2,4,64,768]{4,3,2,1,0:T(8,128)(2,1)S(1)}, bf16[2,2,4,64,768]{4,3,2,1,0:T(8,128)(2,1)}, u32[]{:S(2)}) copy-start(bf16[2,2,4,64,768]{4,3,2,1,0:T(8,128)(2,1)} %get-tuple-element.120) | copy-start | bytes 4718596
  568.3 14.1 %collective-permute-start.6 = (bf16[4,64,768]{2,1,0:T(8,128)(2,1)}, bf16[4,64,768]{2,1,0:T(8,128)(2,1)}, u32[]{:S(2)}, u32[]{:S(2)}) collective-permute-start(bf16[4,64,768]{2,1,0:T(8,128)(2,1)} %get-tuple-element.133), channel_id=1, source_target_pairs={{0,5},{1,4},{2,7},{3,6},{4,1},{5,0},{6,3},{7,2},{8,13},{9,12},{10,... | collective-permute-start | bytes 1179656 | tf_op jit(solution)/shard_map/ppermute | solution.py:1128
  572.1 19.7 %collective-permute-start.7 = (bf16[4,64,768]{2,1,0:T(8,128)(2,1)}, bf16[4,64,768]{2,1,0:T(8,128)(2,1)}, u32[]{:S(2)}, u32[]{:S(2)}) collective-permute-start(bf16[4,64,768]{2,1,0:T(8,128)(2,1)} %get-tuple-element.134), channel_id=1, source_target_pairs={{0,1},{1,0},{2,3},{3,2},{4,5},{5,4},{6,7},{7,6},{8,9},{9,8},{10,11... | collective-permute-start | bytes 1179656 | tf_op jit(solution)/shard_map/ppermute | solution.py:1128
  573.0 28.9 %collective-permute-start.8 = (bf16[4,64,768]{2,1,0:T(8,128)(2,1)}, bf16[4,64,768]{2,1,0:T(8,128)(2,1)}, u32[]{:S(2)}, u32[]{:S(2)}) collective-permute-start(bf16[4,64,768]{2,1,0:T(8,128)(2,1)} %get-tuple-element.135), channel_id=1, source_target_pairs={{0,4},{2,6},{4,0},{6,2},{1,5},{3,7},{5,1},{7,3},{8,12},{10,14},{12... | collective-permute-start | bytes 1179656 | tf_op jit(solution)/shard_map/ppermute | solution.py:1128
  577.9 25.5 %copy-start.15 = (bf16[2,2,4,64,256]{4,3,2,1,0:T(8,128)(2,1)S(1)}, bf16[2,2,4,64,256]{4,3,2,1,0:T(8,128)(2,1)}, u32[]{:S(2)}) copy-start(bf16[2,2,4,64,256]{4,3,2,1,0:T(8,128)(2,1)} %get-tuple-element.136) | copy-start | bytes 1572868
  577.9 25.5 %collective-permute-start.5 = (bf16[2,2,4,64,256]{4,3,2,1,0:T(8,128)(2,1)}, bf16[2,2,4,64,256]{4,3,2,1,0:T(8,128)(2,1)S(1)}, u32[]{:S(2)}, u32[]{:S(2)}) collective-permute-start(bf16[2,2,4,64,256]{4,3,2,1,0:T(8,128)(2,1)} %get-tuple-element.132), channel_id=1, source_target_pairs={{0,2},{2,0},{4,6},{6,4},{1,3},{3,1},{5,7},{7,5},{8,10},{10,8},{12,... | collective-permute-start | bytes 1572872 | tf_op jit(solution)/shard_map/ppermute | solution.py:1128
  578.0 25.5 %collective-permute-start.9 = (bf16[4,64,768]{2,1,0:T(8,128)(2,1)}, bf16[4,64,768]{2,1,0:T(8,128)(2,1)S(1)}, u32[]{:S(2)}, u32[]{:S(2)}) collective-permute-start(bf16[4,64,768]{2,1,0:T(8,128)(2,1)} %get-tuple-element.138), channel_id=1, source_target_pairs={{0,5},{1,4},{2,7},{3,6},{4,1},{5,0},{6,3},{7,2},{8,13},{9,12},{10,... | collective-permute-start | bytes 1179656 | tf_op jit(solution)/shard_map/ppermute | solution.py:1128
  582.4 26.7 %collective-permute-start.10 = (bf16[4,64,768]{2,1,0:T(8,128)(2,1)}, bf16[4,64,768]{2,1,0:T(8,128)(2,1)S(1)}, u32[]{:S(2)}, u32[]{:S(2)}) collective-permute-start(bf16[4,64,768]{2,1,0:T(8,128)(2,1)} %get-tuple-element.139), channel_id=1, source_target_pairs={{0,4},{2,6},{4,0},{6,2},{1,5},{3,7},{5,1},{7,3},{8,12},{10,14},{12... | collective-permute-start | bytes 1179656 | tf_op jit(solution)/shard_map/ppermute | solution.py:1128
  591.8 23.8 %collective-permute-start.11 = (bf16[4,64,768]{2,1,0:T(8,128)(2,1)}, bf16[4,64,768]{2,1,0:T(8,128)(2,1)S(1)}, u32[]{:S(2)}, u32[]{:S(2)}) collective-permute-start(bf16[4,64,768]{2,1,0:T(8,128)(2,1)} %get-tuple-element.140), channel_id=1, source_target_pairs={{0,1},{1,0},{2,3},{3,2},{4,5},{5,4},{6,7},{7,6},{8,9},{9,8},{10,11... | collective-permute-start | bytes 1179656 | tf_op jit(solution)/shard_map/ppermute | solution.py:1128
  603.4 37.5 %copy-start.12 = (bf16[512,1024]{1,0:T(8,128)(2,1)S(1)}, bf16[512,1024]{1,0:T(8,128)(2,1)}, u32[]{:S(2)}) copy-start(bf16[512,1024]{1,0:T(8,128)(2,1)} %get-tuple-element.125) | copy-start | bytes 3145732
  603.4 37.5 %copy-start.13 = (bf16[512,1024]{1,0:T(8,128)(2,1)S(1)}, bf16[512,1024]{1,0:T(8,128)(2,1)}, u32[]{:S(2)}) copy-start(bf16[512,1024]{1,0:T(8,128)(2,1)} %get-tuple-element.124) | copy-start | bytes 3145732
  615.7 6.3 collective-permute-start.12
  618.0 6.3 collective-permute-start.13
  619.2 6.0 collective-permute-start.14
  625.3 20.1 %collective-permute-start.15 = (bf16[64,256]{1,0:T(8,128)(2,1)S(1)}, bf16[64,256]{1,0:T(8,128)(2,1)S(1)}, u32[]{:S(2)}, u32[]{:S(2)}) collective-permute-start(bf16[64,256]{1,0:T(8,128)(2,1)S(1)} %get-tuple-element.176), channel_id=1, source_target_pairs={{0,24},{8,16},{16,8},{24,0},{1,25},{9,17},{17,9},{25,1},{2,26},{10... | collective-permute-start | bytes 98312 | tf_op jit(solution)/shard_map/ppermute | solution.py:1128
  625.3 21.4 %collective-permute-start.17 = (bf16[64,256]{1,0:T(8,128)(2,1)S(1)}, bf16[64,256]{1,0:T(8,128)(2,1)S(1)}, u32[]{:S(2)}, u32[]{:S(2)}) collective-permute-start(bf16[64,256]{1,0:T(8,128)(2,1)S(1)} %get-tuple-element.177), channel_id=1, source_target_pairs={{0,8},{8,0},{16,24},{24,16},{1,9},{9,1},{17,25},{25,17},{2,10},{10... | collective-permute-start | bytes 98312 | tf_op jit(solution)/shard_map/ppermute | solution.py:1128
  640.9 10.2 %collective-permute-start.16 = (bf16[64,256]{1,0:T(8,128)(2,1)S(1)}, bf16[64,256]{1,0:T(8,128)(2,1)S(1)}, u32[]{:S(2)}, u32[]{:S(2)}) collective-permute-start(bf16[64,256]{1,0:T(8,128)(2,1)S(1)} %get-tuple-element.178), channel_id=1, source_target_pairs={{0,16},{8,24},{16,0},{24,8},{1,17},{9,25},{17,1},{25,9},{2,18},{10... | collective-permute-start | bytes 98312 | tf_op jit(solution)/shard_map/ppermute | solution.py:1128
  642.4 10.3 %collective-permute-start.19 = (bf16[64,768]{1,0:T(8,128)(2,1)S(1)}, bf16[64,768]{1,0:T(8,128)(2,1)S(1)}, u32[]{:S(2)}, u32[]{:S(2)}) collective-permute-start(bf16[64,768]{1,0:T(8,128)(2,1)S(1)} %get-tuple-element.154), channel_id=1, source_target_pairs={{0,24},{8,16},{16,8},{24,0},{1,25},{9,17},{17,9},{25,1},{2,26},{10... | collective-permute-start | bytes 294920 | tf_op jit(solution)/shard_map/ppermute | solution.py:1128
  644.7 11.7 %collective-permute-start.20 = (bf16[64,768]{1,0:T(8,128)(2,1)S(1)}, bf16[64,768]{1,0:T(8,128)(2,1)S(1)}, u32[]{:S(2)}, u32[]{:S(2)}) collective-permute-start(bf16[64,768]{1,0:T(8,128)(2,1)S(1)} %get-tuple-element.155), channel_id=1, source_target_pairs={{0,16},{8,24},{16,0},{24,8},{1,17},{9,25},{17,1},{25,9},{2,18},{10... | collective-permute-start | bytes 294920 | tf_op jit(solution)/shard_map/ppermute | solution.py:1128
  645.4 11.1 %collective-permute-start.21 = (bf16[64,768]{1,0:T(8,128)(2,1)S(1)}, bf16[64,768]{1,0:T(8,128)(2,1)S(1)}, u32[]{:S(2)}, u32[]{:S(2)}) collective-permute-start(bf16[64,768]{1,0:T(8,128)(2,1)S(1)} %get-tuple-element.156), channel_id=1, source_target_pairs={{0,8},{8,0},{16,24},{24,16},{1,9},{9,1},{17,25},{25,17},{2,10},{10... | collective-permute-start | bytes 294920 | tf_op jit(solution)/shard_map/ppermute | solution.py:1128
  651.1 11.0 %collective-permute-start.18 = (bf16[16,1024]{1,0:T(8,128)(2,1)S(1)}, bf16[16,1024]{1,0:T(8,128)(2,1)S(1)}, u32[]{:S(2)}, u32[]{:S(2)}) collective-permute-start(bf16[16,1024]{1,0:T(8,128)(2,1)S(1)} %convert_element_type.595), channel_id=1, source_target_pairs={{0,1},{1,0},{2,3},{3,2},{4,5},{5,4},{6,7},{7,6},{8,9},{9,8},{10,11... | collective-permute-start | bytes 98312 | tf_op jit(solution)/shard_map/ppermute | solution.py:1128
  656.5 15.2 %copy-start.1 = (f32[16,2048]{1,0:T(8,128)S(1)}, f32[16,2048]{1,0:T(8,128)}, u32[]{:S(2)}) copy-start(f32[16,2048]{1,0:T(8,128)} %param.16) | copy-start | bytes 393220
  657.7 7.6 %collective-permute-start.22 = (bf16[64,768]{1,0:T(8,128)(2,1)S(1)}, bf16[64,768]{1,0:T(8,128)(2,1)S(1)}, u32[]{:S(2)}, u32[]{:S(2)}) collective-permute-start(bf16[64,768]{1,0:T(8,128)(2,1)S(1)} %get-tuple-element.157), channel_id=1, source_target_pairs={{0,24},{8,16},{16,8},{24,0},{1,25},{9,17},{17,9},{25,1},{2,26},{10... | collective-permute-start | bytes 294920 | tf_op jit(solution)/shard_map/ppermute | solution.py:1128
  658.0 9.2 %collective-permute-start.23 = (bf16[64,768]{1,0:T(8,128)(2,1)S(1)}, bf16[64,768]{1,0:T(8,128)(2,1)S(1)}, u32[]{:S(2)}, u32[]{:S(2)}) collective-permute-start(bf16[64,768]{1,0:T(8,128)(2,1)S(1)} %get-tuple-element.158), channel_id=1, source_target_pairs={{0,16},{8,24},{16,0},{24,8},{1,17},{9,25},{17,1},{25,9},{2,18},{10... | collective-permute-start | bytes 294920 | tf_op jit(solution)/shard_map/ppermute | solution.py:1128
  658.2 9.0 %collective-permute-start.24 = (bf16[64,768]{1,0:T(8,128)(2,1)S(1)}, bf16[64,768]{1,0:T(8,128)(2,1)S(1)}, u32[]{:S(2)}, u32[]{:S(2)}) collective-permute-start(bf16[64,768]{1,0:T(8,128)(2,1)S(1)} %get-tuple-element.159), channel_id=1, source_target_pairs={{0,8},{8,0},{16,24},{24,16},{1,9},{9,1},{17,25},{25,17},{2,10},{10... | collective-permute-start | bytes 294920 | tf_op jit(solution)/shard_map/ppermute | solution.py:1128
Sparse Core Ops, SparseCore 0:
  11.5 76.2 all-gather.2
  91.3 167.0 all-gather.4
  365.2 289.6 reduce-scatter.1

commit v4 on v3

--- a/solution.py
+++ b/solution.py
@@ -1,11 +1,11 @@
 import functools
-import math
 
 import jax
 import jax.numpy as jnp
 from jax import lax
 from jax.experimental import pallas as pl
 from jax.experimental.pallas import tpu as pltpu
+from jax.sharding import Mesh
 from jax.sharding import PartitionSpec as P
 
 HEAD_DIM = 64
@@ -352,18 +352,20 @@
     return values.astype(jnp.float32).T.astype(values.dtype)
 
 
-def turned_apart(into_ref, values, chunk_at, chunks):
-    turned = values.astype(jnp.float32).T.astype(values.dtype)
+def turned_apart(into_ref, values, core, chunks):
+    turned = transposed(values)
     high = turned.shape[0] // chunks
-    bits = chunks.bit_length() - 1
     for chunk in range(chunks):
-        apart = chunk ^ chunk_at
-        place = 0
-        for bit in range(bits):
-            place += ((apart >> bit) & 1) << (bits - 1 - bit)
-        into_ref[pl.ds(pl.multiple_of(place * high, high), high), :] = turned[
-            chunk * high : (chunk + 1) * high, :
-        ]
+        inner = (chunk // 2 % 2) * (chunks // 4) + chunk // 4
+        at = ((chunk % 2) ^ core) * (chunks // 2) + inner
+        into_ref[pl.ds(pl.multiple_of(at * high, high), high), :] = turned[chunk * high : (chunk + 1) * high]
+
+
+def put_apart(keep_ref, send_ref, grad):
+    middle = grad.shape[0] // 2
+    shape = (keep_ref.shape[0],) + keep_ref.shape[2:]
+    keep_ref[:, 0] = grad[:middle].reshape(shape)
+    send_ref[:, 0] = grad[middle:].reshape(shape)
 
 
 def low_lanes(shape):
@@ -388,72 +390,64 @@
     )
 
 
-def time_scales(te_ref, w_ref, scales_ref, k_rows, q_cols, t_cols):
-    exact = te_ref[...]
-    high = exact.astype(jnp.bfloat16)
-    rest = exact - high.astype(jnp.float32)
-    middle = rest.astype(jnp.bfloat16)
-    last = (rest - middle.astype(jnp.float32)).astype(jnp.bfloat16)
-    chunks, halves, tall, _ = w_ref.shape
-    folds = tall // k_rows
-    for half in range(halves):
-        for fold in range(folds):
-            weights = w_ref[:, half, fold * k_rows : (fold + 1) * k_rows, q_cols : q_cols + t_cols]
-            weights = weights.reshape(chunks * k_rows, t_cols)
-            total = dot_nn(last, weights) + dot_nn(middle, weights) + dot_nn(high, weights)
-            at = (half * folds + fold) * t_cols
-            scales_ref[:, at : at + t_cols] = 1.0 + total
-
-
-def project_kernel(te_ref, tok_ref, w_ref, qkv_ref, normed_ref, scales_ref, *, row, k_rows, q_cols, t_cols):
-    @pl.when(pl.program_id(0) == 0)
+def project_kernel(place_ref, scales_ref, *refs, row, pieces, parts):
+    weight_refs, token_refs = refs[:parts], refs[parts : parts + pieces]
+    qkv_ref, normed_ref, held_ref, w_ref, sem_ref = refs[parts + pieces :]
+    step = pl.program_id(0)
+
+    def fetch(piece):
+        source = token_refs[piece]
+        source = source.at[row] if len(source.shape) == 3 else source
+        return pltpu.make_async_copy(source, held_ref.at[piece], sem_ref.at[piece])
+
+    @pl.when(step == 0)
     def _():
-        time_scales(te_ref, w_ref, scales_ref, k_rows, q_cols, t_cols)
-
-    halves = w_ref.shape[1]
-    values = tok_ref[0].astype(jnp.float32)
+        for piece in range(pieces):
+            fetch(piece).start()
+        tall = weight_refs[0].shape[0]
+        for apart, weight_ref in enumerate(weight_refs):
+            at = pl.multiple_of((apart ^ place_ref[1]) * tall, tall)
+            w_ref[pl.ds(at, tall), :] = pair_apart(weight_ref[...].astype(jnp.float32)).astype(jnp.bfloat16)
+    pltpu.make_async_copy(held_ref.at[step], held_ref.at[step], sem_ref.at[step]).wait()
+    values = held_ref[step].astype(jnp.float32)
     width = values.shape[1]
     hat, _ = normalize(values)
     normed = (hat * scales_ref[row : row + 1, :width]).astype(jnp.bfloat16)
-    normed_ref[...] = normed
-    pair = 6 * HEAD_DIM
-    for half in range(halves):
-        weights = w_ref[:, half, :, :q_cols].reshape(width, q_cols)
-        out = dot_nn(normed, weights)
-        for group in range(q_cols // pair):
-            qkv_ref[half * (q_cols // pair) + group] = pair_apart(
-                out[:, group * pair : (group + 1) * pair]
-            ).astype(jnp.bfloat16)
-
-
-def project(row, time_embed, tokens, w_all, k_rows, q_cols, t_cols):
-    rows, length, width = tokens.shape
-    chunks, halves = w_all.shape[:2]
-    pair = 6 * HEAD_DIM
-    groups = halves * q_cols // pair
-    tile = 256
+    normed_ref[0] = normed
+    qkv_ref[0] = dot_nn(normed, w_ref[...]).astype(jnp.bfloat16)
+
+
+def project(row, place, scales, weights, tokens, others):
+    _, length, width = tokens.shape
+    pair = weights[0].shape[1]
+    pieces = 1 + len(others)
+    anywhere = pl.BlockSpec(memory_space=pl.ANY)
     return pl.pallas_call(
-        functools.partial(project_kernel, row=row, k_rows=k_rows, q_cols=q_cols, t_cols=t_cols),
-        grid=(length // tile,),
-        in_specs=[
-            whole(time_embed.shape),
-            pl.BlockSpec((1, tile, width), lambda i: (row, i, 0)),
-            whole(w_all.shape),
-        ],
-        out_specs=[
-            pl.BlockSpec((groups, tile, pair), lambda i: (0, i, 0)),
-            pl.BlockSpec((tile, width), lambda i: (i, 0)),
-            whole((rows, 2 * width)),
-        ],
+        functools.partial(project_kernel, row=row, pieces=pieces, parts=len(weights)),
+        grid_spec=pltpu.PrefetchScalarGridSpec(
+            num_scalar_prefetch=1,
+            grid=(pieces,),
+            in_specs=[whole(scales.shape)]
+            + [whole(one.shape) for one in weights]
+            + [anywhere] * pieces,
+            out_specs=[
+                pl.BlockSpec((1, length, pair), lambda i, place: (i ^ place[0], 0, 0)),
+                pl.BlockSpec((1, length, width), lambda i, place: (i ^ place[0], 0, 0)),
+            ],
+            scratch_shapes=[
+                pltpu.VMEM((pieces, length, width), jnp.bfloat16),
+                pltpu.VMEM((width, pair), jnp.bfloat16),
+                pltpu.SemaphoreType.DMA((pieces,)),
+            ],
+        ),
         out_shape=[
-            jax.ShapeDtypeStruct((groups, length, pair), jnp.bfloat16),
-            jax.ShapeDtypeStruct((length, width), jnp.bfloat16),
-            jax.ShapeDtypeStruct((rows, 2 * width), jnp.float32),
+            jax.ShapeDtypeStruct((pieces, length, pair), jnp.bfloat16),
+            jax.ShapeDtypeStruct((pieces, length, width), jnp.bfloat16),
         ],
         compiler_params=params(),
-        cost_estimate=cost(2 * length * width * halves * q_cols, 2 * w_all.size + 10 * length * width),
+        cost_estimate=cost(2 * pieces * length * width * pair, 5 * pieces * length * width),
         name="project",
-    )(time_embed, tokens, w_all)
+    )(place, scales, *weights, tokens, *others)
 
 
 HALF = BLK // 2
@@ -752,17 +746,16 @@
     )(listed, edges, qkv, grad, mixed, lse, segc, segr)
 
 
-def joined(ref, first, count):
-    return jnp.concatenate([ref[first + i] for i in range(count)], axis=1)
+def joined(ref, half, halves):
+    return jnp.concatenate([ref[i * halves + half] for i in range(ref.shape[0] // halves)], axis=1)
 
 
 def outward_kernel(mixed_ref, tok_ref, w_ref, scales_ref, hidden_ref, normed_ref, *, row):
     halves = w_ref.shape[1]
-    per_half = mixed_ref.shape[0] // halves
     hidden = tok_ref[0].astype(jnp.float32)
     width = hidden.shape[1]
     for half in range(halves):
-        hidden += dot_nt(joined(mixed_ref, half * per_half, per_half), w_ref[:, half].reshape(width, -1))
+        hidden += dot_nt(joined(mixed_ref, half, halves), w_ref[:, half].reshape(width, -1))
     hidden_ref[...] = hidden
     hat, _ = normalize(hidden)
     normed_ref[...] = (hat * scales_ref[row : row + 1, width:]).astype(jnp.bfloat16)
@@ -795,8 +788,8 @@
 
 
 def mlp_kernel(
-    nm0_ref, nm1_ref, cot_ref, hidden0_ref, hidden1_ref, scales_ref, up_ref, down_ref,
-    grads_ref, layer_ref, grad_hidden_ref, grad_attn_ref, gscale_ref,
+    place_ref, nm0_ref, nm1_ref, cot_ref, hidden0_ref, hidden1_ref, scales_ref, up_ref, down_ref,
+    keep_ref, send_ref, layer_ref, grad_hidden_ref, grad_attn_ref, gscale_ref,
     nmt_ref, cott_ref, out_ref, gn_ref, act_ref, gpre_ref,
 ):
     tile = pl.program_id(0)
@@ -808,9 +801,10 @@
 
     @pl.when((tile == 0) & (phase == 0))
     def _():
-        nmt_ref[:, :length] = transposed(nm0_ref[...])
-        nmt_ref[:, length:] = transposed(nm1_ref[...])
-        cott_ref[...] = transposed(cot_ref[...])
+        chunks = up_ref.shape[0]
+        turned_apart(nmt_ref.at[:, :length], nm0_ref[...], place_ref[2], chunks)
+        turned_apart(nmt_ref.at[:, length:], nm1_ref[...], place_ref[2], chunks)
+        turned_apart(cott_ref, cot_ref[...], place_ref[2], chunks)
         out_ref[...] = jnp.zeros(out_ref.shape, jnp.float32)
         gn_ref[...] = jnp.zeros(gn_ref.shape, jnp.float32)
 
@@ -828,8 +822,7 @@
             act_ref[part, :] = (pre * half).astype(jnp.bfloat16)
             slope = half + (0.5 * root) * pre * (1.0 - bent * bent) * (1.0 + (3.0 * cube) * square)
             gpre_ref[part, :] = (grad_act * slope).astype(jnp.bfloat16)
-        grad = dot_nn(nmt_ref[...], gpre_ref[...]).astype(jnp.bfloat16)
-        grads_ref[:, 0] = grad.reshape(grads_ref.shape[0], grads_ref.shape[2], -1)
+        put_apart(keep_ref, send_ref, dot_nn(nmt_ref[...], gpre_ref[...]).astype(jnp.bfloat16))
 
     @pl.when(phase == 1)
     def _():
@@ -837,8 +830,7 @@
         down = down_ref[:, 0].reshape(width, -1)
         out_ref[...] += dot_nt(act_ref[...], down)
         gn_ref[...] += dot_nt(gpre_ref[...], up)
-        grad = dot_nn(cott_ref[...], act_ref[...]).astype(jnp.bfloat16)
-        grads_ref[:, 0] = grad.reshape(grads_ref.shape[0], grads_ref.shape[2], -1)
+        put_apart(keep_ref, send_ref, dot_nn(cott_ref[...], act_ref[...]).astype(jnp.bfloat16))
 
     @pl.when((tile == pl.num_programs(0) - 1) & (phase == 1))
     def _():
@@ -859,55 +851,65 @@
             gscale_ref[row : row + 1, :] = total
 
 
-def mlp(normed, cotangent, hidden, scales, w_all, skip, hidden_cols):
+def mlp(place, normed, cotangent, hidden, scales, w_all, room):
     rows, length, width = cotangent.shape
     count = rows * length
     chunks, halves, high, columns = w_all.shape
     tile = 512
+    hidden_cols = columns // 2
     per_half = hidden_cols // tile
-    first = skip // tile
     flat = (count, width)
     one = (length, width)
     block = (chunks, 1, high, tile)
+    apart = pl.BlockSpec(
+        (2, 1, chunks // 4, high, tile),
+        lambda f, s, at: (0, f // per_half, 0, 0, room // tile + s * per_half + f % per_half),
+    )
+    grads = jax.ShapeDtypeStruct((2, halves, chunks // 4, high, room + columns), jnp.bfloat16)
     return pl.pallas_call(
         mlp_kernel,
-        grid=(halves * per_half, 2),
-        in_specs=[
-            whole(one),
-            whole(one),
-            whole(flat),
-            whole(one),
-            whole(one),
-            whole(scales.shape),
-            pl.BlockSpec(block, lambda f, s: (0, f // per_half, 0, first + f % per_half)),
-            pl.BlockSpec(block, lambda f, s: (0, f // per_half, 0, first + per_half + f % per_half)),
-        ],
-        out_specs=[
-            pl.BlockSpec(block, lambda f, s: (0, f // per_half, 0, first + s * per_half + f % per_half)),
-            whole(flat),
-            whole(flat),
-            whole(flat),
-            whole((rows, width)),
-        ],
+        grid_spec=pltpu.PrefetchScalarGridSpec(
+            num_scalar_prefetch=1,
+            grid=(halves * per_half, 2),
+            in_specs=[
+                whole(one),
+                whole(one),
+                whole(flat),
+                whole(one),
+                whole(one),
+                whole(scales.shape),
+                pl.BlockSpec(block, lambda f, s, at: (0, f // per_half, 0, f % per_half)),
+                pl.BlockSpec(block, lambda f, s, at: (0, f // per_half, 0, per_half + f % per_half)),
+            ],
+            out_specs=[
+                apart,
+                apart,
+                whole(flat),
+                whole(flat),
+                whole(flat),
+                whole((rows, width)),
+            ],
+            scratch_shapes=[
+                pltpu.VMEM((width, count), jnp.bfloat16),
+                pltpu.VMEM((width, count), jnp.bfloat16),
+                pltpu.VMEM(flat, jnp.float32),
+                pltpu.VMEM(flat, jnp.float32),
+                pltpu.VMEM((count, tile), jnp.bfloat16),
+                pltpu.VMEM((count, tile), jnp.bfloat16),
+            ],
+        ),
         out_shape=[
-            jax.ShapeDtypeStruct(w_all.shape, jnp.bfloat16),
+            grads,
+            grads,
             jax.ShapeDtypeStruct(flat, jnp.bfloat16),
             jax.ShapeDtypeStruct(flat, jnp.float32),
             jax.ShapeDtypeStruct(flat, jnp.bfloat16),
             jax.ShapeDtypeStruct((rows, width), jnp.float32),
         ],
-        scratch_shapes=[
-            pltpu.VMEM((width, count), jnp.bfloat16),
-            pltpu.VMEM((width, count), jnp.bfloat16),
-            pltpu.VMEM(flat, jnp.float32),
-            pltpu.VMEM(flat, jnp.float32),
-            pltpu.VMEM((count, tile), jnp.bfloat16),
-            pltpu.VMEM((count, tile), jnp.bfloat16),
-        ],
         compiler_params=params(60),
         cost_estimate=cost(12 * count * width * halves * hidden_cols, 4 * w_all.size + 16 * count * width),
         name="mlp",
-    )(*normed, cotangent.reshape(flat), *hidden, scales, w_all, w_all)
+    )(place, *normed, cotangent.reshape(flat), *hidden, scales, w_all, w_all)
 
 
 def grad_mixed_kernel(grad_ref, w_ref, out_ref):
@@ -918,7 +920,7 @@
     for half in range(halves):
         out = dot_nn(grad, w_ref[:, half].reshape(grad.shape[1], -1)).astype(jnp.bfloat16)
         for group in range(per_half):
-            out_ref[half * per_half + group] = out[:, group * pair : (group + 1) * pair]
+            out_ref[group * halves + half] = out[:, group * pair : (group + 1) * pair]
 
 
 def grad_mixed_of(row, grad_attn, w_all, mixed_shape, columns):
@@ -942,46 +944,54 @@
     )(grad_attn, w_all)
 
 
-def grad_proj_kernel(grad_ref, mixed0_ref, mixed1_ref, into_ref, out_ref, turned_ref):
-    @pl.when(pl.program_id(0) == 0)
+def grad_proj_kernel(place_ref, grad_ref, mixed0_ref, mixed1_ref, _k, _s, keep_ref, send_ref, turned_ref):
+    half = pl.program_id(0)
+    halves = pl.num_programs(0)
+
+    @pl.when(half == 0)
     def _():
-        turned_ref[...] = transposed(grad_ref[...])
-
-    groups, length, _ = mixed0_ref.shape
-    grad = dot_nn(turned_ref[:, :length], joined(mixed0_ref, 0, groups))
-    grad += dot_nn(turned_ref[:, length:], joined(mixed1_ref, 0, groups))
-    out_ref[:, 0] = grad.astype(jnp.bfloat16).reshape(out_ref.shape[0], out_ref.shape[2], -1)
-
-
-def grad_proj_into(grads, grad_attn, mixed, columns):
-    groups, length, pair = mixed[0].shape
-    chunks, halves, high, _ = grads.shape
+        turned_apart(turned_ref, grad_ref[...], place_ref[2], 4 * keep_ref.shape[2])
+
+    groups, length, pair = mixed0_ref.shape
+    count = keep_ref.shape[4] // pair
+    grad = 0.0
+    for row, mixed_ref in enumerate((mixed0_ref, mixed1_ref)):
+        mixed = jnp.concatenate([mixed_ref[i * halves + half] for i in range(count)], axis=1)
+        grad += dot_nn(turned_ref[:, row * length : (row + 1) * length], mixed)
+    put_apart(keep_ref, send_ref, grad.astype(jnp.bfloat16))
+
+
+def grad_proj_into(place, keep, send, grad_attn, mixed, columns):
     count, width = grad_attn.shape
-    given = pl.BlockSpec((groups // halves, length, pair), lambda h: (h, 0, 0))
+    given = whole(mixed[0].shape)
+    anywhere = pl.BlockSpec(memory_space=pl.ANY)
+    out = pl.BlockSpec((2, 1) + keep.shape[2:4] + (columns,), lambda h, at: (0, h, 0, 0, 0))
     return pl.pallas_call(
         grad_proj_kernel,
-        grid=(halves,),
-        in_specs=[whole(grad_attn.shape), given, given, pl.BlockSpec(memory_space=pl.ANY)],
-        out_specs=pl.BlockSpec((chunks, 1, high, columns), lambda h: (0, h, 0, 0)),
-        out_shape=jax.ShapeDtypeStruct(grads.shape, jnp.bfloat16),
-        scratch_shapes=[pltpu.VMEM((width, count), jnp.bfloat16)],
-        input_output_aliases={3: 0},
+        grid_spec=pltpu.PrefetchScalarGridSpec(
+            num_scalar_prefetch=1,
+            grid=(keep.shape[1],),
+            in_specs=[whole(grad_attn.shape), given, given, anywhere, anywhere],
+            out_specs=[out, out],
+            scratch_shapes=[pltpu.VMEM((width, count), jnp.bfloat16)],
+        ),
+        out_shape=[jax.ShapeDtypeStruct(keep.shape, jnp.bfloat16)] * 2,
+        input_output_aliases={4: 0, 5: 1},
         compiler_params=params(),
         cost_estimate=cost(2 * count * width * width, 6 * count * width),
         name="grad_proj",
-    )(grad_attn, *mixed, grads)
+    )(place, grad_attn, *mixed, keep, send)
 
 
 def first_norm_kernel(gq_ref, tok_ref, grad_hidden_ref, w_ref, scales_ref, out_ref, gscale_ref, *, row, q_cols):
     step = pl.program_id(0)
     halves = w_ref.shape[1]
-    per_half = gq_ref.shape[0] // halves
     values = tok_ref[0].astype(jnp.float32)
     width = values.shape[1]
     grad = jnp.zeros(values.shape, jnp.float32)
     for half in range(halves):
         weights = w_ref[:, half, :, :q_cols].reshape(width, q_cols)
-        grad += dot_nt(joined(gq_ref, half * per_half, per_half), weights)
+        grad += dot_nt(joined(gq_ref, half, halves), weights)
     hat, inverse = normalize(values)
     total = jnp.sum(grad * hat, axis=0, keepdims=True)
 
@@ -1023,185 +1033,103 @@
     )(grad_qkv, tokens, grad_hidden, w_all, scales)
 
 
-def grad_qkv_kernel(me_ref, normed_ref, gq_ref, *refs, chunks):
-    *base_refs, keep_ref, send_ref, turned_ref = refs
-    width = normed_ref.shape[1]
-
-    @pl.when(pl.program_id(0) == 0)
+def grad_qkv_kernel(place_ref, normed_ref, gq_ref, *refs):
+    step = pl.program_id(0)
+    base_refs, out_refs, total_ref = refs[:-2], refs[-2:-1], refs[-1]
+    if len(refs) > 3:
+        base_refs, out_refs, (total_ref, turned_ref) = refs[:1], refs[1:-2], refs[-2:]
+
+    @pl.when(step == 0)
     def _():
-        turned_apart(turned_ref, normed_ref[...], me_ref[0], chunks)
-
-    pair = gq_ref.shape[2]
-    for one in range(gq_ref.shape[0]):
-        found = dot_nn(turned_ref[...], gq_ref[one])
-        lanes = slice(one * pair, (one + 1) * pair)
-        if keep_ref.shape[0] == 1:
-            at = (0, slice(None), slice(None), slice(None), lanes)
+        total_ref[...] = base_refs[0][...] if base_refs else jnp.zeros(total_ref.shape, jnp.float32)
+
+    total_ref[...] += dot_nn(transposed(gq_ref[0]), normed_ref[0])
+
+    @pl.when(step == pl.num_programs(0) - 1)
+    def _():
+        if base_refs:
+            turned_ref[...] = total_ref[...].T
+            tall = out_refs[0].shape[0]
+            for apart, out_ref in enumerate(out_refs):
+                at = pl.multiple_of((apart ^ place_ref[1]) * tall, tall)
+                out_ref[...] = turned_ref[pl.ds(at, tall), :].astype(jnp.bfloat16)
         else:
-            at = (slice(None), 0, slice(None), slice(None), lanes)
-        for number, out_ref in enumerate((keep_ref, send_ref)):
-            part = found[number * width // 2 : (number + 1) * width // 2]
-            part = part.reshape(2, chunks // 4, width // chunks, pair)
-            for base_ref in base_refs[number : number + 1]:
-                part += base_ref[at]
-            out_ref[at] = part.astype(out_ref.dtype)
-
-
-def grad_qkv_of(me, normed, grad_qkv, chunks, halves, first, some, at_front, base=()):
-    length, width = normed.shape
-    groups, _, pair = grad_qkv.shape
-    pairs = groups // halves
-    high = width // chunks
-    quarter = chunks // 4
-    columns = some * pair
-    if at_front:
-        out = pl.BlockSpec((1, 2, quarter, high, columns), lambda h, me: (h ^ me[1], 0, 0, 0, 0))
+            out_refs[0][...] = total_ref[...]
+
+
+def grad_qkv_of(place, normed, grad_qkv, parts, base=()):
+    blocks, length, width = normed.shape
+    pair = grad_qkv.shape[2]
+    turned = (pair, width)
+    if base:
+        shapes = [jax.ShapeDtypeStruct((width // parts, pair), jnp.bfloat16)] * parts
     else:
-        out = pl.BlockSpec((2, 1, quarter, high, columns), lambda h, me: (0, h ^ me[1], 0, 0, 0))
-    dtype = jnp.bfloat16 if base else jnp.float32
-    wide = jax.ShapeDtypeStruct((halves, 2, quarter, high, columns), dtype)
-    given = pl.BlockSpec((some, length, pair), lambda h, me: ((h * pairs + first) // some, 0, 0))
+        shapes = [jax.ShapeDtypeStruct(turned, jnp.float32)]
     return pl.pallas_call(
-        functools.partial(grad_qkv_kernel, chunks=chunks),
+        grad_qkv_kernel,
         grid_spec=pltpu.PrefetchScalarGridSpec(
             num_scalar_prefetch=1,
-            grid=(halves,),
-            in_specs=[whole((length, width)), given] + [out] * len(base),
-            out_specs=[out, out],
-            scratch_shapes=[pltpu.VMEM((width, length), jnp.bfloat16)],
+            grid=(blocks,),
+            in_specs=[
+                pl.BlockSpec((1, length, width), lambda i, place: (i, 0, 0)),
+                pl.BlockSpec((1, length, pair), lambda i, place: (i, 0, 0)),
+            ]
+            + [whole(turned)] * len(base),
+            out_specs=[whole(one.shape) for one in shapes],
+            scratch_shapes=[pltpu.VMEM(turned, jnp.float32)]
+            + [pltpu.VMEM((width, pair), jnp.float32)] * len(base),
         ),
-        out_shape=[wide] * 2,
+        out_shape=shapes,
         compiler_params=params(),
-        cost_estimate=cost(2 * length * width * halves * some * pair, 6 * length * width),
+        cost_estimate=cost(2 * blocks * length * width * pair, 3 * blocks * length * width),
         name="grad_qkv",
-    )(me, normed, grad_qkv, *base)
-
-
-def grad_time_kernel(me_ref, tet_ref, gs_ref, keep_ref, send_ref, apart_ref, *, chunks, folds, t_cols):
-    bits = chunks.bit_length() - 1
-    k_rows = tet_ref.shape[0] // chunks
-    for chunk in range(chunks):
-        apart = chunk ^ me_ref[0]
-        place = 0
-        for bit in range(bits):
-            place += ((apart >> bit) & 1) << (bits - 1 - bit)
-        apart_ref[pl.ds(pl.multiple_of(place * k_rows, k_rows), k_rows), :] = tet_ref[
-            chunk * k_rows : (chunk + 1) * k_rows, :
-        ]
-    half = pl.program_id(0)
-    shape = keep_ref.shape[1:3] + (k_rows, t_cols)
-    middle = chunks * k_rows // 2
-    for fold in range(folds):
-        at = pl.multiple_of((half * folds + fold) * t_cols, t_cols)
-        total = jnp.zeros((chunks * k_rows, t_cols), jnp.float32)
-        for row in range(gs_ref.shape[0]):
-            total += apart_ref[:, row : row + 1] * gs_ref[row : row + 1, pl.ds(at, t_cols)]
-        total = total.astype(jnp.bfloat16)
-        rows = slice(fold * k_rows, (fold + 1) * k_rows)
-        keep_ref[0, :, :, rows, :] = total[:middle].reshape(shape)
-        send_ref[0, :, :, rows, :] = total[middle:].reshape(shape)
-
-
-def grad_time_of(me, time_embed, grad_scales, chunks, halves, high, k_rows, t_cols):
-    turned = time_embed.T
-    quarter = chunks // 4
-    thin = jax.ShapeDtypeStruct((halves, 2, quarter, high, t_cols), jnp.bfloat16)
-    out = pl.BlockSpec((1, 2, quarter, high, t_cols), lambda h, me: (h ^ me[1], 0, 0, 0, 0))
-    return pl.pallas_call(
-        functools.partial(grad_time_kernel, chunks=chunks, folds=high // k_rows, t_cols=t_cols),
-        grid_spec=pltpu.PrefetchScalarGridSpec(
-            num_scalar_prefetch=1,
-            grid=(halves,),
-            in_specs=[whole(turned.shape), whole(grad_scales.shape)],
-            out_specs=[out, out],
-            scratch_shapes=[pltpu.VMEM(turned.shape, jnp.float32)],
-        ),
-        out_shape=[thin] * 2,
-        compiler_params=params(),
-        cost_estimate=cost(4 * turned.shape[0] * grad_scales.size, 4 * grad_scales.size),
-        name="grad_time",
-    )(me, turned, grad_scales)
+    )(place, normed, grad_qkv, *base)
+
+
+CTX = ("x", "core")
+GROUP = ("x", "core", "tp")
+EVERY = ("fsdp", "x", "core", "tp")
+
+
+def size_of(axis):
+    names = (axis,) if isinstance(axis, str) else axis
+    return functools.reduce(lambda size, name: size * lax.axis_size(name), names, 1)
 
 
 def across(values, axis, apart):
-    size = math.prod(lax.axis_size(name) for name in ([axis] if isinstance(axis, str) else axis))
+    size = size_of(axis)
     return lax.ppermute(values, axis, [(i, i ^ apart) for i in range(size)])
 
 
-def summed(parts, index):
-    total = parts[0][index].astype(jnp.float32)
-    for part in parts[1:]:
-        total += part[index].astype(jnp.float32)
-    return total
-
-
-HOPS = {"x": ("ctx", 2), "y": ("tp", 1)}
-
-
-class TreeSum:
-    def __init__(self, keep, send, order, stages):
-        self.parts = [keep, across(send, "ctx", 1)]
-        self.order = order
-        self.left = list(stages)
-
-    def ready(self):
-        name = self.left[0]
-        if name in HOPS:
-            places = {1: HOPS[name]}
-        elif name == "xy":
-            first, second = HOPS[self.order[0]], HOPS[self.order[1]]
-            both = (GROUP, 2 * lax.axis_size("tp") + 1)
-            places = {(1, 1): both, (1, 0): first, (0, 1): second}
-        else:
-            places = {3: ("fsdp", 3), 1: ("fsdp", 2), 2: ("fsdp", 1)}
-        self.hops = list(places.values())
-        self.given = [summed(self.parts, place).astype(jnp.bfloat16) for place in places]
-        return self.given
-
-    def go(self):
-        lower = (0, 0) if self.left.pop(0) == "xy" else 0
-        got = [across(one, *hop) for one, hop in zip(self.given, self.hops)]
-        self.parts = [part[lower] for part in self.parts] + got
-
-    def finish(self):
-        while self.left:
-            self.ready()
-            self.go()
-        return summed(self.parts, slice(None))
-
-
-def together(value, trees):
-    given = [tree.ready() for tree in trees]
-    value, given = lax.optimization_barrier((value, given))
-    for tree, some in zip(trees, given):
-        tree.given = some
-        tree.go()
-    return value
-
-
-def after(value, tree):
-    value, tree.parts = lax.optimization_barrier((value, tree.parts))
-    return value
+def summed(parts):
+    return sum(part.astype(jnp.float32) for part in parts)
+
+
+def exchange(values, axes):
+    return lax.all_to_all(values, axes, 0, 0, tiled=True)
+
+
+HOPS = {1: "tp", 2: "core", 4: "x"}
+
+
+def widened(found, apart):
+    return {**found, **{held ^ apart: across(one, HOPS[apart], 1) for held, one in found.items()}}
 
 
 def listed_table(block_pairs, pair_counts, row_blocks, ctx_size):
     rows, _, slots, _ = block_pairs.shape
     packed = jnp.concatenate([block_pairs.reshape(rows, 1, slots * 2), pair_counts[:, :, None]], axis=2)
     packed = jnp.concatenate(
-        [packed] + [across(packed, "ctx", apart) for apart in range(1, ctx_size)], axis=1
+        [packed] + [across(packed, CTX, apart) for apart in range(1, ctx_size)], axis=1
     )
     pairs = packed[:, :, : slots * 2].reshape(rows, ctx_size, slots, 2)
     live = jnp.arange(slots, dtype=jnp.int32)[None, None, :] < packed[:, :, slots * 2 :]
-    owner = lax.axis_index("ctx") ^ jnp.arange(ctx_size, dtype=jnp.int32)[None, :, None]
+    owner = lax.axis_index(CTX) ^ jnp.arange(ctx_size, dtype=jnp.int32)[None, :, None]
     base = owner * (row_blocks // ctx_size)
     code = jnp.where(live, (base + pairs[..., 0]) * row_blocks + pairs[..., 1], -1)
     code = code.reshape(rows, ctx_size * slots)
     cells = jnp.arange(row_blocks * row_blocks, dtype=jnp.int32)
     return jnp.any(code[:, :, None] == cells[None, None, :], axis=1).astype(jnp.int32)
-
-
-EVERY = ("fsdp", "ctx", "tp")
-GROUP = ("ctx", "tp")
 
 
 def spread_body(
@@ -1214,147 +1142,159 @@
     high = w_qkv.shape[0]
     q_cols, o_cols, f_cols = w_qkv.shape[1], w_out.shape[1], w_up.shape[1]
     k_rows = w_time.shape[0]
-    t_all = w_time.shape[1] // halves
-    folds = high // k_rows
-    t_cols = t_all // folds
     mine = lax.axis_index("tp")
-    me = jnp.stack([lax.axis_index("fsdp") * lax.axis_size("ctx") + lax.axis_index("ctx"), mine])
-    time_part = lax.dynamic_slice_in_dim(w_time, mine * t_all, t_all, 1)
-    time_part = time_part.reshape(k_rows, folds, t_cols).transpose(1, 0, 2).reshape(high, t_cols)
-    first = jnp.concatenate([w_qkv, time_part], axis=1).astype(jnp.bfloat16)
-    second = jnp.concatenate([w_out, w_up, w_down], axis=1).astype(jnp.bfloat16)
-    first = lax.all_gather(first, EVERY, axis=0, tiled=True).reshape(chunks, halves, high, -1)
-    second = lax.all_gather(second, EVERY, axis=0, tiled=True).reshape(chunks, halves, high, -1)
+    ctx, fsdp = lax.axis_index(CTX), lax.axis_index("fsdp")
+    n_ctx, n_fsdp = size_of(CTX), lax.axis_size("fsdp")
+    bf16, f32 = jnp.bfloat16, jnp.float32
+    chunk = fsdp * n_ctx + ctx
+    place = jnp.stack([ctx * halves + mine, fsdp, lax.axis_index("core")])
+
+    w_out = lax.all_gather(w_out.astype(bf16), EVERY, axis=0, tiled=True).reshape(chunks, halves, high, -1)
+
+    found = [{0: tokens[row]} for row in range(rows)]
+    orders = [(4, 1, 2) if row % 2 == 0 else (1, 4, 2) for row in range(rows)]
+    found = [widened(one, order[0]) for one, order in zip(found, orders)]
+    w_qkv = w_qkv.astype(bf16)
+    columns = exchange(w_qkv.reshape(high, n_ctx, -1).transpose(1, 0, 2), CTX).reshape(n_ctx * high, -1)
+    columns = [columns] + [across(columns, "fsdp", apart) for apart in range(1, n_fsdp)]
+    embeds = [time_embed] + [across(time_embed, "fsdp", apart) for apart in range(1, n_fsdp)]
+    mine_of = [lax.dynamic_slice_in_dim(one, chunk * k_rows, k_rows, 1) for one in embeds]
+    given = jnp.dot(jnp.concatenate(mine_of, axis=0), w_time.astype(bf16).astype(f32), precision=highest)
+    given = given.reshape(n_fsdp, rows, -1)
+    scales = given[0]
+    for apart in range(1, n_fsdp):
+        scales += across(given[apart], "fsdp", apart)
+    scales = 1.0 + scales + sum(across(scales, CTX, apart) for apart in range(1, n_ctx))
 
     row_blocks = segment_ids.shape[1] // BLK
-    listed = listed_table(block_pairs, pair_counts, row_blocks, lax.axis_size("ctx"))
+    listed = listed_table(block_pairs, pair_counts, row_blocks, n_ctx)
     edges = jnp.concatenate([segment_ids[:, ::HALF], segment_ids[:, HALF - 1 :: HALF]], axis=1)
     segc = segment_ids[:, :, None]
     segr = segment_ids[:, None, :]
-
-    time_embed, listed, edges, segc, segr = lax.optimization_barrier(
-        (time_embed, listed, edges, segc, segr)
-    )
+    found, scales, columns, listed, edges, segc, segr = lax.optimization_barrier(
+        (found, scales, columns, listed, edges, segc, segr)
+    )
+    found = [widened(one, order[1]) for one, order in zip(found, orders)]
+    second = jnp.concatenate([w_up, w_down], axis=1).astype(bf16)
+    found, second = lax.optimization_barrier((found, second))
+    second = lax.all_gather(second, EVERY, axis=0, tiled=True)
+    found = [widened(one, order[2]) for one, order in zip(found, orders)]
+    others = [[one[apart] for apart in range(1, len(one))] for one in found]
+
     qkv, normed = [], []
     for row in range(rows):
-        out, one, scales = project(row, time_embed, tokens, first, k_rows, q_cols, t_cols)
-        qkv.append(lax.all_to_all(out, GROUP, 0, 0, tiled=True))
+        out, one = project(row, place, scales, columns, tokens, others[row])
+        qkv.append(out)
         normed.append(one)
     mixed_own, lse, mixed = [], [], []
     for row in range(rows):
         out, one = attend(row, listed, edges, qkv[row], segc, segr)
         mixed_own.append(out)
         lse.append(one)
-        mixed.append(lax.all_to_all(out, GROUP, 0, 0, tiled=True))
+        mixed.append(exchange(out, GROUP))
+    mixed[0], mixed_own = lax.optimization_barrier((mixed[0], mixed_own))
+    second = second.reshape(chunks, halves, high, -1)
     hidden, normed_mlp = [], []
     for row in range(rows):
-        out, one = outward(row, mixed[row], tokens, second, scales, o_cols)
+        if row:
+            mixed[row], hidden[row - 1] = lax.optimization_barrier((mixed[row], hidden[row - 1]))
+        out, one = outward(row, mixed[row], tokens, w_out, scales, o_cols)
         hidden.append(out)
         normed_mlp.append(one)
-    grads, layer_out, grad_hidden, grad_attn, gscale_mlp = mlp(
-        normed_mlp, cotangent, hidden, scales, second, o_cols, f_cols
-    )
+    w_qkv, normed_mlp = lax.optimization_barrier((w_qkv, normed_mlp))
+    third = lax.all_gather(w_qkv, EVERY, axis=0, tiled=True).reshape(chunks, halves, high, -1)
+    keep, send, layer_out, grad_hidden, grad_attn, gscale_mlp = mlp(
+        place, normed_mlp, cotangent, hidden, scales, second, o_cols
+    )
+    keep, send = grad_proj_into(place, keep, send, grad_attn, mixed, o_cols)
+    grad_attn, keep, send, third = lax.optimization_barrier((grad_attn, keep, send, third))
+    sent = across(send, "core", 1)
     grad_mixed = {}
     for row in reversed(range(rows)):
-        out = grad_mixed_of(row, grad_attn, second, mixed[row].shape, o_cols)
-        grad_mixed[row] = lax.all_to_all(out, GROUP, 0, 0, tiled=True)
-    grads = grad_proj_into(grads, grad_attn, mixed, o_cols)
+        out = grad_mixed_of(row, grad_attn, w_out, mixed[row].shape, o_cols)
+        grad_mixed[row] = exchange(out, GROUP)
     last = rows - 1
+    grads = summed([keep, sent]).astype(bf16)
     grad_mixed[last], grads = lax.optimization_barrier((grad_mixed[last], grads))
-    grads = lax.psum_scatter(grads.reshape(-1, grads.shape[3]), EVERY, scatter_dimension=0, tiled=True)
-    grad_qkv = {}
+    grads = lax.psum_scatter(
+        grads.reshape(-1, grads.shape[4]), ("x", "tp"), scatter_dimension=0, tiled=True
+    )
+    own, grad_qkv = {}, {}
     for row in reversed(range(rows)):
-        out = attend_back(row, listed, edges, qkv[row], grad_mixed[row], mixed_own[row], lse[row], segc, segr)
-        grad_qkv[row] = lax.all_to_all(out, GROUP, 0, 0, tiled=True)
-    some = q_cols // (6 * HEAD_DIM) // 2
-    held, _ = lax.optimization_barrier((grad_qkv[last], out))
-    a_base = grad_qkv_of(me, normed[last], held, chunks, halves, 0, some, True)
-    b_base = grad_qkv_of(me, normed[last], held, chunks, halves, some, some, False)
+        if row < last:
+            grad_mixed[row], own[row + 1] = lax.optimization_barrier((grad_mixed[row], own[row + 1]))
+        own[row] = attend_back(row, listed, edges, qkv[row], grad_mixed[row], mixed_own[row], lse[row], segc, segr)
+        if row < last:
+            grad_qkv[row + 1] = exchange(own[row + 1], GROUP)
+    grad_qkv[0] = exchange(own[0], GROUP)
+    held, _ = lax.optimization_barrier((own[last], own[0]))
+    base = grad_qkv_of(place, normed[last], held, n_fsdp)
+    cut = list(grad_qkv_of(place, normed[0], own[0], n_fsdp, base))
     grad_tokens, gscale_attn = {}, {}
+    held, _ = lax.optimization_barrier((grad_qkv[last], cut[0]))
     grad_tokens[last], gscale_attn[last] = first_norm_back(
-        last, held, tokens, grad_hidden, first, scales, q_cols
-    )
-    held, gscale_attn[last], a_base, b_base = lax.optimization_barrier(
-        (grad_qkv[0], gscale_attn[last], a_base, b_base)
-    )
-    a_keep, a_send = grad_qkv_of(me, normed[0], held, chunks, halves, 0, some, True, a_base)
-    a_tree = TreeSum(a_keep, a_send, "yx", ["xy", "z"])
-    held, a_keep = lax.optimization_barrier((held, a_keep))
-    b_keep, b_send = grad_qkv_of(me, normed[0], held, chunks, halves, some, some, False, b_base)
-    b_tree = TreeSum(b_keep, b_send, "xy", ["xy", "z"])
-    held, b_keep = lax.optimization_barrier((held, b_keep))
-    held = together(held, [a_tree])
-    grad_tokens[0], gscale_attn[0] = first_norm_back(0, held, tokens, grad_hidden, first, scales, q_cols)
-    gscale_attn = jnp.concatenate([gscale_attn[row] for row in range(rows)], axis=0)
-    grad_scales = jnp.concatenate([gscale_attn, gscale_mlp], axis=1)
-    grad_scales = together(grad_scales, [b_tree])
-    t_keep, t_send = grad_time_of(me, time_embed, grad_scales, chunks, halves, high, k_rows, t_cols)
-    t_tree = TreeSum(t_keep, t_send, "yx", ["xy", "z"])
-    t_tree.parts = together(t_tree.parts, [a_tree])
-    b_tree.parts = together(b_tree.parts, [t_tree])
-    a_sum = a_tree.finish()
-    t_tree.parts = together(t_tree.parts, [b_tree])
-    grad_time = t_tree.finish().reshape(folds, k_rows, t_cols)
-    grad_time = grad_time.transpose(1, 0, 2).reshape(k_rows, t_all)
-    other = across(grad_time.astype(jnp.bfloat16), "tp", 1).astype(jnp.float32)
-    b_sum = b_tree.finish()
-    grad_time = jnp.concatenate(
-        [jnp.where(mine == 0, grad_time, other), jnp.where(mine == 0, other, grad_time)], axis=1
-    )
-    f32 = jnp.float32
+        last, held, tokens, grad_hidden, third, scales, q_cols
+    )
+    cut[0], gscale_attn[last] = lax.optimization_barrier((cut[0], gscale_attn[last]))
+    total = summed([cut[0]] + [across(cut[apart], "fsdp", apart) for apart in range(1, n_fsdp)])
+    grads, gscale_attn[last], total = lax.optimization_barrier(
+        (grads, gscale_attn[last], total.astype(bf16))
+    )
+    grads = lax.psum_scatter(grads, "fsdp", scatter_dimension=0, tiled=True)
+    total = exchange(total.reshape(n_ctx, high, -1), CTX)
+    grad_tokens[0], gscale_attn[0] = first_norm_back(
+        0, grad_qkv[0], tokens, grad_hidden, third, scales, q_cols
+    )
+    devices = n_fsdp * n_ctx * halves
+    both = jnp.concatenate([gscale_mlp, gscale_attn[last], gscale_attn[0]], axis=0)
+    both = exchange(jnp.broadcast_to(both[None], (devices,) + both.shape), EVERY)
+    both, total = lax.optimization_barrier((both, total))
+    grad_w_qkv = total.transpose(1, 0, 2).reshape(high, q_cols).astype(f32)
+    both = jnp.sum(both.reshape(n_fsdp, n_ctx * halves, 2 * rows, width), axis=1)
+    both = jnp.concatenate([both[:, 3], both[:, 0], both[:, 2], both[:, 1]], axis=1)
+    both = both.reshape(n_fsdp * rows, 2 * width)
+    mine_of = [lax.dynamic_index_in_dim(jnp.stack(mine_of), i ^ fsdp, 0, False) for i in range(n_fsdp)]
+    grad_time = jnp.dot(jnp.concatenate(mine_of, axis=0).T, both, precision=highest)
     return (
         layer_out.reshape(tokens.shape),
         jnp.stack([grad_tokens[row] for row in range(rows)]),
         grad_time,
-        jnp.concatenate([a_sum, b_sum], axis=1),
+        grad_w_qkv,
         grads[:, :o_cols].astype(f32),
         grads[:, o_cols : o_cols + f_cols].astype(f32),
         grads[:, o_cols + f_cols :].astype(f32),
     )
 
 
-def choose(*args):
-    tokens, w_qkv, w_out, w_up = args[0], args[6], args[7], args[8]
-    group = lax.axis_size("ctx") * lax.axis_size("tp")
-    heads_pair = 6 * HEAD_DIM
-    fits = (
-        (lax.axis_size("fsdp"), lax.axis_size("ctx"), lax.axis_size("tp")) == (4, 4, 2)
-        and tokens.shape[1] == BLK
-        and group * BLK == args[2].shape[1]
-        and w_qkv.shape[1] * lax.axis_size("tp") == group * heads_pair
-        and w_out.shape[1] % 512 == 0
-        and w_up.shape[1] % 512 == 0
-        and w_qkv.shape[0] % args[5].shape[0] == 0
-    )
-    return spread_body(*args) if fits else body(*args)
+def specs_of(ctx):
+    flat = ctx if isinstance(ctx, tuple) else (ctx,)
+    tokens, weights = P("fsdp", (*flat, "tp"), None), P(("fsdp", *flat), "tp")
+    placed = (tokens, P("fsdp", None), P("fsdp", None), P("fsdp", ctx, None, None), P("fsdp", ctx))
+    placed += (P(("fsdp", *flat), None), weights, weights, weights, weights, tokens)
+    return placed, (tokens, tokens, P(("fsdp", *flat), None), weights, weights, weights, weights)
 
 
 def solution(mesh):
-    placed = (
-        P("fsdp", ("ctx", "tp"), None),
-        P("fsdp", None),
-        P("fsdp", None),
-        P("fsdp", "ctx", None, None),
-        P("fsdp", "ctx"),
-        P(("fsdp", "ctx"), None),
-        P(("fsdp", "ctx"), "tp"),
-        P(("fsdp", "ctx"), "tp"),
-        P(("fsdp", "ctx"), "tp"),
-        P(("fsdp", "ctx"), "tp"),
-        P("fsdp", ("ctx", "tp"), None),
-    )
-    return jax.shard_map(
-        choose,
-        mesh=mesh,
-        in_specs=placed,
-        out_specs=(
-            P("fsdp", ("ctx", "tp"), None),
-            P("fsdp", ("ctx", "tp"), None),
-            P(("fsdp", "ctx"), None),
-            P(("fsdp", "ctx"), "tp"),
-            P(("fsdp", "ctx"), "tp"),
-            P(("fsdp", "ctx"), "tp"),
-            P(("fsdp", "ctx"), "tp"),
-        ),
-        check_vma=False,
-    )
+    sizes = tuple(mesh.shape[name] for name in ("fsdp", "ctx", "tp"))
+
+    def run(*args):
+        tokens, w_qkv, w_out, w_up = args[0], args[6], args[7], args[8]
+        group = sizes[1] * sizes[2]
+        fits = (
+            sizes == (4, 4, 2)
+            and tokens.shape[:2] == (8, group * BLK)
+            and w_qkv.shape[1] == group * 6 * HEAD_DIM
+            and w_out.shape[1] % (512 * sizes[2]) == 0
+            and w_up.shape[1] % (512 * sizes[2]) == 0
+        )
+        if fits:
+            devices = mesh.devices.reshape(sizes[0], 2, 2, sizes[2])
+            parted = Mesh(devices, ("fsdp", "x", "core", "tp"))
+            placed, given = specs_of(CTX)
+            return jax.shard_map(
+                spread_body, mesh=parted, in_specs=placed, out_specs=given, check_vma=False
+            )(*args)
+        placed, given = specs_of("ctx")
+        return jax.shard_map(body, mesh=mesh, in_specs=placed, out_specs=given, check_vma=False)(*args)
+
+    return run

time: 685 us -> 616 us (0.90)
  waiting for transfers between devices: 213 us -> 125 us
  local copies, waits for them, and re-layouts: 16.2 us -> 33.4 us
  starting transfers between devices: 84.5 us -> 70.1 us
  Pallas kernels: 329 us -> 337 us
    all_gather x2 -> x3, waiting for transfers between devices: 77.1 us -> 0.04 us  [the longest x1 0.02 us: spread_body(): second = lax.all_gather(second, EVERY, axis=0, tiled=True)]
    all_to_all x8 -> x9, waiting for transfers between devices: 94.4 us -> 32.7 us  [exchange(): return lax.all_to_all(values, axes, 0, 0, tiled=True)]
    ppermute x25 -> x33, waiting for transfers between devices: 41.2 us -> 73.3 us  [across(): return lax.ppermute(values, axis, [(i, i ^ apart) for i in range(size)])]
    ppermute x25 -> x33, starting transfers between devices: 53.5 us -> 32.6 us  [across(): return lax.ppermute(values, axis, [(i, i ^ apart) for i in range(size)])]
    reduce_scatter x1 -> x2, waiting for transfers between devices: 0.01 us -> 18.9 us  [the longest x1 10.7 us: spread_body(): lax.psum_scatter(grads.reshape(-1, grads.shape[4]), ('x', 'tp'), scatter_...]
    convert_element_type x7 -> x4, other arithmetic: 5.43 us -> 13.7 us  [the longest x1 10.4 us: spread_body(): grads = summed([keep, sent]).astype(bf16)]
    all_to_all x8 -> x9, starting transfers between devices: 30.9 us -> 37.3 us  [exchange(): return lax.all_to_all(values, axes, 0, 0, tiled=True)]
    pallas_call x9 -> x6, Pallas kernels: 131 us -> 131 us  [the longest x1 74.6 us: mlp(): pl.pallas_call(mlp_kernel, grid_spec=pltpu.PrefetchScalarGridSpec(num_sca...]
  transfers between devices with their start and end apart: 36 -> 47, of which waited for: 18 -> 17; matrix products, arithmetic and copies ran while one was open for 3% -> 9% of each run, Pallas kernels for 36% -> 55%
where the time goes in v4:
time: 616 us; the launch traced here: 610 us
  Pallas kernels  337 us (55%)
  waiting for transfers between devices  125 us (20%)
  starting transfers between devices  70.1 us (11%)
  local copies, waits for them, and re-layouts  33.4 us (5%)
  other arithmetic  27.9 us (5%)
  between operations  14.7 us (2%)
    pallas_call x2, Pallas kernels, attend_back(): pl.pallas_call(functools.partial(attend_back_kernel, row=row), grid_spec=...  106 us
    pallas_call x1, Pallas kernels, mlp(): pl.pallas_call(mlp_kernel, grid_spec=pltpu.PrefetchScalarGridSpec(num_sca...  74.6 us
    ppermute x33, waiting for transfers between devices, across(): return lax.ppermute(values, axis, [(i, i ^ apart) for i in range(size)])  73.3 us
    pallas_call x2, Pallas kernels, attend(): pl.pallas_call(functools.partial(attend_kernel, row=row), grid_spec=pltpu...  64 us
    all_to_all x9, starting transfers between devices, exchange(): return lax.all_to_all(values, axes, 0, 0, tiled=True)  37.3 us
    all_to_all x9, waiting for transfers between devices, exchange(): return lax.all_to_all(values, axes, 0, 0, tiled=True)  32.7 us
    ppermute x33, starting transfers between devices, across(): return lax.ppermute(values, axis, [(i, i ^ apart) for i in range(size)])  32.6 us
    pallas_call x2, Pallas kernels, project(): pl.pallas_call(functools.partial(project_kernel, row=row, pieces=pieces,...  26.3 us
  transfers between devices with their start and end apart: 47, of which 17 were waited for; matrix products, arithmetic and copies ran while one was open for 9% of the time, Pallas kernels for 55%

profile of v4, /device:TPU:0, one launch (start us, length us, event | category | flops | bytes accessed | tf_op | source)
XLA Modules:
  0.0 610.4 jit_solution(14875324692536638515)
XLA Ops:
  7.2 5.1 collective-permute-start.4
  14.5 1.5 collective-permute-start.15
  18.1 3.5 all-to-all-start
  21.7 1.5 convert_element_type.59
  23.3 1.3 constant_dynamic-slice_fusion.7
  27.5 1.7 slice_bitcast_fusion
  31.9 1.9 collective-permute-start
  33.8 1.7 collective-permute-start.1
  36.9 1.3 fusion.28
  38.3 1.4 slice.84
  39.6 1.4 copy.81
  41.0 1.3 squeeze.43
  48.0 1.3 collective-permute-start.5
  49.3 2.9 collective-permute-start.6
  54.0 3.8 collective-permute-done.7
  58.1 1.9 collective-permute-start.9
  61.2 2.2 collective-permute-start.12
  63.4 2.1 collective-permute-start.13
  65.6 1.4 add_add_fusion.scales_ref
  66.9 4.7 collective-permute-done.11.refs_1_
  71.7 8.3 %collective-permute-done.12.refs_2_ = bf16[256,384]{1,0:T(8,128)(2,1)S(1)} collective-permute-done((bf16[256,384]{1,0:T(8,128)(2,1)S(1)}, bf16[256,384]{1,0:T(8,128)(2,1)S(1)}, u32[]{:S(2)}, u32[]{:S(2)}) %collective-permute-start.12) | collective-permute-done | bytes 196640 | tf_op jit(solution)/shard_map/ppermute | solution.py:1101
  80.3 1.8 collective-permute-start.18
  82.1 2.1 collective-permute-start.20
  85.1 21.2 %collective-permute-done.17.refs_5_ = bf16[512,1024]{1,0:T(8,128)(2,1)} collective-permute-done((bf16[512,1024]{1,0:T(8,128)(2,1)S(1)}, bf16[512,1024]{1,0:T(8,128)(2,1)}, u32[]{:S(2)}, u32[]{:S(2)}) %collective-permute-start.17) | collective-permute-done | bytes 1048608 | tf_op jit(solution)/shard_map/ppermute | solution.py:1101
  106.3 19.6 %collective-permute-done.18.refs_9_ = bf16[512,1024]{1,0:T(8,128)(2,1)} collective-permute-done((bf16[512,1024]{1,0:T(8,128)(2,1)}, bf16[512,1024]{1,0:T(8,128)(2,1)}, u32[]{:S(2)}, u32[]{:S(2)}) %collective-permute-start.18) | collective-permute-done | bytes 1048608 | tf_op jit(solution)/shard_map/ppermute | solution.py:1101
  125.9 1.5 collective-permute-done.20.refs_9_
  129.0 3.4 copy.83.segc_ref
  133.6 1.4 collective-permute-done.24.refs_11_
  134.9 13.1 %project.2 = (bf16[8,512,384]{2,1,0:T(8,128)(2,1)}, bf16[8,512,1024]{2,1,0:T(8,128)(2,1)}) custom-call(s32[3]{0:T(128)} %pad_add_fusion.3.place_ref, f32[2,2048]{1,0:T(2,128)} %add_add_fusion.scales_ref, bf16[256,384]{1,0:T(8,128)(2,1)} %bitcast.80, bf16[256,384]{1,0:T(8,128)(2,1)} %copy-done.17, bf16[256,384]{1,0:T(8,128)(2,1)} %copy-done.18, ...), custom_call_target="tpu_custom_call" | custom-call | flops 3221225472 | bytes 20971520 | tf_op jit(solution)/shard_map/project/pallas_call | solution.py:425
  148.1 35.6 %attend.2 = (bf16[8,512,128]{2,1,0:T(8,128)(2,1)}, f32[2,4096]{1,0:T(2,128)}) custom-call(s32[2,64]{1,0:T(2,128)} %convert_element_type.58.listed_ref, s32[2,32]{1,0:T(2,128)} %pad_add_fusion.2.edge_ref, bf16[8,512,384]{2,1,0:T(8,128)(2,1)} %get-tuple-element.97.qkv_ref, s32[2,4096,1]{2,1,0:T(8,128)} %copy.83.segc_ref, s32[2,1,4096]{2,1,0:T(1,128)} %broadcast_in_dim.25.segr_ref), custom_call_target="tpu_custom_call" | custom-call | flops 20000000000 | bytes 6000000 | tf_op jit(solution)/shard_map/attend/pallas_call | solution.py:609
  183.6 4.5 all-to-all-start.1
  189.1 13.1 %project.3 = (bf16[8,512,384]{2,1,0:T(8,128)(2,1)}, bf16[8,512,1024]{2,1,0:T(8,128)(2,1)}) custom-call(s32[3]{0:T(128)} %pad_add_fusion.3.place_ref, f32[2,2048]{1,0:T(2,128)} %add_add_fusion.scales_ref, bf16[256,384]{1,0:T(8,128)(2,1)} %bitcast.81, bf16[256,384]{1,0:T(8,128)(2,1)} %copy-done.17, bf16[256,384]{1,0:T(8,128)(2,1)} %copy-done.18, ...), custom_call_target="tpu_custom_call" | custom-call | flops 3221225472 | bytes 20971520 | tf_op jit(solution)/shard_map/project/pallas_call | solution.py:425
  202.3 28.4 %attend.3 = (bf16[8,512,128]{2,1,0:T(8,128)(2,1)}, f32[2,4096]{1,0:T(2,128)}) custom-call(s32[2,64]{1,0:T(2,128)} %convert_element_type.58.listed_ref, s32[2,32]{1,0:T(2,128)} %pad_add_fusion.2.edge_ref, bf16[8,512,384]{2,1,0:T(8,128)(2,1)} %get-tuple-element.105.qkv_ref, s32[2,4096,1]{2,1,0:T(8,128)} %copy.83.segc_ref, s32[2,1,4096]{2,1,0:T(1,128)} %broadcast_in_dim.25.segr_ref), custom_call_target="tpu_custom_call" | custom-call | flops 20000000000 | bytes 6000000 | tf_op jit(solution)/shard_map/attend/pallas_call | solution.py:609
  230.7 4.2 all-to-all-start.2
  235.0 5.0 outward.2
  240.0 9.5 %all-to-all-done.2.mixed_ref.mixed1_ref = bf16[8,512,128]{2,1,0:T(8,128)(2,1)S(1)} async-done(((bf16[8,512,128]{2,1,0:T(8,128)(2,1)}), bf16[8,512,128]{2,1,0:T(8,128)(2,1)S(1)}, u32[]{:S(2)}, u32[]{:S(2)}) %all-to-all-start.2) | async-done | bytes 1048608 | tf_op jit(solution)/shard_map/all_to_all | solution.py:1109
  250.5 4.9 outward.3
  255.4 74.6 %mlp.1 = (bf16[2,2,4,64,4608]{4,3,2,1,0:T(8,128)(2,1)}, bf16[2,2,4,64,4608]{4,3,2,1,0:T(8,128)(2,1)}, bf16[1024,1024]{1,0:T(8,128)(2,1)}, f32[1024,1024]{1,0:T(8...) custom-call(s32[3]{0:T(128)} %pad_add_fusion.3.place_ref, bf16[512,1024]{1,0:T(8,128)(2,1)} %get-tuple-element.112.nm0_ref, ...), custom_call_target="tpu_custom_call" | custom-call | flops 51539607552 | bytes 50331648 | tf_op jit(solution)/shard_map/mlp/pallas_call | solution.py:869
  330.1 7.6 %grad_proj.1 = (bf16[2,2,4,64,4608]{4,3,2,1,0:T(8,128)(2,1)}, bf16[2,2,4,64,4608]{4,3,2,1,0:T(8,128)(2,1)}) custom-call(s32[3]{0:T(128)} %pad_add_fusion.3.place_ref, bf16[1024,1024]{1,0:T(8,128)(2,1)} %get-tuple-element.124.grad_ref, bf16[8,512,128]{2,1,0:T(8,128)(2,1)} %copy-done.2, ...), custom_call_target="tpu_custom_call", output_to_operand_aliasing={{0}: (4, {}), {1}: (5, {})} | custom-call | flops 2147483648 | bytes 6291456 | tf_op jit(solution)/shard_map/grad_proj/pallas_call | solution.py:969
  337.7 4.0 grad_mixed.3
  341.7 3.6 all-to-all-start.4
  345.3 7.4 %collective-permute-done.29 = bf16[2,2,4,64,4608]{4,3,2,1,0:T(8,128)(2,1)} collective-permute-done((bf16[2,2,4,64,4608]{4,3,2,1,0:T(8,128)(2,1)}, bf16[2,2,4,64,4608]{4,3,2,1,0:T(8,128)(2,1)}, u32[]{:S(2)}, u32[]{:S(2)}) %collective-permute-start.29) | collective-permute-done | bytes 9437216 | tf_op jit(solution)/shard_map/ppermute | solution.py:1101
  352.7 10.4 %add_convert_fusion = bf16[2,2,4,64,4608]{4,3,2,1,0:T(8,128)(2,1)} fusion(bf16[2,2,4,64,4608]{4,3,2,1,0:T(8,128)(2,1)} %collective-permute-done.29, bf16[2,2,4,64,4608]{4,3,2,1,0:T(8,128)(2,1)} %get-tuple-element.125), kind=kLoop, calls=%fused_computation | loop fusion | flops 18874368 | bytes 28311552 | tf_op jit(solution)/shard_map/convert_element_type | solution.py:1217
  364.0 4.0 grad_mixed.2
  368.0 3.6 all-to-all-start.3
  371.6 42.7 %attend_back.2.gq_ref = bf16[8,512,384]{2,1,0:T(8,128)(2,1)} custom-call(s32[2,64]{1,0:T(2,128)} %convert_element_type.58.listed_ref, s32[2,32]{1,0:T(2,128)} %pad_add_fusion.2.edge_ref, bf16[8,512,384]{2,1,0:T(8,128)(2,1)} %get-tuple-element.105.qkv_ref, bf16[8,512,128]{2,1,0:T(8,128)(2,1)} %copy-done.5, bf16[8,512,128]{2,1,0:T(8,128)(2,1)} %get-tuple-element.128.mixed_ref, ...), custom_call_target="tpu_custom_call" | custom-call | flops 49999998976 | bytes 10000000 | tf_op jit(solution)/shard_map/attend_back/pallas_call | solution.py:718
  415.3 4.2 all-to-all-start.6
  419.5 62.9 %attend_back.3.gq_ref = bf16[8,512,384]{2,1,0:T(8,128)(2,1)} custom-call(s32[2,64]{1,0:T(2,128)} %convert_element_type.58.listed_ref, s32[2,32]{1,0:T(2,128)} %pad_add_fusion.2.edge_ref, bf16[8,512,384]{2,1,0:T(8,128)(2,1)} %get-tuple-element.97.qkv_ref, bf16[8,512,128]{2,1,0:T(8,128)(2,1)} %copy-done.6, bf16[8,512,128]{2,1,0:T(8,128)(2,1)} %get-tuple-element.131.mixed_ref, ...), custom_call_target="tpu_custom_call" | custom-call | flops 49999998976 | bytes 10000000 | tf_op jit(solution)/shard_map/attend_back/pallas_call | solution.py:718
  482.4 1.7 copy-done.1
  484.1 4.1 all-to-all-start.5
  488.2 11.3 %grad_qkv.2.refs_0_ = f32[384,1024]{1,0:T(8,128)} custom-call(s32[3]{0:T(128)} %pad_add_fusion.3.place_ref, bf16[8,512,1024]{2,1,0:T(8,128)(2,1)} %get-tuple-element.138.normed_ref, bf16[8,512,384]{2,1,0:T(8,128)(2,1)} %attend_back.2.gq_ref), custom_call_target="tpu_custom_call" | custom-call | flops 3221225472 | bytes 12582912 | tf_op jit(solution)/shard_map/grad_qkv/pallas_call | solution.py:1068
  499.5 11.6 %grad_qkv.3 = (bf16[256,384]{1,0:T(8,128)(2,1)}, bf16[256,384]{1,0:T(8,128)(2,1)}, bf16[256,384]{1,0:T(8,128)(2,1)}, bf16[256,384]{1,0:T(8,128)(2,1)}) custom-call(s32[3]{0:T(128)} %pad_add_fusion.3.place_ref, bf16[8,512,1024]{2,1,0:T(8,128)(2,1)} %get-tuple-element.137.normed_ref, bf16[8,512,384]{2,1,0:T(8,128)(2,1)} %attend_back.3.gq_ref, ...), custom_call_target="tpu_custom_call" | custom-call | flops 3221225472 | bytes 12582912 | tf_op jit(solution)/shard_map/grad_qkv/pallas_call | solution.py:1068
  511.1 4.3 collective-permute-start.32
  515.5 9.2 %first_norm_back.3 = (bf16[512,1024]{1,0:T(8,128)(2,1)}, f32[1,1024]{1,0:T(1,128)}) custom-call(bf16[8,512,384]{2,1,0:T(8,128)(2,1)} %copy-done.1, bf16[2,512,1024]{2,1,0:T(8,128)(2,1)} %tok_ref.7, f32[1024,1024]{1,0:T(8,128)} %get-tuple-element.133.grad_hidden_ref, bf16[16,2,64,1536]{3,2,1,0:T(8,128)(2,1)} %bitcast.71, f32[2,2048]{1,0:T(2,128)} %add_add_fusion.scales_ref), custom_call_target="tpu_custom_call" | custom-call | flops 3221225472 | bytes 16777216 | tf_op jit(solution)/shard_map/first_norm_back/pallas_call | solution.py:1015
  524.7 3.8 collective-permute-done.31
  529.2 10.7 %reduce-scatter.3.cloned.1.call-done = bf16[256,4608]{1,0:T(8,128)(2,1)} async-done(((bf16[1024,4608]{1,0:T(8,128)(2,1)}), bf16[256,4608]{1,0:T(8,128)(2,1)}) %reduce-scatter.3.cloned.1.call-update) | async-done | bytes 2359312 | tf_op jit(solution)/shard_map/reduce_scatter | solution.py:1219
  540.2 3.4 all-to-all-start.8
  543.6 9.2 %first_norm_back.2 = (bf16[512,1024]{1,0:T(8,128)(2,1)}, f32[1,1024]{1,0:T(1,128)}) custom-call(bf16[8,512,384]{2,1,0:T(8,128)(2,1)} %copy-done, bf16[2,512,1024]{2,1,0:T(8,128)(2,1)} %tok_ref.7, f32[1024,1024]{1,0:T(8,128)} %get-tuple-element.133.grad_hidden_ref, bf16[16,2,64,1536]{3,2,1,0:T(8,128)(2,1)} %bitcast.72, f32[2,2048]{1,0:T(2,128)} %add_add_fusion.scales_ref), custom_call_target="tpu_custom_call" | custom-call | flops 3221225472 | bytes 16777216 | tf_op jit(solution)/shard_map/first_norm_back/pallas_call | solution.py:1015
  554.4 6.3 %all-to-all-start.7 = ((f32[32,4,1024]{2,1,0:T(4,128)}), f32[32,4,1024]{2,1,0:T(4,128)S(1)}, u32[]{:S(2)}, u32[]{:S(2)}) async-start(f32[32,4,1024]{2,1,0:T(4,128)} %broadcast_in_dim.26), calls=%async_computation.8 | async-start | bytes 1048576 | tf_op jit(solution)/shard_map/all_to_all | solution.py:1109
  563.6 3.1 pad_maximum_fusion
  566.7 22.9 %all-to-all-done.7 = f32[32,4,1024]{2,1,0:T(4,128)S(1)} async-done(((f32[32,4,1024]{2,1,0:T(4,128)}), f32[32,4,1024]{2,1,0:T(4,128)S(1)}, u32[]{:S(2)}, u32[]{:S(2)}) %all-to-all-start.7) | async-done | bytes 524320 | tf_op jit(solution)/shard_map/all_to_all | solution.py:1109
  591.6 8.2 %reduce-scatter.5.cloned.1.call-done = bf16[64,4608]{1,0:T(8,128)(2,1)} async-done(((bf16[256,4608]{1,0:T(8,128)(2,1)}), bf16[64,4608]{1,0:T(8,128)(2,1)}) %reduce-scatter.5.cloned.1.call-update) | async-done | bytes 589840 | tf_op jit(solution)/shard_map/reduce_scatter | solution.py:1243
  599.8 2.1 slice_convert_fusion
  601.9 1.5 slice_convert_fusion.2
  (157 shorter events, 35.9 us)
Async XLA Ops:
  7.2 37.6 %collective-permute-start.4 = (f32[2,256]{1,0:T(2,128)}, f32[2,256]{1,0:T(2,128)}, u32[]{:S(2)}, u32[]{:S(2)}) collective-permute-start(f32[2,256]{1,0:T(2,128)} %param.12), channel_id=1, source_target_pairs={{0,24},{8,16},{16,8},{24,0},{1,25},{9,17},{17,9},{25,1},{2,26},{10... | collective-permute-start | bytes 6152 | tf_op jit(solution)/shard_map/ppermute | solution.py:1101
  12.3 33.1 %collective-permute-start.3 = (f32[2,256]{1,0:T(2,128)}, f32[2,256]{1,0:T(2,128)}, u32[]{:S(2)}, u32[]{:S(2)}) collective-permute-start(f32[2,256]{1,0:T(2,128)} %param.12), channel_id=1, source_target_pairs={{0,16},{8,24},{16,0},{24,8},{1,17},{9,25},{17,1},{25,9},{2,18},{10... | collective-permute-start | bytes 6152 | tf_op jit(solution)/shard_map/ppermute | solution.py:1101
  14.5 16.7 %collective-permute-start.14 = (s32[2,1,31]{2,0,1:T(2,128)}, s32[2,1,31]{2,0,1:T(2,128)S(1)}, u32[]{:S(2)}, u32[]{:S(2)}) collective-permute-start(s32[2,1,31]{2,0,1:T(2,128)} %pad_add_fusion.1), channel_id=1, source_target_pairs={{0,2},{2,0},{4,6},{6,4},{1,3},{3,1},{5,7},{7,5},{8,10},{10,8},{12,... | collective-permute-start | bytes 752 | tf_op jit(solution)/shard_map/ppermute | solution.py:1101
  14.5 17.3 %collective-permute-start.15 = (s32[2,1,31]{2,0,1:T(2,128)}, s32[2,1,31]{2,0,1:T(2,128)}, u32[]{:S(2)}, u32[]{:S(2)}) collective-permute-start(s32[2,1,31]{2,0,1:T(2,128)} %pad_add_fusion.1), channel_id=1, source_target_pairs={{0,4},{2,6},{4,0},{6,2},{1,5},{3,7},{5,1},{7,3},{8,12},{10,14},{12... | collective-permute-start | bytes 752 | tf_op jit(solution)/shard_map/ppermute | solution.py:1101
  16.0 17.8 %collective-permute-start.16 = (s32[2,1,31]{2,0,1:T(2,128)}, s32[2,1,31]{2,0,1:T(2,128)}, u32[]{:S(2)}, u32[]{:S(2)}) collective-permute-start(s32[2,1,31]{2,0,1:T(2,128)} %pad_add_fusion.1), channel_id=1, source_target_pairs={{0,6},{2,4},{4,2},{6,0},{1,7},{3,5},{5,3},{7,1},{8,14},{10,12},{12... | collective-permute-start | bytes 752 | tf_op jit(solution)/shard_map/ppermute | solution.py:1101
  17.4 66.8 %copy-start.4 = (bf16[64,1536]{1,0:T(8,128)(2,1)}, bf16[64,1536]{1,0:T(8,128)(2,1)S(1)}, u32[]{:S(2)}) copy-start(bf16[64,1536]{1,0:T(8,128)(2,1)S(1)} %convert_element_type.56) | copy-start | bytes 589828
  17.4 66.8 %copy-start.7 = (f32[64,2048]{1,0:T(8,128)S(1)}, f32[64,2048]{1,0:T(8,128)}, u32[]{:S(2)}) copy-start(f32[64,2048]{1,0:T(8,128)} %param.19) | copy-start | bytes 1572868
  18.1 66.1 %copy-start.8 = (f32[64,2048]{1,0:T(8,128)S(1)}, f32[64,2048]{1,0:T(8,128)}, u32[]{:S(2)}) copy-start(f32[64,2048]{1,0:T(8,128)} %param.20) | copy-start | bytes 1572868
  18.1 43.0 %all-to-all-start = ((bf16[4,64,384]{2,1,0:T(8,128)(2,1)}), bf16[4,64,384]{2,1,0:T(8,128)(2,1)S(1)}, u32[]{:S(2)}, u32[]{:S(2)}) async-start(bf16[4,64,384]{2,1,0:T(8,128)(2,1)} %bitcast.64), calls=%async_computation | async-start | bytes 393216 | tf_op jit(solution)/shard_map/all_to_all | solution.py:1109
  21.6 213.4 %all-gather.4.cloned.1.call-start = ((), (), s32[]{:S(2)}) async-start(), calls=%async_computation.11 | async-start | bytes 2162688 | tf_op jit(solution)/shard_map/all_gather | solution.py:1152
  23.3 232.2 %all-gather.6.cloned.1.call-start = ((), (), s32[]{:S(2)}) async-start(), calls=%async_computation.12 | async-start | bytes 17301504 | tf_op jit(solution)/shard_map/all_gather | solution.py:1180
  26.9 2.4 copy-start.11
  26.9 3.0 copy-start.15
  31.2 15.0 %collective-permute-start.2 = (f32[2,256]{1,0:T(2,128)}, f32[2,256]{1,0:T(2,128)}, u32[]{:S(2)}, u32[]{:S(2)}) collective-permute-start(f32[2,256]{1,0:T(2,128)} %param.12), channel_id=1, source_target_pairs={{0,8},{8,0},{16,24},{24,16},{1,9},{9,1},{17,25},{25,17},{2,10},{10... | collective-permute-start | bytes 6152 | tf_op jit(solution)/shard_map/ppermute | solution.py:1101
  31.9 48.1 %collective-permute-start = (bf16[512,1024]{1,0:T(8,128)(2,1)S(1)}, bf16[512,1024]{1,0:T(8,128)(2,1)}, u32[]{:S(2)}, u32[]{:S(2)}) collective-permute-start(bf16[512,1024]{1,0:T(8,128)(2,1)S(1)} %get-tuple-element.94), channel_id=1, source_target_pairs={{0,4},{4,0},{1,5},{5,1},{2,6},{6,2},{3,7},{7,3},{8,12},{12,8},{9,1... | collective-permute-start | bytes 3145736 | tf_op jit(solution)/shard_map/ppermute | solution.py:1101
  33.8 46.2 %collective-permute-start.1 = (bf16[512,1024]{1,0:T(8,128)(2,1)S(1)}, bf16[512,1024]{1,0:T(8,128)(2,1)}, u32[]{:S(2)}, u32[]{:S(2)}) collective-permute-start(bf16[512,1024]{1,0:T(8,128)(2,1)S(1)} %get-tuple-element.102), channel_id=1, source_target_pairs={{0,1},{1,0},{2,3},{3,2},{4,5},{5,4},{6,7},{7,6},{8,9},{9,8},{10,11... | collective-permute-start | bytes 3145736 | tf_op jit(solution)/shard_map/ppermute | solution.py:1101
  48.0 5.1 collective-permute-start.5
  49.3 4.7 collective-permute-start.6
  52.3 5.5 collective-permute-start.7
  57.8 3.3 collective-permute-start.10
  57.9 3.3 collective-permute-start.8
  58.1 5.3 collective-permute-start.9
  61.2 71.2 %copy-start.9 = (bf16[4,64,384]{2,1,0:T(8,128)(2,1)}, bf16[4,64,384]{2,1,0:T(8,128)(2,1)S(1)}, u32[]{:S(2)}) copy-start(bf16[4,64,384]{2,1,0:T(8,128)(2,1)S(1)} %all-to-all-done) | copy-start | bytes 589828
  61.2 10.5 %collective-permute-start.11 = (bf16[256,384]{1,0:T(8,128)(2,1)S(1)}, bf16[256,384]{1,0:T(8,128)(2,1)S(1)}, u32[]{:S(2)}, u32[]{:S(2)}) collective-permute-start(bf16[256,384]{1,0:T(8,128)(2,1)S(1)} %bitcast.77), channel_id=1, source_target_pairs={{0,8},{8,0},{16,24},{24,16},{1,9},{9,1},{17,25},{25,17},{2,10},{10... | collective-permute-start | bytes 589832 | tf_op jit(solution)/shard_map/ppermute | solution.py:1101
  61.2 18.8 %collective-permute-start.12 = (bf16[256,384]{1,0:T(8,128)(2,1)S(1)}, bf16[256,384]{1,0:T(8,128)(2,1)S(1)}, u32[]{:S(2)}, u32[]{:S(2)}) collective-permute-start(bf16[256,384]{1,0:T(8,128)(2,1)S(1)} %bitcast.78), channel_id=1, source_target_pairs={{0,16},{8,24},{16,0},{24,8},{1,17},{9,25},{17,1},{25,9},{2,18},{10... | collective-permute-start | bytes 589832 | tf_op jit(solution)/shard_map/ppermute | solution.py:1101
  63.4 16.6 %collective-permute-start.13 = (bf16[256,384]{1,0:T(8,128)(2,1)S(1)}, bf16[256,384]{1,0:T(8,128)(2,1)S(1)}, u32[]{:S(2)}, u32[]{:S(2)}) collective-permute-start(bf16[256,384]{1,0:T(8,128)(2,1)S(1)} %bitcast.79), channel_id=1, source_target_pairs={{0,24},{8,16},{16,8},{24,0},{1,25},{9,17},{17,9},{25,1},{2,26},{10... | collective-permute-start | bytes 589832 | tf_op jit(solution)/shard_map/ppermute | solution.py:1101
  71.7 10.4 %copy-start.17 = (bf16[256,384]{1,0:T(8,128)(2,1)}, bf16[256,384]{1,0:T(8,128)(2,1)S(1)}, u32[]{:S(2)}) copy-start(bf16[256,384]{1,0:T(8,128)(2,1)S(1)} %collective-permute-done.11.refs_1_) | copy-start | bytes 589828
  80.0 2.1 copy-start.18
  80.0 2.1 copy-start.19
  80.0 26.3 %collective-permute-start.17 = (bf16[512,1024]{1,0:T(8,128)(2,1)S(1)}, bf16[512,1024]{1,0:T(8,128)(2,1)}, u32[]{:S(2)}, u32[]{:S(2)}) collective-permute-start(bf16[512,1024]{1,0:T(8,128)(2,1)S(1)} %get-tuple-element.94), channel_id=1, source_target_pairs={{0,1},{1,0},{2,3},{3,2},{4,5},{5,4},{6,7},{7,6},{8,9},{9,8},{10,11... | collective-permute-start | bytes 3145736 | tf_op jit(solution)/shard_map/ppermute | solution.py:1101
  80.3 45.6 %collective-permute-start.18 = (bf16[512,1024]{1,0:T(8,128)(2,1)}, bf16[512,1024]{1,0:T(8,128)(2,1)}, u32[]{:S(2)}, u32[]{:S(2)}) collective-permute-start(bf16[512,1024]{1,0:T(8,128)(2,1)} %collective-permute-done.refs_8_), channel_id=1, source_target_pairs={{0,1},{1,0},{2,3},{3,2},{4,5},{5,4},{6,7},{7,6},{8,9},{9,8},{10,11... | collective-permute-start | bytes 3145736 | tf_op jit(solution)/shard_map/ppermute | solution.py:1101
  82.1 43.8 %collective-permute-start.19 = (bf16[512,1024]{1,0:T(8,128)(2,1)S(1)}, bf16[512,1024]{1,0:T(8,128)(2,1)}, u32[]{:S(2)}, u32[]{:S(2)}) collective-permute-start(bf16[512,1024]{1,0:T(8,128)(2,1)S(1)} %get-tuple-element.102), channel_id=1, source_target_pairs={{0,4},{4,0},{1,5},{5,1},{2,6},{6,2},{3,7},{7,3},{8,12},{12,8},{9,1... | collective-permute-start | bytes 3145736 | tf_op jit(solution)/shard_map/ppermute | solution.py:1101
  82.1 45.2 %collective-permute-start.20 = (bf16[512,1024]{1,0:T(8,128)(2,1)}, bf16[512,1024]{1,0:T(8,128)(2,1)}, u32[]{:S(2)}, u32[]{:S(2)}) collective-permute-start(bf16[512,1024]{1,0:T(8,128)(2,1)} %collective-permute-done.1.refs_5_), channel_id=1, source_target_pairs={{0,4},{4,0},{1,5},{5,1},{2,6},{6,2},{3,7},{7,3},{8,12},{12,8},{9,1... | collective-permute-start | bytes 3145736 | tf_op jit(solution)/shard_map/ppermute | solution.py:1101
  127.4 5.1 collective-permute-start.21
  127.4 5.5 collective-permute-start.22
  127.9 5.5 collective-permute-start.23
  128.0 6.9 %collective-permute-start.24 = (bf16[512,1024]{1,0:T(8,128)(2,1)}, bf16[512,1024]{1,0:T(8,128)(2,1)}, u32[]{:S(2)}, u32[]{:S(2)}) collective-permute-start(bf16[512,1024]{1,0:T(8,128)(2,1)} %collective-permute-done.18.refs_9_), channel_id=1, source_target_pairs={{0,2},{2,0},{1,3},{3,1},{4,6},{6,4},{5,7},{7,5},{8,10},{10,8},{9,1... | collective-permute-start | bytes 3145736 | tf_op jit(solution)/shard_map/ppermute | solution.py:1101
  132.4 55.8 %collective-permute-start.25 = (bf16[512,1024]{1,0:T(8,128)(2,1)S(1)}, bf16[512,1024]{1,0:T(8,128)(2,1)S(1)}, u32[]{:S(2)}, u32[]{:S(2)}) collective-permute-start(bf16[512,1024]{1,0:T(8,128)(2,1)S(1)} %get-tuple-element.102), channel_id=1, source_target_pairs={{0,2},{2,0},{1,3},{3,1},{4,6},{6,4},{5,7},{7,5},{8,10},{10,8},{9,1... | collective-permute-start | bytes 3145736 | tf_op jit(solution)/shard_map/ppermute | solution.py:1101
  132.5 55.7 %collective-permute-start.26 = (bf16[512,1024]{1,0:T(8,128)(2,1)}, bf16[512,1024]{1,0:T(8,128)(2,1)}, u32[]{:S(2)}, u32[]{:S(2)}) collective-permute-start(bf16[512,1024]{1,0:T(8,128)(2,1)} %collective-permute-done.1.refs_5_), channel_id=1, source_target_pairs={{0,2},{2,0},{1,3},{3,1},{4,6},{6,4},{5,7},{7,5},{8,10},{10,8},{9,1... | collective-permute-start | bytes 3145736 | tf_op jit(solution)/shard_map/ppermute | solution.py:1101
  132.9 55.3 %collective-permute-start.27 = (bf16[512,1024]{1,0:T(8,128)(2,1)}, bf16[512,1024]{1,0:T(8,128)(2,1)}, u32[]{:S(2)}, u32[]{:S(2)}) collective-permute-start(bf16[512,1024]{1,0:T(8,128)(2,1)} %collective-permute-done.19.refs_8_), channel_id=1, source_target_pairs={{0,2},{2,0},{1,3},{3,1},{4,6},{6,4},{5,7},{7,5},{8,10},{10,8},{9,1... | collective-permute-start | bytes 3145736 | tf_op jit(solution)/shard_map/ppermute | solution.py:1101
  133.4 54.8 %collective-permute-start.28 = (bf16[512,1024]{1,0:T(8,128)(2,1)}, bf16[512,1024]{1,0:T(8,128)(2,1)}, u32[]{:S(2)}, u32[]{:S(2)}) collective-permute-start(bf16[512,1024]{1,0:T(8,128)(2,1)} %collective-permute-done.20.refs_9_), channel_id=1, source_target_pairs={{0,2},{2,0},{1,3},{3,1},{4,6},{6,4},{5,7},{7,5},{8,10},{10,8},{9,1... | collective-permute-start | bytes 3145736 | tf_op jit(solution)/shard_map/ppermute | solution.py:1101
  183.6 47.1 %all-to-all-start.1 = ((bf16[8,512,128]{2,1,0:T(8,128)(2,1)}), bf16[8,512,128]{2,1,0:T(8,128)(2,1)S(1)}, u32[]{:S(2)}, u32[]{:S(2)}) async-start(bf16[8,512,128]{2,1,0:T(8,128)(2,1)} %get-tuple-element.131.mixed_ref), calls=%async_computation.1 | async-start | bytes 2097152 | tf_op jit(solution)/shard_map/all_to_all | solution.py:1109
  188.2 1.0 copy-start.16
  230.7 4.3 copy-start.2
  230.7 18.8 %all-to-all-start.2 = ((bf16[8,512,128]{2,1,0:T(8,128)(2,1)}), bf16[8,512,128]{2,1,0:T(8,128)(2,1)S(1)}, u32[]{:S(2)}, u32[]{:S(2)}) async-start(bf16[8,512,128]{2,1,0:T(8,128)(2,1)} %get-tuple-element.128.mixed_ref), calls=%async_computation.2 | async-start | bytes 2097152 | tf_op jit(solution)/shard_map/all_to_all | solution.py:1109
  234.9 102.7 %all-gather.8.cloned.1.call-start = ((), (), s32[]{:S(2)}) async-start(), calls=%async_computation.13 | async-start | bytes 6488064 | tf_op jit(solution)/shard_map/all_gather | solution.py:1205
  249.5 1.0 copy-start.3
  337.7 15.0 %collective-permute-start.29 = (bf16[2,2,4,64,4608]{4,3,2,1,0:T(8,128)(2,1)}, bf16[2,2,4,64,4608]{4,3,2,1,0:T(8,128)(2,1)}, u32[]{:S(2)}, u32[]{:S(2)}) collective-permute-start(bf16[2,2,4,64,4608]{4,3,2,1,0:T(8,128)(2,1)} %get-tuple-element.126), channel_id=1, source_target_pairs={{0,2},{2,0},{1,3},{3,1},{4,6},{6,4},{5,7},{7,5},{8,10},{10,8},{9,1... | collective-permute-start | bytes 28311560 | tf_op jit(solution)/shard_map/ppermute | solution.py:1101
  341.7 21.3 %all-to-all-start.4 = ((bf16[8,512,128]{2,1,0:T(8,128)(2,1)}), bf16[8,512,128]{2,1,0:T(8,128)(2,1)S(1)}, u32[]{:S(2)}, u32[]{:S(2)}) async-start(bf16[8,512,128]{2,1,0:T(8,128)(2,1)} %grad_mixed.3), calls=%async_computation.4 | async-start | bytes 2097152 | tf_op jit(solution)/shard_map/all_to_all | solution.py:1109
  345.3 194.6 %reduce-scatter.3.cloned.1.call-start = ((), (), s32[]{:S(2)}) async-start(), calls=%async_computation.14 | async-start | bytes 11796480 | tf_op jit(solution)/shard_map/reduce_scatter | solution.py:1219
  368.0 46.3 %all-to-all-start.3 = ((bf16[8,512,128]{2,1,0:T(8,128)(2,1)}), bf16[8,512,128]{2,1,0:T(8,128)(2,1)S(1)}, u32[]{:S(2)}, u32[]{:S(2)}) async-start(bf16[8,512,128]{2,1,0:T(8,128)(2,1)} %grad_mixed.2), calls=%async_computation.3 | async-start | bytes 2097152 | tf_op jit(solution)/shard_map/all_to_all | solution.py:1109
  415.3 67.1 %all-to-all-start.6 = ((bf16[8,512,384]{2,1,0:T(8,128)(2,1)}), bf16[8,512,384]{2,1,0:T(8,128)(2,1)S(1)}, u32[]{:S(2)}, u32[]{:S(2)}) async-start(bf16[8,512,384]{2,1,0:T(8,128)(2,1)} %attend_back.2.gq_ref), calls=%async_computation.6 | async-start | bytes 6291456 | tf_op jit(solution)/shard_map/all_to_all | solution.py:1109
  482.4 1.7 copy-start.1
  484.1 56.1 %all-to-all-start.5 = ((bf16[8,512,384]{2,1,0:T(8,128)(2,1)}), bf16[8,512,384]{2,1,0:T(8,128)(2,1)S(1)}, u32[]{:S(2)}, u32[]{:S(2)}) async-start(bf16[8,512,384]{2,1,0:T(8,128)(2,1)} %attend_back.3.gq_ref), calls=%async_computation.5 | async-start | bytes 6291456 | tf_op jit(solution)/shard_map/all_to_all | solution.py:1109
  488.2 111.6 %reduce-scatter.5.cloned.1.call-start = ((), (), s32[]{:S(2)}) async-start(), calls=%async_computation.15 | async-start | bytes 2949120 | tf_op jit(solution)/shard_map/reduce_scatter | solution.py:1243
  511.1 13.6 %collective-permute-start.30 = (bf16[256,384]{1,0:T(8,128)(2,1)}, bf16[256,384]{1,0:T(8,128)(2,1)S(1)}, u32[]{:S(2)}, u32[]{:S(2)}) collective-permute-start(bf16[256,384]{1,0:T(8,128)(2,1)} %get-tuple-element.148), channel_id=1, source_target_pairs={{0,8},{8,0},{16,24},{24,16},{1,9},{9,1},{17,25},{25,17},{2,10},{10... | collective-permute-start | bytes 589832 | tf_op jit(solution)/shard_map/ppermute | solution.py:1101
  511.1 17.4 %collective-permute-start.31 = (bf16[256,384]{1,0:T(8,128)(2,1)}, bf16[256,384]{1,0:T(8,128)(2,1)S(1)}, u32[]{:S(2)}, u32[]{:S(2)}) collective-permute-start(bf16[256,384]{1,0:T(8,128)(2,1)} %get-tuple-element.149), channel_id=1, source_target_pairs={{0,16},{8,24},{16,0},{24,8},{1,17},{9,25},{17,1},{25,9},{2,18},{10... | collective-permute-start | bytes 589832 | tf_op jit(solution)/shard_map/ppermute | solution.py:1101
  511.1 17.3 %collective-permute-start.32 = (bf16[256,384]{1,0:T(8,128)(2,1)}, bf16[256,384]{1,0:T(8,128)(2,1)S(1)}, u32[]{:S(2)}, u32[]{:S(2)}) collective-permute-start(bf16[256,384]{1,0:T(8,128)(2,1)} %get-tuple-element.150), channel_id=1, source_target_pairs={{0,24},{8,16},{16,8},{24,0},{1,25},{9,17},{17,9},{25,1},{2,26},{10... | collective-permute-start | bytes 589832 | tf_op jit(solution)/shard_map/ppermute | solution.py:1101
  515.5 13.0 %copy-start.10 = (bf16[256,384]{1,0:T(8,128)(2,1)S(1)}, bf16[256,384]{1,0:T(8,128)(2,1)}, u32[]{:S(2)}) copy-start(bf16[256,384]{1,0:T(8,128)(2,1)} %get-tuple-element.147) | copy-start | bytes 589828
  540.2 3.4 copy-start
  540.2 13.3 %all-to-all-start.8 = ((bf16[4,64,384]{2,1,0:T(8,128)(2,1)}), bf16[4,64,384]{2,1,0:T(8,128)(2,1)S(1)}, u32[]{:S(2)}, u32[]{:S(2)}) async-start(bf16[4,64,384]{2,1,0:T(8,128)(2,1)} %bitcast.27), calls=%async_computation.9 | async-start | bytes 393216 | tf_op jit(solution)/shard_map/all_to_all | solution.py:1109
  543.6 9.2 %copy-start.13 = (f32[2,1024]{1,0:T(2,128)S(1)}, f32[2,1024]{1,0:T(2,128)}, u32[]{:S(2)}) copy-start(f32[2,1024]{1,0:T(2,128)} %get-tuple-element.143) | copy-start | bytes 24580
  543.6 9.2 %copy-start.14 = (f32[1,1024]{1,0:T(1,128)S(1)}, f32[1,1024]{1,0:T(1,128)}, u32[]{:S(2)}) copy-start(f32[1,1024]{1,0:T(1,128)} %get-tuple-element.151) | copy-start | bytes 12292
  554.4 35.2 %all-to-all-start.7 = ((f32[32,4,1024]{2,1,0:T(4,128)}), f32[32,4,1024]{2,1,0:T(4,128)S(1)}, u32[]{:S(2)}, u32[]{:S(2)}) async-start(f32[32,4,1024]{2,1,0:T(4,128)} %broadcast_in_dim.26), calls=%async_computation.8 | async-start | bytes 1048576 | tf_op jit(solution)/shard_map/all_to_all | solution.py:1109
  (3 other events, 2.7 us)
Sparse Core Ops, SparseCore 0:
  26.1 63.3 all-gather.3
  127.5 126.7 all-gather.5
  257.2 76.3 all-gather.7
  363.2 176.6 reduce-scatter.2
  542.0 57.7 reduce-scatter.4
